TPU v7x, 32 devices: a whole 2x2x4 slice. The times are simulated.
32 devices in a mesh: dp: 8 (over z, y), tensor: 4 (over x, core).
Axes of the slice: x: 2, y: 2, z: 4, core: 2. Of those that a mesh axis runs over, the one named last changes fastest.
Arguments:
- frames: bfloat16 [16, 256, 1024], P('dp', 'tensor'), may hold values from -6 to 6
- lengths: int32 [16], P('dp'), may hold values from 128 to 256, as said below
- span_starts: int32 [16, 32], P('dp'), may hold values from 0 to 256, as said below
- mask_vector: bfloat16 [1024], P(('dp', 'tensor')), may hold values from -6 to 6
- ffn1_gain: float32 [1024], P(('dp', 'tensor')), may hold values from 0.5 to 1.5
- ffn1_up: bfloat16 [1024, 4096], P(None, 'tensor'), may hold values from -0.1875 to 0.1875
- ffn1_down: bfloat16 [4096, 1024], P('tensor'), may hold values from -0.1875 to 0.1875
- attn_gain: float32 [1024], P(('dp', 'tensor')), may hold values from 0.5 to 1.5
- query_weight: bfloat16 [1024, 1024], P(None, 'tensor'), may hold values from -0.1875 to 0.1875
- key_weight: bfloat16 [1024, 1024], P(None, 'tensor'), may hold values from -0.1875 to 0.1875
- value_weight: bfloat16 [1024, 1024], P(None, 'tensor'), may hold values from -0.1875 to 0.1875
- output_weight: bfloat16 [1024, 1024], P('tensor'), may hold values from -1.5 to 1.5
- rel_slope: float32 [8], P('tensor'), may hold values from -2 to 2
- conv_gain: float32 [1024], P(('dp', 'tensor')), may hold values from 0.5 to 1.5
- conv_up: bfloat16 [1024, 2, 1024], P('dp', None, 'tensor'), may hold values from -0.1875 to 0.1875
- conv_depth: float32 [5, 1024], P(None, 'tensor'), may hold values from -2.5 to 2.5
- bn_scale: float32 [1024], P('tensor'), may hold values from 0.5 to 1.5
- bn_shift: float32 [1024], P('tensor'), may hold values from -1 to 1
- conv_down: bfloat16 [1024, 1024], P('tensor', 'dp'), may hold values from -0.25 to 0.25
- ffn2_gain: float32 [1024], P(('dp', 'tensor')), may hold values from 0.5 to 1.5
- ffn2_up: bfloat16 [1024, 4096], P(None, 'tensor'), may hold values from -0.1875 to 0.1875
- ffn2_down: bfloat16 [4096, 1024], P('tensor'), may hold values from -0.1875 to 0.1875
- final_gain: float32 [1024], P(('dp', 'tensor')), may hold values from 0.5 to 1.5
- cotangent: bfloat16 [16, 256, 1024], P('dp', 'tensor'), may hold values from -6 to 6
Outputs:
- layer_out: bfloat16 [16, 256, 1024], P('dp', 'tensor')
- frames_grad: float32 [16, 256, 1024], P('dp', 'tensor')
- mask_vector_grad: float32 [1024], P(('dp', 'tensor'))
- ffn1_gain_grad: float32 [1024], P(('dp', 'tensor'))
- ffn1_up_grad: float32 [1024, 4096], P('dp', 'tensor')
- ffn1_down_grad: float32 [4096, 1024], P('tensor', 'dp')
- attn_gain_grad: float32 [1024], P(('dp', 'tensor'))
- query_weight_grad: float32 [1024, 1024], P('dp', 'tensor')
- key_weight_grad: float32 [1024, 1024], P('dp', 'tensor')
- value_weight_grad: float32 [1024, 1024], P('dp', 'tensor')
- output_weight_grad: float32 [1024, 1024], P('tensor', 'dp')
- rel_slope_grad: float32 [8], P('tensor')
- conv_gain_grad: float32 [1024], P(('dp', 'tensor'))
- conv_up_grad: float32 [1024, 2, 1024], P('dp', None, 'tensor')
- conv_depth_grad: float32 [5, 1024], P(None, 'tensor')
- bn_scale_grad: float32 [1024], P('tensor')
- bn_shift_grad: float32 [1024], P('tensor')
- conv_down_grad: float32 [1024, 1024], P('tensor', 'dp')
- ffn2_gain_grad: float32 [1024], P(('dp', 'tensor'))
- ffn2_up_grad: float32 [1024, 4096], P('dp', 'tensor')
- ffn2_down_grad: float32 [4096, 1024], P('tensor', 'dp')
- final_gain_grad: float32 [1024], P(('dp', 'tensor'))
Inputs may be any that keep to these rules, and one draw needn't show every extreme that they name: `lengths`: the valid frames of an utterance are its first ones; in every draw some utterance has 256 valid frames and some has 128. `span_starts`: A start of 256 marks an unused span slot; used slots come first, and each utterance uses from 8 to 31 of them. Spans may intersect one another and the padding.
All inputs are finite; a program needn't handle non-finite values.
Results may differ from a plain program's by a relative error of at most 0.04.
Values may be sent and summed in bfloat16 or wider, within the bound.
No kernel may reach another device: no remote copies, remote signals or barrier semaphores. Data moves between devices by JAX's collectives and lax.ppermute only.
A program may use at most 128 MiB of HBM per device.

v0:
```python
import jax
import jax.numpy as jnp
from jax import lax
from jax.sharding import PartitionSpec as P

DH = 128
KW = 5
MB = 2
SPAN = 10
REACH = 128


EPSILON = 1e-05
MASKED_SCORE = -1000000000.0


def product(left, right):
    return jnp.dot(left, right, preferred_element_type=jnp.float32)


def inner_rows(left, right):
    return lax.dot_general(
        left, right, (((0,), (0,)), ((), ())), preferred_element_type=jnp.float32
    )


def times_back(left, right):
    return lax.dot_general(
        left, right, (((1,), (1,)), ((), ())), preferred_element_type=jnp.float32
    )


def norm_rows(values, norm_gain):
    centre = jnp.mean(values, axis=-1, keepdims=True)
    centred = values - centre
    inverse = lax.rsqrt(jnp.mean(centred * centred, axis=-1, keepdims=True) + EPSILON)
    unit_rows = centred * inverse
    return (unit_rows * norm_gain, unit_rows, inverse)


def norm_back(grad_out, unit_rows, inverse, norm_gain):
    grad_unit = grad_out * norm_gain
    first_mean = jnp.mean(grad_unit, axis=-1, keepdims=True)
    second_mean = jnp.mean(grad_unit * unit_rows, axis=-1, keepdims=True)
    return (
        inverse * (grad_unit - first_mean - unit_rows * second_mean),
        jnp.sum(grad_out * unit_rows, axis=0),
    )


def silu_slope(values):
    gate_value = jax.nn.sigmoid(values)
    return gate_value * (1.0 + values * (1.0 - gate_value))


def widen_rows(row_block):
    return lax.all_gather(row_block.astype(jnp.bfloat16), "tensor", axis=0, tiled=True)


def narrow_sum(partial_sum):
    return lax.psum_scatter(
        partial_sum.astype(jnp.bfloat16), "tensor", scatter_dimension=0, tiled=True
    ).astype(jnp.float32)


def widen_grad(row_block):
    return lax.all_gather(row_block.astype(jnp.bfloat16), "tensor", axis=0, tiled=True)


def narrow_grad(partial_sum):
    return lax.psum_scatter(
        partial_sum.astype(jnp.bfloat16), "tensor", scatter_dimension=0, tiled=True
    ).astype(jnp.float32)


def relative_table(length):
    places = jnp.arange(length, dtype=jnp.int32)
    return jnp.clip(places[None, :] - places[:, None], -REACH, REACH).astype(jnp.float32) / REACH


def depthwise(padded, depth_weight, length):
    convolved = depth_weight[0] * padded[0:length]
    for offset in range(1, KW):
        convolved = convolved + depth_weight[offset] * padded[offset : offset + length]
    return convolved


def ffn_forward(row_block, norm_gain, up_weight, down_weight):
    normed, unit_rows, inverse = norm_rows(row_block, norm_gain)
    gathered = widen_rows(normed)
    hidden = product(gathered, up_weight)
    active = jax.nn.silu(hidden).astype(jnp.bfloat16)
    result = narrow_sum(product(active, down_weight))
    return (result, (unit_rows, inverse, gathered, hidden, active))


def ffn_backward(grad_rows, kept_state, norm_gain, up_weight, down_weight):
    unit_rows, inverse, gathered, hidden, active = kept_state
    grad_branch = widen_grad(0.5 * grad_rows)
    grad_down = inner_rows(active, grad_branch)
    grad_hidden = (times_back(grad_branch, down_weight) * silu_slope(hidden)).astype(jnp.bfloat16)
    grad_up = inner_rows(gathered, grad_hidden)
    grad_normed = narrow_grad(times_back(grad_hidden, up_weight))
    grad_input, grad_gain = norm_back(grad_normed, unit_rows, inverse, norm_gain)
    return (grad_input, grad_gain, grad_up, grad_down)


def attn_scores(query_rows, key_rows, slopes, relative, valid_keys):
    head_count = slopes.shape[0]
    length = query_rows.shape[0]
    query_heads = query_rows.reshape(length, head_count, DH)
    key_heads = key_rows.reshape(length, head_count, DH)
    scores = jnp.einsum(
        "qhd,khd->hqk", query_heads, key_heads, preferred_element_type=jnp.float32
    ) * DH ** (-0.5)
    scores = scores + slopes[:, None, None] * relative[None]
    return jnp.where(valid_keys[None, None, :], scores, MASKED_SCORE)


def attn_forward(
    row_block,
    norm_gain,
    query_weight,
    key_weight,
    value_weight,
    output_weight,
    slopes,
    relative,
    valid_keys,
):
    normed, unit_rows, inverse = norm_rows(row_block, norm_gain)
    gathered = widen_rows(normed)
    query_rows = product(gathered, query_weight).astype(jnp.bfloat16)
    key_rows = product(gathered, key_weight).astype(jnp.bfloat16)
    value_rows = product(gathered, value_weight).astype(jnp.bfloat16)
    head_count = slopes.shape[0]
    length = gathered.shape[0]
    scores = attn_scores(query_rows, key_rows, slopes, relative, valid_keys)
    row_peak = jnp.max(scores, axis=-1, keepdims=True)
    raised = jnp.exp(scores - row_peak)
    row_total = jnp.sum(raised, axis=-1, keepdims=True)
    weights_soft = (raised / row_total).astype(jnp.bfloat16)
    value_heads = value_rows.reshape(length, head_count, DH)
    context = jnp.einsum(
        "hqk,khd->qhd", weights_soft, value_heads, preferred_element_type=jnp.float32
    )
    context = context.reshape(length, head_count * DH).astype(jnp.bfloat16)
    result = narrow_sum(product(context, output_weight))
    log_total = row_peak + jnp.log(row_total)
    return (
        result,
        (unit_rows, inverse, gathered, query_rows, key_rows, value_rows, log_total, context),
    )


def attn_backward(
    grad_rows,
    kept_state,
    norm_gain,
    query_weight,
    key_weight,
    value_weight,
    output_weight,
    slopes,
    relative,
    valid_keys,
):
    unit_rows, inverse, gathered, query_rows, key_rows, value_rows, log_total, context = kept_state
    head_count = slopes.shape[0]
    length = gathered.shape[0]
    grad_branch = widen_grad(grad_rows)
    grad_output = inner_rows(context, grad_branch)
    grad_context = times_back(grad_branch, output_weight).astype(jnp.bfloat16)
    scores = attn_scores(query_rows, key_rows, slopes, relative, valid_keys)
    weights_soft = jnp.exp(scores - log_total)
    grad_heads = grad_context.reshape(length, head_count, DH)
    value_heads = value_rows.reshape(length, head_count, DH)
    query_heads = query_rows.reshape(length, head_count, DH)
    key_heads = key_rows.reshape(length, head_count, DH)
    grad_value = (
        jnp.einsum(
            "hqk,qhd->khd",
            weights_soft.astype(jnp.bfloat16),
            grad_heads,
            preferred_element_type=jnp.float32,
        )
        .reshape(length, head_count * DH)
        .astype(jnp.bfloat16)
    )
    grad_weights = jnp.einsum(
        "qhd,khd->hqk", grad_heads, value_heads, preferred_element_type=jnp.float32
    )
    grad_scores = weights_soft * (
        grad_weights - jnp.sum(weights_soft * grad_weights, axis=-1, keepdims=True)
    )
    grad_scores = grad_scores.astype(jnp.bfloat16)
    grad_slopes = jnp.einsum(
        "hqk,qk->h", grad_scores, relative.astype(jnp.bfloat16), preferred_element_type=jnp.float32
    )
    grad_query = jnp.einsum(
        "hqk,khd->qhd", grad_scores, key_heads, preferred_element_type=jnp.float32
    ) * DH ** (-0.5)
    grad_query = grad_query.reshape(length, head_count * DH).astype(jnp.bfloat16)
    grad_key = jnp.einsum(
        "hqk,qhd->khd", grad_scores, query_heads, preferred_element_type=jnp.float32
    ) * DH ** (-0.5)
    grad_key = grad_key.reshape(length, head_count * DH).astype(jnp.bfloat16)
    grad_query_weight = inner_rows(gathered, grad_query)
    grad_key_weight = inner_rows(gathered, grad_key)
    grad_value_weight = inner_rows(gathered, grad_value)
    grad_whole = (
        times_back(grad_query, query_weight)
        + times_back(grad_key, key_weight)
        + times_back(grad_value, value_weight)
    )
    grad_normed = narrow_grad(grad_whole)
    grad_input, grad_gain = norm_back(grad_normed, unit_rows, inverse, norm_gain)
    return (
        grad_input,
        grad_gain,
        grad_query_weight,
        grad_key_weight,
        grad_value_weight,
        grad_output,
        grad_slopes,
    )


def conv_start(row_block, norm_gain, up_full, depth_weight, valid_keys):
    normed, unit_rows, inverse = norm_rows(row_block, norm_gain)
    gathered = widen_rows(normed)
    channels = depth_weight.shape[1]
    length = gathered.shape[0]
    mixed = product(gathered, up_full.reshape(up_full.shape[0], 2 * channels))
    value_half = mixed[:, :channels]
    gate_value = jax.nn.sigmoid(mixed[:, channels:])
    valid_col = valid_keys.astype(jnp.float32)[:, None]
    gated_rows = value_half * gate_value * valid_col
    padded = jnp.pad(gated_rows, ((KW // 2, KW // 2), (0, 0)))
    convolved = depthwise(padded, depth_weight, length)
    return (convolved, valid_col, (unit_rows, inverse, gathered, value_half, gate_value, padded))


def conv_finish(convolved, centre, bn_inverse, scale_row, shift_row, down_full):
    centred = convolved - centre
    unit_bn = centred * bn_inverse
    shaped = unit_bn * scale_row + shift_row
    activated = jax.nn.silu(shaped).astype(jnp.bfloat16)
    result = narrow_sum(product(activated, down_full))
    return (result, (unit_bn, centred, shaped, activated))


def conv_back_start(grad_rows, rear_state, down_full):
    unit_bn, centred, shaped, activated = rear_state
    grad_branch = widen_grad(grad_rows)
    grad_down = inner_rows(activated, grad_branch)
    grad_shaped = times_back(grad_branch, down_full) * silu_slope(shaped)
    return (
        grad_shaped,
        grad_down,
        jnp.sum(grad_shaped, axis=0),
        jnp.sum(grad_shaped * unit_bn, axis=0),
    )


def conv_back_finish(
    grad_shaped,
    front_state,
    rear_state,
    valid_col,
    sum_shift,
    sum_scale,
    bn_inverse,
    frame_count,
    norm_gain,
    up_full,
    depth_weight,
    scale_row,
):
    unit_rows, inverse, gathered, value_half, gate_value, padded = front_state
    unit_bn, centred, shaped, activated = rear_state
    channels = depth_weight.shape[1]
    length = gathered.shape[0]
    grad_centre = -bn_inverse * scale_row * sum_shift
    grad_spread = -bn_inverse * bn_inverse * scale_row * sum_scale
    grad_conv = (
        grad_shaped * scale_row * bn_inverse
        + valid_col * (grad_centre + grad_spread * centred) / frame_count
    )
    grad_padded = jnp.pad(grad_conv, ((KW // 2, KW // 2), (0, 0)))
    grad_gated = depth_weight[0] * grad_padded[2 * (KW // 2) : 2 * (KW // 2) + length]
    for offset in range(1, KW):
        begin = 2 * (KW // 2) - offset
        grad_gated = grad_gated + depth_weight[offset] * grad_padded[begin : begin + length]
    grad_depth = jnp.stack(
        [jnp.sum(grad_conv * padded[offset : offset + length], axis=0) for offset in range(KW)]
    )
    grad_gated = grad_gated * valid_col
    grad_mixed = jnp.concatenate(
        [grad_gated * gate_value, grad_gated * value_half * gate_value * (1.0 - gate_value)], axis=1
    ).astype(jnp.bfloat16)
    up_flat = up_full.reshape(up_full.shape[0], 2 * channels)
    grad_up = inner_rows(gathered, grad_mixed).reshape(up_full.shape[0], 2, channels)
    grad_normed = narrow_grad(times_back(grad_mixed, up_flat))
    grad_input, grad_gain = norm_back(grad_normed, unit_rows, inverse, norm_gain)
    return (grad_input, grad_gain, grad_up, grad_depth)


def share_grads(row_grads, column_grads, gain_grads, kernel_grads):
    first_up, second_up, query_grad, key_grad, value_grad, conv_up_grad = row_grads
    rows_out = (
        lax.psum_scatter(first_up, "dp", scatter_dimension=0, tiled=True),
        lax.psum_scatter(second_up, "dp", scatter_dimension=0, tiled=True),
        lax.psum_scatter(query_grad, "dp", scatter_dimension=0, tiled=True),
        lax.psum_scatter(key_grad, "dp", scatter_dimension=0, tiled=True),
        lax.psum_scatter(value_grad, "dp", scatter_dimension=0, tiled=True),
        lax.psum_scatter(conv_up_grad, "dp", scatter_dimension=0, tiled=True),
    )
    first_down, second_down, output_grad, conv_down_grad = column_grads
    cols_out = (
        lax.psum_scatter(first_down, "dp", scatter_dimension=1, tiled=True),
        lax.psum_scatter(second_down, "dp", scatter_dimension=1, tiled=True),
        lax.psum_scatter(output_grad, "dp", scatter_dimension=1, tiled=True),
        lax.psum_scatter(conv_down_grad, "dp", scatter_dimension=1, tiled=True),
    )
    mask_grad, gain_one, gain_attn, gain_conv, gain_two, gain_final = gain_grads
    small_out = (
        lax.psum_scatter(mask_grad, ("dp", "tensor"), scatter_dimension=0, tiled=True),
        lax.psum_scatter(gain_one, ("dp", "tensor"), scatter_dimension=0, tiled=True),
        lax.psum_scatter(gain_attn, ("dp", "tensor"), scatter_dimension=0, tiled=True),
        lax.psum_scatter(gain_conv, ("dp", "tensor"), scatter_dimension=0, tiled=True),
        lax.psum_scatter(gain_two, ("dp", "tensor"), scatter_dimension=0, tiled=True),
        lax.psum_scatter(gain_final, ("dp", "tensor"), scatter_dimension=0, tiled=True),
    )
    depth_grad, slope_grad = kernel_grads
    channel_out = lax.psum((depth_grad, slope_grad), "dp")
    return (rows_out, cols_out, small_out, channel_out)


def add_up(total, fresh):
    return fresh if total is None else jax.tree.map(jnp.add, total, fresh)


def per_device(
    frames,
    lengths,
    span_starts,
    mask_vector,
    ffn1_gain,
    ffn1_up,
    ffn1_down,
    attn_gain,
    query_weight,
    key_weight,
    value_weight,
    output_weight,
    rel_slope,
    conv_gain,
    conv_up,
    conv_depth,
    bn_scale,
    bn_shift,
    conv_down,
    ffn2_gain,
    ffn2_up,
    ffn2_down,
    final_gain,
    cotangent,
):
    batches, row_count, feature_count = frames.shape
    length = row_count * lax.axis_size("tensor")
    first_row = lax.axis_index("tensor") * row_count
    row_places = first_row + jnp.arange(row_count, dtype=jnp.int32)
    full_places = jnp.arange(length, dtype=jnp.int32)
    relative = relative_table(length)
    outputs = [None] * batches
    input_grads = [None] * batches
    totals = None
    bn_totals = None
    for group_index in range(MB):
        members = [index for index in range(batches) if index % MB == group_index]
        mask_full, gain_one, gain_attn, gain_conv, gain_two, gain_final = (
            lax.all_gather(mask_vector.astype(jnp.float32), ("dp", "tensor"), axis=0, tiled=True),
            lax.all_gather(ffn1_gain, ("dp", "tensor"), axis=0, tiled=True),
            lax.all_gather(attn_gain, ("dp", "tensor"), axis=0, tiled=True),
            lax.all_gather(conv_gain, ("dp", "tensor"), axis=0, tiled=True),
            lax.all_gather(ffn2_gain, ("dp", "tensor"), axis=0, tiled=True),
            lax.all_gather(final_gain, ("dp", "tensor"), axis=0, tiled=True),
        )
        up_full, down_full = (
            lax.all_gather(conv_up, "dp", axis=0, tiled=True),
            lax.all_gather(conv_down, "dp", axis=1, tiled=True),
        )
        front = {}
        sum_local = None
        for batch_index in members:
            valid_rows = row_places < lengths[batch_index]
            valid_keys = full_places < lengths[batch_index]
            starts = span_starts[batch_index]
            covered = jnp.any(
                (starts[:, None] <= row_places[None, :])
                & (row_places[None, :] < starts[:, None] + SPAN),
                axis=0,
            )
            masked = covered & valid_rows
            inputs = jnp.where(
                masked[:, None], mask_full[None, :], frames[batch_index].astype(jnp.float32)
            )
            branch_one, kept_one = ffn_forward(inputs, gain_one, ffn1_up, ffn1_down)
            stream_one = inputs + 0.5 * branch_one
            branch_attn, kept_attn = attn_forward(
                stream_one,
                gain_attn,
                query_weight,
                key_weight,
                value_weight,
                output_weight,
                rel_slope,
                relative,
                valid_keys,
            )
            stream_two = stream_one + branch_attn
            convolved, valid_col, conv_state = conv_start(
                stream_two, gain_conv, up_full, conv_depth, valid_keys
            )
            front[batch_index] = (
                masked,
                valid_keys,
                kept_one,
                kept_attn,
                stream_two,
                convolved,
                valid_col,
                conv_state,
            )
            fresh = (jnp.sum(convolved * valid_col, axis=0), jnp.sum(valid_col))
            sum_local = add_up(sum_local, fresh)
        sum_conv, frame_count = lax.psum(sum_local, "dp")
        centre = sum_conv / frame_count
        square_local = None
        for batch_index in members:
            convolved, valid_col = (front[batch_index][5], front[batch_index][6])
            centred = convolved - centre
            square_local = add_up(square_local, jnp.sum(centred * centred * valid_col, axis=0))
        variance = lax.psum(square_local, "dp") / frame_count
        bn_inverse = lax.rsqrt(variance + EPSILON)
        middle = {}
        back_local = None
        group_grads = None
        for batch_index in members:
            (
                masked,
                valid_keys,
                kept_one,
                kept_attn,
                stream_two,
                convolved,
                valid_col,
                conv_state,
            ) = front[batch_index]
            branch_conv, rear_state = conv_finish(
                convolved, centre, bn_inverse, bn_scale, bn_shift, down_full
            )
            stream_three = stream_two + branch_conv
            branch_two, kept_two = ffn_forward(stream_three, gain_two, ffn2_up, ffn2_down)
            stream_four = stream_three + 0.5 * branch_two
            final_rows, final_unit, final_inverse = norm_rows(stream_four, gain_final)
            outputs[batch_index] = final_rows.astype(jnp.bfloat16)
            grad_stream, grad_final = norm_back(
                cotangent[batch_index].astype(jnp.float32), final_unit, final_inverse, gain_final
            )
            back_two = ffn_backward(grad_stream, kept_two, gain_two, ffn2_up, ffn2_down)
            grad_stream = grad_stream + back_two[0]
            grad_shaped, grad_down, part_shift, part_scale = conv_back_start(
                grad_stream, rear_state, down_full
            )
            back_local = add_up(back_local, (part_shift, part_scale))
            middle[batch_index] = (
                grad_stream,
                grad_shaped,
                grad_down,
                rear_state,
                back_two,
                grad_final,
            )
        sum_shift, sum_scale = lax.psum(back_local, "dp")
        bn_totals = add_up(bn_totals, (sum_scale, sum_shift))
        for batch_index in members:
            (
                masked,
                valid_keys,
                kept_one,
                kept_attn,
                stream_two,
                convolved,
                valid_col,
                conv_state,
            ) = front[batch_index]
            grad_stream, grad_shaped, grad_down, rear_state, back_two, grad_final = middle[
                batch_index
            ]
            back_conv = conv_back_finish(
                grad_shaped,
                conv_state,
                rear_state,
                valid_col,
                sum_shift,
                sum_scale,
                bn_inverse,
                frame_count,
                gain_conv,
                up_full,
                conv_depth,
                bn_scale,
            )
            grad_stream = grad_stream + back_conv[0]
            back_attn = attn_backward(
                grad_stream,
                kept_attn,
                gain_attn,
                query_weight,
                key_weight,
                value_weight,
                output_weight,
                rel_slope,
                relative,
                valid_keys,
            )
            grad_stream = grad_stream + back_attn[0]
            back_one = ffn_backward(grad_stream, kept_one, gain_one, ffn1_up, ffn1_down)
            grad_stream = grad_stream + back_one[0]
            input_grads[batch_index] = jnp.where(masked[:, None], 0.0, grad_stream)
            grad_mask = jnp.sum(jnp.where(masked[:, None], grad_stream, 0.0), axis=0)
            fresh_grads = (
                (back_one[2], back_two[2], back_attn[2], back_attn[3], back_attn[4], back_conv[2]),
                (back_one[3], back_two[3], back_attn[5], grad_down),
                (grad_mask, back_one[1], back_attn[1], back_conv[1], back_two[1], grad_final),
                (back_conv[3], back_attn[6]),
            )
            group_grads = add_up(group_grads, fresh_grads)
        shared = share_grads(group_grads[0], group_grads[1], group_grads[2], group_grads[3])
        totals = add_up(totals, shared)
    rows_out, cols_out, small_out, channel_out = totals
    return (
        jnp.stack(outputs),
        jnp.stack(input_grads),
        small_out[0],
        small_out[1],
        rows_out[0],
        cols_out[0],
        small_out[2],
        rows_out[2],
        rows_out[3],
        rows_out[4],
        cols_out[2],
        channel_out[1],
        small_out[3],
        rows_out[5],
        channel_out[0],
        bn_totals[0],
        bn_totals[1],
        cols_out[3],
        small_out[4],
        rows_out[1],
        cols_out[1],
        small_out[5],
    )


def solution(mesh):
    return jax.shard_map(
        per_device,
        mesh=mesh,
        in_specs=(
            P("dp", "tensor", None),
            P("dp"),
            P("dp", None),
            P(("dp", "tensor")),
            P(("dp", "tensor")),
            P(None, "tensor"),
            P("tensor", None),
            P(("dp", "tensor")),
            P(None, "tensor"),
            P(None, "tensor"),
            P(None, "tensor"),
            P("tensor", None),
            P("tensor"),
            P(("dp", "tensor")),
            P("dp", None, "tensor"),
            P(None, "tensor"),
            P("tensor"),
            P("tensor"),
            P("tensor", "dp"),
            P(("dp", "tensor")),
            P(None, "tensor"),
            P("tensor", None),
            P(("dp", "tensor")),
            P("dp", "tensor", None),
        ),
        out_specs=(
            P("dp", "tensor", None),
            P("dp", "tensor", None),
            P(("dp", "tensor")),
            P(("dp", "tensor")),
            P("dp", "tensor"),
            P("tensor", "dp"),
            P(("dp", "tensor")),
            P("dp", "tensor"),
            P("dp", "tensor"),
            P("dp", "tensor"),
            P("tensor", "dp"),
            P("tensor"),
            P(("dp", "tensor")),
            P("dp", None, "tensor"),
            P(None, "tensor"),
            P("tensor"),
            P("tensor"),
            P("tensor", "dp"),
            P(("dp", "tensor")),
            P("dp", "tensor"),
            P("tensor", "dp"),
            P(("dp", "tensor")),
        ),
        check_vma=False,
    )
```

profile of v0, /device:TPU:0, one launch (start us, length us, event | category | flops | bytes accessed | tf_op | source)
XLA Modules:
  0.0 1393.8 jit_solution(16739801594121393604)
XLA Ops:
  17.3 42.7 %all-reduce.18 = (f32[1024]{0:T(1024)S(1)}, f32[1024]{0:T(1024)S(1)}, f32[1024]{0:T(1024)S(1)}, f32[1024]{0:T(1024)}, f32[1024]{0:T(1024)}, /*index=5*/f32[1024]{0:T(1024)}) all-reduce(f32[1024]{0:T(1024)S(1)} %dynamic-update-slice.1, f32[1024]{0:T(1024)S(1)} %convert_dynamic-update-slice_fusion, ...), channel_id=1, replica_groups=mesh['dp'=8,'tensor'=4] {'dp','tensor'}, use_global_device_ids=true, to_apply=%add.5 | all-reduce | flops 6144 | bytes 49152
  63.4 8.1 all_gather.82
  77.3 21.1 %reduce-scatter.26.cloned.1.call-done = bf16[64,1024]{1,0:T(8,128)(2,1)} async-done(((bf16[256,1024]{1,0:T(8,128)(2,1)}), bf16[64,1024]{1,0:T(8,128)(2,1)}) %reduce-scatter.26.cloned.1.call-update) | async-done | bytes 131088 | tf_op jit(solution)/shard_map/reduce_scatter | solution.py:61
  99.7 6.9 all_gather.92
  116.0 18.5 %reduce-scatter.34.cloned.1.call-done = bf16[64,1024]{1,0:T(8,128)(2,1)} async-done(((bf16[256,1024]{1,0:T(8,128)(2,1)}), bf16[64,1024]{1,0:T(8,128)(2,1)}) %reduce-scatter.34.cloned.1.call-update) | async-done | bytes 131088 | tf_op jit(solution)/shard_map/reduce_scatter | solution.py:61
  138.2 6.8 all_gather.84
  147.7 7.4 all_gather.93
  168.8 28.5 %all_gather.88 = bf16[256,1024]{1,0:T(8,128)(2,1)} all-gather(bf16[256,128]{1,0:T(8,128)(2,1)S(1)} %copy-done.141), channel_id=1, replica_groups=mesh['dp'=8,'tensor'=4] {'dp'}, dimensions={1}, use_global_device_ids=true | all-gather | bytes 589824 | tf_op jit(solution)/shard_map/all_gather | solution.py:392
  198.8 7.1 reduce-scatter.36.cloned.1.call-done
  208.6 7.2 all_gather.86
  215.8 7.3 all_gather.94
  227.4 22.1 %all-reduce.22 = (f32[256]{0:T(256)}, f32[]{:T(128)}, f32[256]{0:T(256)}, f32[]{:T(128)}) all-reduce(f32[256]{0:T(256)} %get-tuple-element.155, f32[]{:T(128)} %convert_reduce_fusion, f32[256]{0:T(256)} %get-tuple-element.130, f32[]{:T(128)} %convert_reduce_fusion.1), channel_id=1, replica_groups=mesh['dp'=8,'tensor'=4] {'dp'}, use_global_device_ids=true, to_apply=%region_35.36 | all-reduce | flops 514 | bytes 4112 | tf_op jit(solution)/shard_map/psum | solution.py:438
  256.0 17.8 %all-reduce.21 = (f32[256]{0:T(256)}, f32[256]{0:T(256)}) all-reduce(f32[256]{0:T(256)} %multiply_reduce_fusion.16, f32[256]{0:T(256)} %multiply_reduce_fusion.22), channel_id=1, replica_groups=mesh['dp'=8,'tensor'=4] {'dp'}, use_global_device_ids=true, to_apply=%region_39.40 | all-reduce | flops 512 | bytes 4096 | tf_op jit(solution)/shard_map/psum | solution.py:445
  282.3 15.6 %reduce-scatter.30.cloned.1.call-done = bf16[64,1024]{1,0:T(8,128)(2,1)} async-done(((bf16[256,1024]{1,0:T(8,128)(2,1)}), bf16[64,1024]{1,0:T(8,128)(2,1)}) %reduce-scatter.30.cloned.1.call-update) | async-done | bytes 131088 | tf_op jit(solution)/shard_map/reduce_scatter | solution.py:61
  300.4 22.2 %reduce-scatter.38.cloned.1.call-done = bf16[64,1024]{1,0:T(8,128)(2,1)} async-done(((bf16[256,1024]{1,0:T(8,128)(2,1)}), bf16[64,1024]{1,0:T(8,128)(2,1)}) %reduce-scatter.38.cloned.1.call-update) | async-done | bytes 131088 | tf_op jit(solution)/shard_map/reduce_scatter | solution.py:61
  326.4 6.8 all_gather.95
  336.6 7.5 all_gather.90
  349.8 8.9 reduce-scatter.40.cloned.1.call-done
  362.1 21.6 %reduce-scatter.32.cloned.1.call-done = bf16[64,1024]{1,0:T(8,128)(2,1)} async-done(((bf16[256,1024]{1,0:T(8,128)(2,1)}), bf16[64,1024]{1,0:T(8,128)(2,1)}) %reduce-scatter.32.cloned.1.call-update) | async-done | bytes 131088 | tf_op jit(solution)/shard_map/reduce_scatter | solution.py:61
  390.4 6.8 all_gather.96
  400.6 7.5 all_gather.100
  413.3 9.5 reduce-scatter.42.cloned.1.call-done
  424.4 23.1 %reduce-scatter.50.cloned.1.call-done = bf16[64,1024]{1,0:T(8,128)(2,1)} async-done(((bf16[256,1024]{1,0:T(8,128)(2,1)}), bf16[64,1024]{1,0:T(8,128)(2,1)}) %reduce-scatter.50.cloned.1.call-update) | async-done | bytes 131088 | tf_op jit(solution)/shard_map/reduce_scatter | solution.py:71
  452.1 6.9 all_gather.101
  461.5 7.4 all_gather.97
  471.4 22.0 %all-reduce.20 = (f32[256]{0:T(256)}, f32[256]{0:T(256)}, f32[256]{0:T(256)}, f32[256]{0:T(256)}) all-reduce(f32[256]{0:T(256)} %get-tuple-element.69, f32[256]{0:T(256)} %get-tuple-element.68, f32[256]{0:T(256)} %get-tuple-element.67, f32[256]{0:T(256)} %get-tuple-element.66), channel_id=1, replica_groups=mesh['dp'=8,'tensor'=4] {'dp'}, use_global_device_ids=true, to_apply=%region_73.74 | all-reduce | flops 1024 | bytes 8192 | tf_op jit(solution)/shard_map/psum | solution.py:486
  505.9 16.9 %reduce-scatter.44.cloned.1.call-done = bf16[64,1024]{1,0:T(8,128)(2,1)} async-done(((bf16[256,1024]{1,0:T(8,128)(2,1)}), bf16[64,1024]{1,0:T(8,128)(2,1)}) %reduce-scatter.44.cloned.1.call-update) | async-done | bytes 131088 | tf_op jit(solution)/shard_map/reduce_scatter | solution.py:71
  524.4 23.1 %reduce-scatter.52.cloned.1.call-done = bf16[64,1024]{1,0:T(8,128)(2,1)} async-done(((bf16[256,1024]{1,0:T(8,128)(2,1)}), bf16[64,1024]{1,0:T(8,128)(2,1)}) %reduce-scatter.52.cloned.1.call-update) | async-done | bytes 131088 | tf_op jit(solution)/shard_map/reduce_scatter | solution.py:71
  551.9 6.8 all_gather.102
  560.2 7.3 all_gather.98
  577.5 2.9 convolution_add_fusion.4
  580.4 4.1 copy.96
  584.6 10.1 reduce-scatter.54.cloned.1.call-done
  594.7 24.8 %reduce-scatter.46.cloned.1.call-done = bf16[64,1024]{1,0:T(8,128)(2,1)} async-done(((bf16[256,1024]{1,0:T(8,128)(2,1)}), bf16[64,1024]{1,0:T(8,128)(2,1)}) %reduce-scatter.46.cloned.1.call-update) | async-done | bytes 131088 | tf_op jit(solution)/shard_map/reduce_scatter | solution.py:71
  623.2 7.0 all_gather.99
  631.2 2.9 fusion.1
  638.2 7.3 all_gather.103
  645.4 2.9 fusion.3
  687.2 22.8 %all-reduce.19 = (f32[2]{0:T(128)}, f32[5,256]{1,0:T(8,128)}) all-reduce(f32[2]{0:T(128)S(1)} %fusion.14, f32[5,256]{1,0:T(8,128)S(1)} %add.620), channel_id=1, replica_groups=mesh['dp'=8,'tensor'=4] {'dp'}, use_global_device_ids=true, to_apply=%region_108.109 | all-reduce | flops 1282 | bytes 10256 | tf_op jit(solution)/shard_map/psum | solution.py:336
  714.7 37.5 %all-reduce.17 = (f32[1024]{0:T(1024)S(1)}, f32[1024]{0:T(1024)S(1)}, f32[1024]{0:T(1024)S(1)}, f32[1024]{0:T(1024)S(1)}, f32[1024]{0:T(1024)S(1)}, /*index=5*/f32[1024]{0:T(1024)S(1)}) all-reduce(f32[1024]{0:T(1024)S(1)} %add.628, f32[1024]{0:T(1024)S(1)} %add.629, ...), channel_id=34, replica_groups=mesh['dp'=8,'tensor'=4] {'dp','tensor'}, use_global_device_ids=true, to_apply=%region_85.86.clone | all-reduce | flops 6144 | bytes 49152
  756.7 61.1 %reduce-scatter.68.cloned.1.call-done = f32[256,128]{1,0:T(8,128)} async-done(((f32[256,1024]{1,0:T(8,128)}), f32[256,128]{1,0:T(8,128)}) %reduce-scatter.68.cloned.1.call-update) | async-done | bytes 131088 | tf_op jit(solution)/shard_map/reduce_scatter | solution.py:323
  817.9 66.5 %reduce-scatter.64.cloned.1.call-done = f32[128,256]{1,0:T(8,128)} async-done(((f32[1024,256]{1,0:T(8,128)}), f32[128,256]{1,0:T(8,128)}) %reduce-scatter.64.cloned.1.call-update) | async-done | bytes 131088 | tf_op jit(solution)/shard_map/reduce_scatter | solution.py:315
  884.4 66.6 %reduce-scatter.62.cloned.1.call-done = f32[128,256]{1,0:T(8,128)} async-done(((f32[1024,256]{1,0:T(8,128)}), f32[128,256]{1,0:T(8,128)}) %reduce-scatter.62.cloned.1.call-update) | async-done | bytes 131088 | tf_op jit(solution)/shard_map/reduce_scatter | solution.py:314
  951.0 66.5 %reduce-scatter.66.cloned.1.call-done = f32[128,256]{1,0:T(8,128)} async-done(((f32[1024,256]{1,0:T(8,128)}), f32[128,256]{1,0:T(8,128)}) %reduce-scatter.66.cloned.1.call-update) | async-done | bytes 131088 | tf_op jit(solution)/shard_map/reduce_scatter | solution.py:316
  1017.5 92.2 %reduce-scatter.74.cloned.1.call-done = f32[1024,128]{1,0:T(8,128)} async-done(((f32[1024,1024]{1,0:T(8,128)}), f32[1024,128]{1,0:T(8,128)}) %reduce-scatter.74.cloned.1.call-update) | async-done | bytes 524304 | tf_op jit(solution)/shard_map/reduce_scatter | solution.py:322
  1109.7 91.9 %reduce-scatter.72.cloned.1.call-done = f32[128,1024]{1,0:T(8,128)} async-done(((f32[1024,1024]{1,0:T(8,128)}), f32[128,1024]{1,0:T(8,128)}) %reduce-scatter.72.cloned.1.call-update) | async-done | bytes 524304 | tf_op jit(solution)/shard_map/reduce_scatter | solution.py:313
  1201.6 92.8 %reduce-scatter.60.cloned.1.call-done = f32[1024,128]{1,0:T(8,128)} async-done(((f32[1024,1024]{1,0:T(8,128)}), f32[1024,128]{1,0:T(8,128)}) %reduce-scatter.60.cloned.1.call-update) | async-done | bytes 524304 | tf_op jit(solution)/shard_map/reduce_scatter | solution.py:321
  1294.3 91.9 %reduce-scatter.58.cloned.1.call-done = f32[128,1024]{1,0:T(8,128)} async-done(((f32[1024,1024]{1,0:T(8,128)}), f32[128,1024]{1,0:T(8,128)}) %reduce-scatter.58.cloned.1.call-update) | async-done | bytes 524304 | tf_op jit(solution)/shard_map/reduce_scatter | solution.py:312
  (773 shorter events, 201.1 us)
Async XLA Ops:
  8.0 326.9 %copy-start = (bf16[1024,1024]{1,0:T(8,128)(2,1)S(1)}, bf16[1024,1024]{1,0:T(8,128)(2,1)}, u32[]{:S(2)}) copy-start(bf16[1024,1024]{1,0:T(8,128)(2,1)} %param.45) | copy-start | bytes 6291460
  8.0 90.3 %reduce-scatter.26.cloned.1.call-start = ((), (), s32[]{:S(2)}) async-start(), calls=%async_computation.25 | async-start | bytes 655360 | tf_op jit(solution)/shard_map/reduce_scatter | solution.py:61
  60.0 77.1 %copy-start.136 = (f32[1024]{0:T(1024)}, f32[1024]{0:T(1024)S(1)}, u32[]{:S(2)}) copy-start(f32[1024]{0:T(1024)S(1)} %get-tuple-element.88) | copy-start | bytes 12292
  77.2 57.4 %reduce-scatter.34.cloned.1.call-start = ((), (), s32[]{:S(2)}) async-start(), calls=%async_computation.30 | async-start | bytes 655360 | tf_op jit(solution)/shard_map/reduce_scatter | solution.py:61
  112.3 85.0 %all-gather.2.cloned.1.call-start = ((), (), s32[]{:S(2)}) async-start(), calls=%async_computation.27 | async-start | bytes 1179648 | tf_op jit(solution)/shard_map/all_gather | solution.py:391
  112.9 85.9 %reduce-scatter.28.cloned.1.call-start = ((), (), s32[]{:S(2)}) async-start(), calls=%async_computation.26 | async-start | bytes 655360 | tf_op jit(solution)/shard_map/reduce_scatter | solution.py:61
  159.0 46.9 %reduce-scatter.36.cloned.1.call-start = ((), (), s32[]{:S(2)}) async-start(), calls=%async_computation.31 | async-start | bytes 655360 | tf_op jit(solution)/shard_map/reduce_scatter | solution.py:61
  162.1 43.8 %copy-start.50 = (bf16[64,1024]{1,0:T(8,128)(2,1)S(1)}, bf16[64,1024]{1,0:T(8,128)(2,1)}, u32[]{:S(2)}) copy-start(bf16[64,1024]{1,0:T(8,128)(2,1)} %reduce-scatter.34.cloned.1.call-done) | copy-start | bytes 393220
  163.2 134.7 %reduce-scatter.30.cloned.1.call-start = ((), (), s32[]{:S(2)}) async-start(), calls=%async_computation.28 | async-start | bytes 655360 | tf_op jit(solution)/shard_map/reduce_scatter | solution.py:61
  278.0 44.7 %reduce-scatter.38.cloned.1.call-start = ((), (), s32[]{:S(2)}) async-start(), calls=%async_computation.32 | async-start | bytes 655360 | tf_op jit(solution)/shard_map/reduce_scatter | solution.py:61
  282.2 76.5 %reduce-scatter.40.cloned.1.call-start = ((), (), s32[]{:S(2)}) async-start(), calls=%async_computation.33 | async-start | bytes 655360 | tf_op jit(solution)/shard_map/reduce_scatter | solution.py:61
  336.5 47.1 %reduce-scatter.32.cloned.1.call-start = ((), (), s32[]{:S(2)}) async-start(), calls=%async_computation.29 | async-start | bytes 655360 | tf_op jit(solution)/shard_map/reduce_scatter | solution.py:61
  349.8 73.0 %reduce-scatter.42.cloned.1.call-start = ((), (), s32[]{:S(2)}) async-start(), calls=%async_computation.34 | async-start | bytes 655360 | tf_op jit(solution)/shard_map/reduce_scatter | solution.py:71
  400.6 46.9 %reduce-scatter.50.cloned.1.call-start = ((), (), s32[]{:S(2)}) async-start(), calls=%async_computation.38 | async-start | bytes 655360 | tf_op jit(solution)/shard_map/reduce_scatter | solution.py:71
  413.0 37.2 %copy-start.200 = (f32[64]{0:T(128)S(1)}, f32[64]{0:T(128)}, u32[]{:S(2)}) copy-start(f32[64]{0:T(128)} %add_rsqrt_fusion.2) | copy-start | bytes 772
  413.0 37.2 %copy-start.234 = (f32[64]{0:T(128)S(1)}, f32[64]{0:T(128)}, u32[]{:S(2)}) copy-start(f32[64]{0:T(128)} %copy-done.233) | copy-start | bytes 772
  413.0 37.2 %copy-start.236 = (f32[64]{0:T(128)S(1)}, f32[64]{0:T(128)}, u32[]{:S(2)}) copy-start(f32[64]{0:T(128)} %copy-done.235) | copy-start | bytes 772
  413.0 46.9 %copy-start.57 = (f32[256,256]{1,0:T(8,128)S(1)}, f32[256,256]{1,0:T(8,128)}, u32[]{:S(2)}) copy-start(f32[256,256]{1,0:T(8,128)} %get-tuple-element.156) | copy-start | bytes 786436
  413.0 46.9 %copy-start.128 = (bf16[256,1024]{1,0:T(8,128)(2,1)S(1)}, bf16[256,1024]{1,0:T(8,128)(2,1)}, u32[]{:S(2)}) copy-start(bf16[256,1024]{1,0:T(8,128)(2,1)} %all_gather.88) | copy-start | bytes 1572868
  413.0 46.9 %copy-start.149 = (f32[256]{0:T(256)S(1)}, f32[256]{0:T(256)}, u32[]{:S(2)}) copy-start(f32[256]{0:T(256)} %param.40) | copy-start | bytes 3076
  413.0 46.8 %copy-start.154 = (f32[256]{0:T(256)S(1)}, f32[256]{0:T(256)}, u32[]{:S(2)}) copy-start(f32[256]{0:T(256)} %copy-done.153) | copy-start | bytes 3076
  413.0 46.8 %copy-start.174 = (f32[256]{0:T(256)S(1)}, f32[256]{0:T(256)}, u32[]{:S(2)}) copy-start(f32[256]{0:T(256)} %copy-done.173) | copy-start | bytes 3076
  413.0 46.8 %copy-start.241 = (f32[256]{0:T(256)S(1)}, f32[256]{0:T(256)}, u32[]{:S(2)}) copy-start(f32[256]{0:T(256)} %param.41) | copy-start | bytes 3076
  413.1 109.7 %reduce-scatter.44.cloned.1.call-start = ((), (), s32[]{:S(2)}) async-start(), calls=%async_computation.35 | async-start | bytes 655360 | tf_op jit(solution)/shard_map/reduce_scatter | solution.py:71
  504.2 43.3 %copy-start.18 = (f32[64,1024]{1,0:T(8,128)S(1)}, f32[64,1024]{1,0:T(8,128)}, u32[]{:S(2)}) copy-start(f32[64,1024]{1,0:T(8,128)} %copy-done.17) | copy-start | bytes 786436
  504.2 43.3 %copy-start.105 = (f32[64,1024]{1,0:T(8,128)S(1)}, f32[64,1024]{1,0:T(8,128)}, u32[]{:S(2)}) copy-start(f32[64,1024]{1,0:T(8,128)} %get-tuple-element.123) | copy-start | bytes 786436
  504.2 43.3 %copy-start.181 = (f32[64]{0:T(128)S(1)}, f32[64]{0:T(128)}, u32[]{:S(2)}) copy-start(f32[64]{0:T(128)} %copy-done.180) | copy-start | bytes 772
  504.3 43.3 %copy-start.208 = (f32[64]{0:T(128)S(1)}, f32[64]{0:T(128)}, u32[]{:S(2)}) copy-start(f32[64]{0:T(128)} %copy-done.207) | copy-start | bytes 772
  504.3 43.3 %reduce-scatter.52.cloned.1.call-start = ((), (), s32[]{:S(2)}) async-start(), calls=%async_computation.39 | async-start | bytes 655360 | tf_op jit(solution)/shard_map/reduce_scatter | solution.py:71
  504.4 45.7 %copy-start.80 = (bf16[256,256]{1,0:T(8,128)(2,1)}, bf16[256,256]{1,0:T(8,128)(2,1)S(1)}, u32[]{:S(2)}) copy-start(bf16[256,256]{1,0:T(8,128)(2,1)S(1)} %multiply_convert_fusion.7) | copy-start | bytes 393220
  505.7 44.4 %copy-start.108 = (f32[64,1024]{1,0:T(8,128)S(1)}, f32[64,1024]{1,0:T(8,128)}, u32[]{:S(2)}) copy-start(f32[64,1024]{1,0:T(8,128)} %get-tuple-element.125) | copy-start | bytes 786436
  505.7 53.0 %copy-start.27 = (bf16[256,1024]{1,0:T(8,128)(2,1)S(1)}, bf16[256,1024]{1,0:T(8,128)(2,1)}, u32[]{:S(2)}) copy-start(bf16[256,1024]{1,0:T(8,128)(2,1)} %param.35) | copy-start | bytes 1572868
  505.8 88.9 %reduce-scatter.54.cloned.1.call-start = ((), (), s32[]{:S(2)}) async-start(), calls=%async_computation.40 | async-start | bytes 655360 | tf_op jit(solution)/shard_map/reduce_scatter | solution.py:71
  505.9 62.3 %copy-start.142 = (f32[2,256]{1,0:T(2,128)}, f32[2,256]{1,0:T(2,128)S(1)}, u32[]{:S(2)}) copy-start(f32[2,256]{1,0:T(2,128)S(1)} %log_add_fusion.1) | copy-start | bytes 6148
  572.4 47.0 %reduce-scatter.46.cloned.1.call-start = ((), (), s32[]{:S(2)}) async-start(), calls=%async_computation.36 | async-start | bytes 655360 | tf_op jit(solution)/shard_map/reduce_scatter | solution.py:71
  575.8 134.2 %all-reduce.25.cloned.1.call-start = ((), (), s32[]{:S(2)}) async-start(), calls=%async_computation.51 | async-start | bytes 4194304
  584.5 127.4 %reduce-scatter.48.cloned.1.call-start = ((), (), s32[]{:S(2)}) async-start(), calls=%async_computation.37 | async-start | bytes 655360 | tf_op jit(solution)/shard_map/reduce_scatter | solution.py:71
  636.5 75.4 %reduce-scatter.56.cloned.1.call-start = ((), (), s32[]{:S(2)}) async-start(), calls=%async_computation.41 | async-start | bytes 655360 | tf_op jit(solution)/shard_map/reduce_scatter | solution.py:71
  650.8 106.0 %reduce-scatter.70.cloned.1.call-start = ((), (), s32[]{:S(2)}) async-start(), calls=%async_computation.48 | async-start | bytes 1179648 | tf_op jit(solution)/shard_map/reduce_scatter | solution.py:324
  653.9 164.0 %reduce-scatter.68.cloned.1.call-start = ((), (), s32[]{:S(2)}) async-start(), calls=%async_computation.47 | async-start | bytes 1179648 | tf_op jit(solution)/shard_map/reduce_scatter | solution.py:323
  657.3 227.1 %reduce-scatter.64.cloned.1.call-start = ((), (), s32[]{:S(2)}) async-start(), calls=%async_computation.45 | async-start | bytes 1179648 | tf_op jit(solution)/shard_map/reduce_scatter | solution.py:315
  659.1 291.9 %reduce-scatter.62.cloned.1.call-start = ((), (), s32[]{:S(2)}) async-start(), calls=%async_computation.44 | async-start | bytes 1179648 | tf_op jit(solution)/shard_map/reduce_scatter | solution.py:314
  661.0 356.5 %reduce-scatter.66.cloned.1.call-start = ((), (), s32[]{:S(2)}) async-start(), calls=%async_computation.46 | async-start | bytes 1179648 | tf_op jit(solution)/shard_map/reduce_scatter | solution.py:316
  662.8 446.9 %reduce-scatter.74.cloned.1.call-start = ((), (), s32[]{:S(2)}) async-start(), calls=%async_computation.50 | async-start | bytes 4718592 | tf_op jit(solution)/shard_map/reduce_scatter | solution.py:322
  667.9 533.6 %reduce-scatter.72.cloned.1.call-start = ((), (), s32[]{:S(2)}) async-start(), calls=%async_computation.49 | async-start | bytes 4718592 | tf_op jit(solution)/shard_map/reduce_scatter | solution.py:313
  672.7 621.6 %reduce-scatter.60.cloned.1.call-start = ((), (), s32[]{:S(2)}) async-start(), calls=%async_computation.43 | async-start | bytes 4718592 | tf_op jit(solution)/shard_map/reduce_scatter | solution.py:321
  677.7 708.5 %reduce-scatter.58.cloned.1.call-start = ((), (), s32[]{:S(2)}) async-start(), calls=%async_computation.42 | async-start | bytes 4718592 | tf_op jit(solution)/shard_map/reduce_scatter | solution.py:312
  710.1 676.2 %copy-start.1 = (bf16[1024,1024]{1,0:T(8,128)(2,1)S(1)}, bf16[1024,1024]{1,0:T(8,128)(2,1)}, u32[]{:S(2)}) copy-start(bf16[1024,1024]{1,0:T(8,128)(2,1)} %param.45) | copy-start | bytes 6291460
  (228 other events, 2010.6 us)
Sparse Core Ops, SparseCore 0:
  77.3 20.9 reduce-scatter.25
  112.4 22.0 reduce-scatter.33
  159.1 21.9 reduce-scatter.27
  184.2 21.6 reduce-scatter.35
  278.1 19.7 reduce-scatter.29
  301.0 21.6 reduce-scatter.37
  336.6 22.0 reduce-scatter.39
  361.9 21.6 reduce-scatter.31
  400.7 22.0 reduce-scatter.41
  425.8 21.6 reduce-scatter.49
  504.4 18.3 reduce-scatter.43
  525.9 21.6 reduce-scatter.51
  572.6 22.0 reduce-scatter.53
  597.7 21.6 reduce-scatter.45
  636.6 22.0 reduce-scatter.47
  661.2 21.7 reduce-scatter.55
  686.8 63.9 reduce-scatter.69
  755.0 62.8 reduce-scatter.67
  821.9 62.4 reduce-scatter.63
  888.6 62.3 reduce-scatter.61
  955.0 62.4 reduce-scatter.65
  1022.2 87.4 reduce-scatter.73
  1113.9 87.6 reduce-scatter.71
  1206.1 88.2 reduce-scatter.59
  1298.5 87.6 reduce-scatter.57
Sparse Core Ops, SparseCore 1:
  114.9 40.8 all-gather.1
  584.6 102.4 all-reduce.24
where the time goes:
time: 1400 us; the launch traced here: 1390 us
  waiting for transfers between devices  853 us (61%)
  blocking collectives  308 us (22%)
  matrix products  88.3 us (6%)
  other arithmetic  80.2 us (6%)
  local copies, waits for them, and re-layouts  42.9 us (3%)
  between operations  19.8 us (1%)
    reduce_scatter x8, waiting for transfers between devices, narrow_sum(): lax.psum_scatter(partial_sum.astype(jnp.bfloat16), 'tensor', scatter_dime...  115 us
    reduce_scatter x8, waiting for transfers between devices, narrow_grad(): lax.psum_scatter(partial_sum.astype(jnp.bfloat16), 'tensor', scatter_dime...  107 us
    reduce_scatter x1, waiting for transfers between devices, share_grads(): lax.psum_scatter(first_down, 'dp', scatter_dimension=1, tiled=True)  92.8 us
    reduce_scatter x1, waiting for transfers between devices, share_grads(): lax.psum_scatter(second_down, 'dp', scatter_dimension=1, tiled=True)  92.2 us
    reduce_scatter x1, waiting for transfers between devices, share_grads(): lax.psum_scatter(first_up, 'dp', scatter_dimension=0, tiled=True)  91.9 us
    reduce_scatter x1, waiting for transfers between devices, share_grads(): lax.psum_scatter(second_up, 'dp', scatter_dimension=0, tiled=True)  91.9 us
    unnamed x2, blocking collectives  80.2 us
    reduce_scatter x1, waiting for transfers between devices, share_grads(): lax.psum_scatter(query_grad, 'dp', scatter_dimension=0, tiled=True)  66.6 us
  transfers between devices with their start and end apart: 27, of which 21 were waited for; matrix products, arithmetic and copies ran while one was open for 8% of the time, Pallas kernels for 0%

commit v1 on v0

v1 whole, which is shorter than its diff:
```python
import jax
import jax.numpy as jnp
from jax import lax
from jax.sharding import PartitionSpec as P

DH = 128
KW = 5
SPAN = 10
REACH = 128
EPSILON = 1e-05
MASKED_SCORE = -1000000000.0
BF = jnp.bfloat16
F32 = jnp.float32


def product(left, right):
    return jnp.dot(left, right, preferred_element_type=F32)


def inner_rows(left, right):
    return lax.dot_general(left, right, (((0,), (0,)), ((), ())), preferred_element_type=F32)


def times_back(left, right):
    return lax.dot_general(left, right, (((1,), (1,)), ((), ())), preferred_element_type=F32)


def norm_unit(values):
    centre = jnp.mean(values, axis=-1, keepdims=True)
    centred = values - centre
    inverse = lax.rsqrt(jnp.mean(centred * centred, axis=-1, keepdims=True) + EPSILON)
    return centred * inverse, inverse


def norm_back(grad_out, unit_rows, inverse, norm_gain):
    grad_unit = grad_out * norm_gain
    first_mean = jnp.mean(grad_unit, axis=-1, keepdims=True)
    second_mean = jnp.mean(grad_unit * unit_rows, axis=-1, keepdims=True)
    return (
        inverse * (grad_unit - first_mean - unit_rows * second_mean),
        jnp.sum(grad_out * unit_rows, axis=0),
    )


def silu_slope(values):
    gate_value = jax.nn.sigmoid(values)
    return gate_value * (1.0 + values * (1.0 - gate_value))


def swap(value, axis, bit):
    size = lax.axis_size(axis)
    return lax.ppermute(value, axis, [(place, place ^ bit) for place in range(size)])


def bit_of(axis, bit):
    return (lax.axis_index(axis) & bit) != 0


def pick(value, axis, second):
    halves = (lax.index_in_dim(value, 0, axis, False), lax.index_in_dim(value, 1, axis, False))
    return jnp.where(second, halves[1], halves[0])


def ordered(mine, theirs, axis, second):
    return jnp.stack(
        [jnp.where(second, theirs, mine), jnp.where(second, mine, theirs)], axis=axis
    )


def widen(half):
    rows = half.shape[0] // 2
    other = swap(half, "tensor", 1)
    low = bit_of("tensor", 1)
    shape = (2, rows, half.shape[1])
    return ordered(half.reshape(shape), other.reshape(shape), 1, low).reshape(
        4 * rows, half.shape[1]
    )


def narrow(partial_sum):
    rows = partial_sum.shape[0] // 4
    low = bit_of("tensor", 1)
    blocks = partial_sum.reshape(2, 2, rows, partial_sum.shape[1])
    sent = pick(blocks, 1, jnp.logical_not(low)).astype(BF)
    summed = (pick(blocks, 1, low) + swap(sent, "tensor", 1).astype(F32)).astype(BF)
    return summed


def narrow_sum(partial_sum):
    summed = narrow(partial_sum)
    other = swap(summed, "tensor", 2)
    total = summed.astype(F32) + other.astype(F32)
    return total.reshape(total.shape[0] * total.shape[1], total.shape[2])


def narrow_last(partial_sum):
    summed = narrow(partial_sum)
    high = bit_of("tensor", 2)
    sent = pick(summed, 0, jnp.logical_not(high))
    return pick(summed, 0, high).astype(F32) + swap(sent, "tensor", 2).astype(F32)


def gather_axis(block, axis):
    size = lax.axis_size(axis)
    bit = size // 2
    held = block
    depth = 0
    while bit:
        held = ordered(held, swap(held, axis, bit), depth, bit_of(axis, bit))
        depth += 1
        bit //= 2
    return held.reshape((size,) + block.shape)


def sum_axis(value, axis):
    bit = 1
    while bit < lax.axis_size(axis):
        value = value + swap(value, axis, bit)
        bit *= 2
    return value


def scatter_rows(partial_sum):
    size = lax.axis_size("dp")
    rows, columns = partial_sum.shape
    levels = size.bit_length() - 1
    held = partial_sum.reshape((2,) * levels + (rows // size, columns))
    for level in range(levels):
        axis = levels - 1 - level
        mine = bit_of("dp", 1 << level)
        sent = pick(held, axis, jnp.logical_not(mine)).astype(BF)
        held = pick(held, axis, mine) + swap(sent, "dp", 1 << level).astype(F32)
    return held


def relative_table(length):
    places = jnp.arange(length, dtype=jnp.int32)
    return jnp.clip(places[None, :] - places[:, None], -REACH, REACH).astype(F32) / REACH


def depthwise(padded, depth_weight, length):
    convolved = depth_weight[0] * padded[0:length]
    for offset in range(1, KW):
        convolved = convolved + depth_weight[offset] * padded[offset : offset + length]
    return convolved


def heads_of(rows, head_count):
    return rows.reshape(rows.shape[0], head_count, DH)


def attend(gathered, query_weight, key_weight, value_weight, slopes, relative, valid_keys):
    head_count = slopes.shape[0]
    length = gathered.shape[0]
    query = heads_of(product(gathered, query_weight).astype(BF), head_count)
    keys = heads_of(product(gathered, key_weight).astype(BF), head_count)
    values = heads_of(product(gathered, value_weight).astype(BF), head_count)
    scores = jnp.einsum("qhd,khd->hqk", query, keys, preferred_element_type=F32) * DH ** (-0.5)
    scores = scores + slopes[:, None, None] * relative[None]
    scores = jnp.where(valid_keys[None, None, :], scores, MASKED_SCORE)
    raised = jnp.exp(scores - jnp.max(scores, axis=-1, keepdims=True))
    weights = raised / jnp.sum(raised, axis=-1, keepdims=True)
    context = jnp.einsum("hqk,khd->qhd", weights.astype(BF), values, preferred_element_type=F32)
    context = context.reshape(length, head_count * DH).astype(BF)
    return context, (query, keys, values, weights)


def attend_back(grad_context, kept, relative):
    query, keys, values, weights = kept
    length, head_count, _ = query.shape
    grad_heads = heads_of(grad_context, head_count)
    width = head_count * DH
    grad_value = jnp.einsum(
        "hqk,qhd->khd", weights.astype(BF), grad_heads, preferred_element_type=F32
    )
    grad_weights = jnp.einsum("qhd,khd->hqk", grad_heads, values, preferred_element_type=F32)
    grad_scores = weights * (
        grad_weights - jnp.sum(weights * grad_weights, axis=-1, keepdims=True)
    )
    grad_scores = grad_scores.astype(BF)
    grad_slopes = jnp.sum(grad_scores.astype(F32) * relative[None], axis=(1, 2))
    grad_query = jnp.einsum("hqk,khd->qhd", grad_scores, keys, preferred_element_type=F32)
    grad_key = jnp.einsum("hqk,qhd->khd", grad_scores, query, preferred_element_type=F32)
    grads = tuple(
        (part * scale).reshape(length, width).astype(BF)
        for part, scale in (
            (grad_query, DH ** (-0.5)),
            (grad_key, DH ** (-0.5)),
            (grad_value, 1.0),
        )
    )
    return grads, grad_slopes


def both(parts):
    return jnp.concatenate(parts, axis=0)


def per_device(
    frames,
    lengths,
    span_starts,
    mask_vector,
    ffn1_gain,
    ffn1_up,
    ffn1_down,
    attn_gain,
    query_weight,
    key_weight,
    value_weight,
    output_weight,
    rel_slope,
    conv_gain,
    conv_up,
    conv_depth,
    bn_scale,
    bn_shift,
    conv_down,
    ffn2_gain,
    ffn2_up,
    ffn2_down,
    final_gain,
    cotangent,
):
    batches, row_count, width = frames.shape
    length = row_count * lax.axis_size("tensor")
    low_bit = bit_of("tensor", 1)
    high_bit = bit_of("tensor", 2)
    relative = relative_table(length)
    places = jnp.arange(length, dtype=jnp.int32)
    channels = conv_depth.shape[1]
    each = range(batches)

    small = jnp.stack(
        [mask_vector.astype(F32), ffn1_gain, attn_gain, conv_gain, ffn2_gain, final_gain]
    )
    small = gather_axis(gather_axis(small, "tensor"), "dp")
    small = jnp.moveaxis(small, 2, 0).reshape(6, width)
    mask_full, gain_one, gain_attn, gain_conv, gain_two, gain_final = (
        small[index] for index in range(6)
    )

    halves = ordered(frames, swap(frames, "tensor", 2), 1, high_bit)
    others = swap(halves, "tensor", 1)
    wholes = ordered(halves, others, 2, low_bit).reshape(batches, length, width)
    grads_out = ordered(cotangent, swap(cotangent, "tensor", 2), 1, high_bit)
    grads_out = grads_out.reshape(batches, 2 * row_count, width)

    up_full = gather_axis(conv_up.reshape(conv_up.shape[0], 2 * channels), "dp")
    up_full = up_full.reshape(width, 2 * channels)
    down_full = gather_axis(conv_down, "dp")
    down_full = jnp.moveaxis(down_full, 0, 1).reshape(conv_down.shape[0], width)

    def half_of(whole):
        blocks = whole.reshape((2, 2, row_count) + whole.shape[1:])
        return pick(blocks, 1, low_bit).reshape((2 * row_count,) + whole.shape[1:])

    valid = [places < lengths[b] for b in each]
    valid_col = [valid[b].astype(F32)[:, None] for b in each]
    masked, masked_half = [], []
    for b in each:
        starts = span_starts[b]
        covered = jnp.any(
            (starts[:, None] <= places[None, :]) & (places[None, :] < starts[:, None] + SPAN),
            axis=0,
        )
        masked.append(covered & valid[b])
        masked_half.append(half_of(masked[b]))

    unit_in, inv_in, gathered_one, hidden_one, active_one, stream_one = [], [], [], [], [], []
    for b in each:
        inputs = jnp.where(masked[b][:, None], mask_full[None, :], wholes[b].astype(F32))
        unit_rows, inverse = norm_unit(inputs)
        gathered_one.append((unit_rows * gain_one).astype(BF))
        inputs_half = half_of(inputs)
        hidden_one.append(product(gathered_one[b], ffn1_up))
        active_one.append(jax.nn.silu(hidden_one[b]).astype(BF))
        branch = narrow_sum(product(active_one[b], ffn1_down))
        stream_one.append(inputs_half + 0.5 * branch)

    unit_attn, inv_attn, gathered_attn, kept_attn, context, stream_two = [], [], [], [], [], []
    for b in each:
        unit_rows, inverse = norm_unit(stream_one[b])
        unit_attn.append(unit_rows)
        inv_attn.append(inverse)
        gathered_attn.append(widen((unit_rows * gain_attn).astype(BF)))
        rows, kept = attend(
            gathered_attn[b], query_weight, key_weight, value_weight, rel_slope, relative, valid[b]
        )
        context.append(rows)
        kept_attn.append(kept)
        stream_two.append(stream_one[b] + narrow_sum(product(rows, output_weight)))

    unit_conv, inv_conv, gathered_conv, value_half, gate, padded, convolved = (
        [], [], [], [], [], [], []
    )
    stats = []
    for b in each:
        unit_rows, inverse = norm_unit(stream_two[b])
        unit_conv.append(unit_rows)
        inv_conv.append(inverse)
        gathered_conv.append(widen((unit_rows * gain_conv).astype(BF)))
        mixed = product(gathered_conv[b], up_full)
        value_half.append(mixed[:, :channels])
        gate.append(jax.nn.sigmoid(mixed[:, channels:]))
        gated = value_half[b] * gate[b] * valid_col[b]
        padded.append(jnp.pad(gated, ((KW // 2, KW // 2), (0, 0))))
        convolved.append(depthwise(padded[b], conv_depth, length))
        count = lengths[b].astype(F32)
        mean = jnp.sum(convolved[b] * valid_col[b], axis=0) / count
        centred = (convolved[b] - mean) * valid_col[b]
        spread = jnp.sum(centred * centred, axis=0)
        held = jnp.stack([jnp.broadcast_to(count, mean.shape), mean, spread])
        bit = 1
        while bit < lax.axis_size("dp"):
            theirs = swap(held, "dp", bit)
            total = held[0] + theirs[0]
            apart = held[1] - theirs[1]
            held = jnp.stack(
                [
                    total,
                    (held[0] * held[1] + theirs[0] * theirs[1]) / total,
                    held[2] + theirs[2] + apart * apart * (held[0] * theirs[0] / total),
                ]
            )
            bit *= 2
        stats.append((held[0], held[1], lax.rsqrt(held[2] / held[0] + EPSILON)))

    unit_bn, centred_conv, shaped, activated, stream_three = [], [], [], [], []
    for b in each:
        count, centre, bn_inverse = stats[b]
        centred_conv.append(convolved[b] - centre)
        unit_bn.append(centred_conv[b] * bn_inverse)
        shaped.append(unit_bn[b] * bn_scale + bn_shift)
        activated.append(jax.nn.silu(shaped[b]).astype(BF))
        stream_three.append(stream_two[b] + narrow_sum(product(activated[b], down_full)))

    unit_two, inv_two, gathered_two, hidden_two, active_two = [], [], [], [], []
    outputs, grad_four, grad_final = [], [], []
    for b in each:
        unit_rows, inverse = norm_unit(stream_three[b])
        unit_two.append(unit_rows)
        inv_two.append(inverse)
        gathered_two.append(widen((unit_rows * gain_two).astype(BF)))
        hidden_two.append(product(gathered_two[b], ffn2_up))
        active_two.append(jax.nn.silu(hidden_two[b]).astype(BF))
        branch = narrow_sum(product(active_two[b], ffn2_down))
        stream_four = stream_three[b] + 0.5 * branch
        unit_rows, inverse = norm_unit(stream_four)
        rows_out = (unit_rows * gain_final).astype(BF)
        outputs.append(pick(rows_out.reshape(2, row_count, width), 0, high_bit))
        grad, gain_sum = norm_back(grads_out[b].astype(F32), unit_rows, inverse, gain_final)
        grad_four.append(grad)
        grad_final.append(gain_sum)

    grad_three, grad_gain_two, branch_grads, hidden_grads = [], [], [], []
    for b in each:
        grad_branch = widen((0.5 * grad_four[b]).astype(BF))
        branch_grads.append(grad_branch)
        grad_hidden = (times_back(grad_branch, ffn2_down) * silu_slope(hidden_two[b])).astype(BF)
        hidden_grads.append(grad_hidden)
        grad_normed = narrow_sum(times_back(grad_hidden, ffn2_up))
        grad, gain_sum = norm_back(grad_normed, unit_two[b], inv_two[b], gain_two)
        grad_three.append(grad_four[b] + grad)
        grad_gain_two.append(gain_sum)
    ffn2_down_grad = scatter_rows(inner_rows(both(branch_grads), both(active_two))).T
    ffn2_up_grad = scatter_rows(inner_rows(both(gathered_two), both(hidden_grads)))

    grad_shaped, sums_bn, branch_grads = [], [], []
    for b in each:
        grad_branch = widen(grad_three[b].astype(BF))
        branch_grads.append(grad_branch)
        grad_shaped.append(times_back(grad_branch, down_full) * silu_slope(shaped[b]))
        sums_bn.append(
            sum_axis(
                jnp.stack(
                    [
                        jnp.sum(grad_shaped[b], axis=0),
                        jnp.sum(grad_shaped[b] * unit_bn[b], axis=0),
                    ]
                ),
                "dp",
            )
        )
    conv_down_grad = scatter_rows(inner_rows(both(branch_grads), both(activated))).T
    grad_two, grad_gain_conv, mixed_grads, grad_depth = [], [], [], None
    for b in each:
        count, centre, bn_inverse = stats[b]
        sum_shift, sum_scale = sums_bn[b][0], sums_bn[b][1]
        grad_centre = -bn_inverse * bn_scale * sum_shift
        grad_spread = -bn_inverse * bn_inverse * bn_scale * sum_scale
        grad_conv = (
            grad_shaped[b] * bn_scale * bn_inverse
            + valid_col[b] * (grad_centre + grad_spread * centred_conv[b]) / count
        )
        grad_padded = jnp.pad(grad_conv, ((KW // 2, KW // 2), (0, 0)))
        grad_gated = conv_depth[0] * grad_padded[2 * (KW // 2) : 2 * (KW // 2) + length]
        for offset in range(1, KW):
            begin = 2 * (KW // 2) - offset
            grad_gated = grad_gated + conv_depth[offset] * grad_padded[begin : begin + length]
        fresh = jnp.stack(
            [
                jnp.sum(grad_conv * padded[b][offset : offset + length], axis=0)
                for offset in range(KW)
            ]
        )
        grad_depth = fresh if grad_depth is None else grad_depth + fresh
        grad_gated = grad_gated * valid_col[b]
        grad_mixed = jnp.concatenate(
            [
                grad_gated * gate[b],
                grad_gated * value_half[b] * gate[b] * (1.0 - gate[b]),
            ],
            axis=1,
        ).astype(BF)
        mixed_grads.append(grad_mixed)
        grad_normed = narrow_sum(times_back(grad_mixed, up_full))
        grad, gain_sum = norm_back(grad_normed, unit_conv[b], inv_conv[b], gain_conv)
        grad_two.append(grad_three[b] + grad)
        grad_gain_conv.append(gain_sum)
    conv_up_grad = scatter_rows(inner_rows(both(gathered_conv), both(mixed_grads)))

    grad_one, grad_gain_attn, branch_grads, three_grads, grad_slopes = [], [], [], [], None
    for b in each:
        grad_branch = widen(grad_two[b].astype(BF))
        branch_grads.append(grad_branch)
        grad_context = times_back(grad_branch, output_weight).astype(BF)
        (grad_query, grad_key, grad_value), fresh = attend_back(
            grad_context, kept_attn[b], relative
        )
        grad_slopes = fresh if grad_slopes is None else grad_slopes + fresh
        three_grads.append(jnp.concatenate([grad_query, grad_key, grad_value], axis=1))
        grad_normed = narrow_sum(
            times_back(grad_query, query_weight)
            + times_back(grad_key, key_weight)
            + times_back(grad_value, value_weight)
        )
        grad, gain_sum = norm_back(grad_normed, unit_attn[b], inv_attn[b], gain_attn)
        grad_one.append(grad_two[b] + grad)
        grad_gain_attn.append(gain_sum)
    output_grad = scatter_rows(inner_rows(both(branch_grads), both(context))).T
    qkv_grad = scatter_rows(inner_rows(both(gathered_attn), both(three_grads)))

    branch_grads, hidden_grads, last_normed = [], [], []
    for b in each:
        grad_branch = widen((0.5 * grad_one[b]).astype(BF))
        branch_grads.append(grad_branch)
        grad_hidden = (times_back(grad_branch, ffn1_down) * silu_slope(hidden_one[b])).astype(BF)
        hidden_grads.append(grad_hidden)
        last_normed.append(narrow_last(times_back(grad_hidden, ffn1_up)))
    ffn1_down_grad = scatter_rows(inner_rows(both(branch_grads), both(active_one))).T
    ffn1_up_grad = scatter_rows(inner_rows(both(gathered_one), both(hidden_grads)))
    frames_grad, grad_mask, grad_gain_one = [], [], []
    for b in each:
        hit = pick(masked_half[b].reshape(2, row_count), 0, high_bit)
        inputs = jnp.where(hit[:, None], mask_full[None, :], frames[b].astype(F32))
        unit_rows, inverse = norm_unit(inputs)
        grad, gain_sum = norm_back(last_normed[b], unit_rows, inverse, gain_one)
        grad = pick(grad_one[b].reshape(2, row_count, width), 0, high_bit) + grad
        frames_grad.append(jnp.where(hit[:, None], 0.0, grad))
        grad_mask.append(jnp.sum(jnp.where(hit[:, None], grad, 0.0), axis=0))
        grad_gain_one.append(gain_sum)

    gains = jnp.stack(
        [
            sum(grad_mask),
            sum(grad_gain_one),
            0.5 * sum(grad_gain_attn),
            0.5 * sum(grad_gain_conv),
            0.5 * sum(grad_gain_two),
            0.5 * sum(grad_final),
        ]
    )
    gains = sum_axis(sum_axis(gains, "tensor"), "dp")
    part = mask_vector.shape[0]
    place = lax.axis_index("dp") * lax.axis_size("tensor") + lax.axis_index("tensor")
    gains = lax.dynamic_slice_in_dim(gains, place * part, part, axis=1)

    head_count = rel_slope.shape[0]
    depth_slope = jnp.concatenate(
        [grad_depth, jnp.pad(grad_slopes[None], ((0, 0), (0, channels - head_count)))]
    )
    depth_slope = sum_axis(depth_slope, "dp")
    wide = query_weight.shape[1]

    return (
        jnp.stack(outputs),
        jnp.stack(frames_grad),
        gains[0],
        gains[1],
        ffn1_up_grad,
        ffn1_down_grad,
        gains[2],
        qkv_grad[:, :wide],
        qkv_grad[:, wide : 2 * wide],
        qkv_grad[:, 2 * wide :],
        output_grad,
        depth_slope[KW, :head_count],
        gains[3],
        conv_up_grad.reshape(conv_up.shape),
        depth_slope[:KW],
        sums_bn[0][1] + sums_bn[1][1],
        sums_bn[0][0] + sums_bn[1][0],
        conv_down_grad,
        gains[4],
        ffn2_up_grad,
        ffn2_down_grad,
        gains[5],
    )


def solution(mesh):
    every, split, columns = P(("dp", "tensor")), P("tensor"), P(None, "tensor")
    rows_by = P("dp", "tensor", None)
    return jax.shard_map(
        per_device,
        mesh=mesh,
        in_specs=(
            rows_by,
            P("dp"),
            P("dp", None),
            every,
            every,
            columns,
            P("tensor", None),
            every,
            columns,
            columns,
            columns,
            P("tensor", None),
            split,
            every,
            P("dp", None, "tensor"),
            columns,
            split,
            split,
            P("tensor", "dp"),
            every,
            columns,
            P("tensor", None),
            every,
            rows_by,
        ),
        out_specs=(
            rows_by,
            rows_by,
            every,
            every,
            P("dp", "tensor"),
            P("tensor", "dp"),
            every,
            P("dp", "tensor"),
            P("dp", "tensor"),
            P("dp", "tensor"),
            P("tensor", "dp"),
            split,
            every,
            P("dp", None, "tensor"),
            columns,
            split,
            split,
            P("tensor", "dp"),
            every,
            P("dp", "tensor"),
            P("tensor", "dp"),
            every,
        ),
        check_vma=False,
    )
```

time: 1400 us -> 642 us (0.46)
  waiting for transfers between devices: 853 us -> 151 us
  blocking collectives: 308 us -> 0 us
  other arithmetic: 80.2 us -> 202 us
  starting transfers between devices: 1.55 us -> 88.9 us
  local copies, waits for them, and re-layouts: 42.9 us -> 119 us
  matrix products: 88.3 us -> 61.3 us
    reduce_scatter x25 -> x0, waiting for transfers between devices: 852 us -> none  [the longest x8 115 us: narrow_sum(): lax.psum_scatter(partial_sum.astype(jnp.bfloat16), 'tensor', scatter_dime...]
    ppermute x0 -> x104, waiting for transfers between devices: none -> 151 us  [swap(): lax.ppermute(value, axis, [(place, place ^ bit) for place in range(size)])]
    all_gather x17 -> x0, blocking collectives: 143 us -> none  [the longest x8 58 us: widen_rows(): lax.all_gather(row_block.astype(jnp.bfloat16), 'tensor', axis=0, tiled=True)]
    ppermute x0 -> x104, starting transfers between devices: none -> 88.9 us  [swap(): lax.ppermute(value, axis, [(place, place ^ bit) for place in range(size)])]
    psum x4 -> x0, blocking collectives: 84.7 us -> none  [the longest x1 22.8 us: share_grads(): channel_out = lax.psum((depth_grad, slope_grad), 'dp')]
    unnamed x2 -> x0, blocking collectives: 80.2 us -> none
    convert_element_type x17 -> x66, other arithmetic: 22.6 us -> 66.6 us  [the longest x24 22.7 us: scatter_rows(): sent = pick(held, axis, jnp.logical_not(mine)).astype(BF)]
    add x10 -> x42, other arithmetic: 0.65 us -> 24.4 us  [the longest x20 20.1 us: scatter_rows(): held = pick(held, axis, mine) + swap(sent, 'dp', 1 << level).astype(F32)]
  transfers between devices with their start and end apart: 27 -> 104, of which waited for: 21 -> 38; matrix products, arithmetic and copies ran while one was open for 8% -> 52% of each run, Pallas kernels for 0% -> 0%
where the time goes in v1:
time: 642 us; the launch traced here: 630 us
  other arithmetic  202 us (31%)
  waiting for transfers between devices  151 us (24%)
  local copies, waits for them, and re-layouts  119 us (19%)
  starting transfers between devices  88.9 us (14%)
  matrix products  61.3 us (10%)
  between operations  7.75 us (1%)
    ppermute x104, waiting for transfers between devices, swap(): lax.ppermute(value, axis, [(place, place ^ bit) for place in range(size)])  151 us
    ppermute x104, starting transfers between devices, swap(): lax.ppermute(value, axis, [(place, place ^ bit) for place in range(size)])  88.9 us
    unnamed x725, local copies, waits for them, and re-layouts  54.4 us
    convert_element_type x24, other arithmetic, scatter_rows(): sent = pick(held, axis, jnp.logical_not(mine)).astype(BF)  22.7 us
    add x20, other arithmetic, scatter_rows(): held = pick(held, axis, mine) + swap(sent, 'dp', 1 << level).astype(F32)  20.1 us
    another operation x60, other arithmetic, ordered(): jnp.stack([jnp.where(second, theirs, mine), jnp.where(second, mine, their...  18.6 us
    dot_general x20, matrix products, product(): return jnp.dot(left, right, preferred_element_type=F32)  17.1 us
    convert_element_type x16, other arithmetic, narrow(): (pick(blocks, 1, low) + swap(sent, 'tensor', 1).astype(F32)).astype(BF)  14.6 us
  transfers between devices with their start and end apart: 104, of which 38 were waited for; matrix products, arithmetic and copies ran while one was open for 52% of the time, Pallas kernels for 0%

profile of v1, /device:TPU:0, one launch (start us, length us, event | category | flops | bytes accessed | tf_op | source)
XLA Modules:
  0.0 629.7 jit_solution(559708163586573190)
XLA Ops:
  2.3 3.0 collective-permute-start
  5.3 2.6 collective-permute-start.19
  20.4 2.7 collective-permute-start.2
  39.8 3.5 collective-permute-done.20
  64.5 5.8 collective-permute-done.8
  72.4 2.7 collective-permute-done.28
  103.5 2.7 fusion.347
  135.1 3.0 multiply_convert_fusion.25
  151.9 2.7 collective-permute-start.18
  157.5 2.3 collective-permute-done.35
  170.7 2.8 collective-permute-done.23
  187.5 2.5 multiply_convert_fusion.23
  205.9 5.0 collective-permute-done.40
  221.9 3.2 fusion.156
  234.8 3.4 multiply_convert_fusion.13
  248.6 3.4 fusion.59
  254.0 2.4 fusion.332
  258.3 2.9 copy.610
  261.2 3.0 fusion.20
  264.2 2.3 fusion.331
  266.5 3.0 copy.613
  269.5 3.3 copy.612
  278.0 2.9 fusion.21
  281.2 2.3 collective-permute-done.44
  283.5 5.1 collective-permute-done.59
  300.2 2.9 fusion.315
  341.0 2.5 multiply_reduce_fusion.39
  364.3 20.3 %collective-permute-done.96 = bf16[2,128,256]{1,2,0:T(8,128)(2,1)S(1)} collective-permute-done((bf16[2,128,256]{1,2,0:T(8,128)(2,1)S(1)}, bf16[2,128,256]{1,2,0:T(8,128)(2,1)S(1)}, u32[]{:S(2)}, u32[]{:S(2)}) %collective-permute-start.96) | collective-permute-done | bytes 131104 | tf_op jit(solution)/shard_map/ppermute | solution.py:52
  388.0 4.4 collective-permute-done.97
  394.7 4.0 collective-permute-done.65
  410.2 3.1 fusion.313
  428.5 2.7 multiply_reduce_fusion.11
  480.8 3.1 collective-permute-done.53
  483.9 2.5 multiply_reduce_fusion.9
  487.0 3.2 multiply_convert_fusion.5
  504.0 3.2 fusion.29
  509.2 2.3 fusion.334
  513.5 2.9 copy.598
  516.5 2.9 fusion.18
  521.6 3.0 copy.601
  524.6 3.1 copy.600
  531.7 2.8 fusion.19
  541.1 3.3 collective-permute-done.73
  546.2 21.6 %collective-permute-done.74 = f32[6,1024]{1,0:T(8,128)S(1)} collective-permute-done((f32[6,1024]{1,0:T(8,128)S(1)}, f32[6,1024]{1,0:T(8,128)S(1)}, u32[]{:S(2)}, u32[]{:S(2)}) %collective-permute-start.74) | collective-permute-done | bytes 24608 | tf_op jit(solution)/shard_map/ppermute | solution.py:52
  574.6 7.1 %collective-permute-done.76 = f32[6,1024]{1,0:T(8,128)S(1)} collective-permute-done((f32[6,1024]{1,0:T(8,128)S(1)}, f32[6,1024]{1,0:T(8,128)S(1)}, u32[]{:S(2)}, u32[]{:S(2)}) %collective-permute-start.76) | collective-permute-done | bytes 24608 | tf_op jit(solution)/shard_map/ppermute | solution.py:52
  588.1 11.1 %collective-permute-done.78 = bf16[2,128,1024]{1,2,0:T(8,128)(2,1)S(1)} collective-permute-done((bf16[2,128,1024]{1,2,0:T(8,128)(2,1)S(1)}, bf16[2,128,1024]{1,2,0:T(8,128)(2,1)S(1)}, u32[]{:S(2)}, u32[]{:S(2)}) %collective-permute-start.78) | collective-permute-done | bytes 524320 | tf_op jit(solution)/shard_map/ppermute | solution.py:52
  599.5 15.2 %collective-permute-done.81 = bf16[2,128,1024]{1,2,0:T(8,128)(2,1)S(1)} collective-permute-done((bf16[2,128,1024]{1,2,0:T(8,128)(2,1)S(1)}, bf16[2,128,1024]{1,2,0:T(8,128)(2,1)S(1)}, u32[]{:S(2)}, u32[]{:S(2)}) %collective-permute-start.81) | collective-permute-done | bytes 524320 | tf_op jit(solution)/shard_map/ppermute | solution.py:52
  619.4 9.0 %collective-permute-done.82 = bf16[128,1024]{0,1:T(8,128)(2,1)S(1)} collective-permute-done((bf16[128,1024]{0,1:T(8,128)(2,1)}, bf16[128,1024]{0,1:T(8,128)(2,1)S(1)}, u32[]{:S(2)}, u32[]{:S(2)}) %collective-permute-start.82) | collective-permute-done | bytes 262176 | tf_op jit(solution)/shard_map/ppermute | solution.py:52
  (1351 shorter events, 407.0 us)
Async XLA Ops:
  2.3 16.8 %collective-permute-start = (f32[6,32]{1,0:T(8,128)S(1)}, f32[6,32]{1,0:T(8,128)S(1)}, u32[]{:S(2)}, u32[]{:S(2)}) collective-permute-start(f32[6,32]{1,0:T(8,128)S(1)} %stack.402), channel_id=1, source_target_pairs={{0,2},{1,3},{2,0},{3,1},{4,6},{5,7},{6,4},{7,5},{8,10},{9,11},{10,... | collective-permute-start | bytes 2312 | tf_op jit(solution)/shard_map/ppermute | solution.py:52
  5.3 32.0 %collective-permute-start.19 = (bf16[256,128]{1,0:T(8,128)(2,1)}, bf16[256,128]{1,0:T(8,128)(2,1)S(1)}, u32[]{:S(2)}, u32[]{:S(2)}) collective-permute-start(bf16[256,128]{1,0:T(8,128)(2,1)} %param.42), channel_id=1, source_target_pairs={{0,16},{4,20},{8,24},{12,28},{16,0},{20,4},{24,8},{28,12},{1,17},{... | collective-permute-start | bytes 196616 | tf_op jit(solution)/shard_map/ppermute | solution.py:52
  8.8 30.2 %collective-permute-start.13 = (bf16[128,512]{1,0:T(8,128)(2,1)S(1)}, bf16[128,512]{1,0:T(8,128)(2,1)S(1)}, u32[]{:S(2)}, u32[]{:S(2)}) collective-permute-start(bf16[128,512]{1,0:T(8,128)(2,1)S(1)} %bitcast.1212), channel_id=1, source_target_pairs={{0,16},{4,20},{8,24},{12,28},{16,0},{20,4},{24,8},{28,12},{1,17},{... | collective-permute-start | bytes 393224 | tf_op jit(solution)/shard_map/ppermute | solution.py:52
  9.2 194.6 %collective-permute-start.41 = (bf16[2,64,1024]{2,1,0:T(8,128)(2,1)}, bf16[2,64,1024]{2,1,0:T(8,128)(2,1)}, u32[]{:S(2)}, u32[]{:S(2)}) collective-permute-start(bf16[2,64,1024]{2,1,0:T(8,128)(2,1)} %param.47), channel_id=1, source_target_pairs={{0,2},{1,3},{2,0},{3,1},{4,6},{5,7},{6,4},{7,5},{8,10},{9,11},{10,... | collective-permute-start | bytes 786440 | tf_op jit(solution)/shard_map/ppermute | solution.py:52
  9.5 30.1 %collective-permute-start.5 = (bf16[2,64,1024]{2,1,0:T(8,128)(2,1)}, bf16[2,64,1024]{2,1,0:T(8,128)(2,1)S(1)}, u32[]{:S(2)}, u32[]{:S(2)}) collective-permute-start(bf16[2,64,1024]{2,1,0:T(8,128)(2,1)} %param.24), channel_id=1, source_target_pairs={{0,2},{1,3},{2,0},{3,1},{4,6},{5,7},{6,4},{7,5},{8,10},{9,11},{10,... | collective-permute-start | bytes 786440 | tf_op jit(solution)/shard_map/ppermute | solution.py:52
  44.7 42.5 %collective-permute-start.21 = (bf16[2,2,256,128]{3,2,1,0:T(8,128)(2,1)}, bf16[2,2,256,128]{3,2,1,0:T(8,128)(2,1)}, u32[]{:S(2)}, u32[]{:S(2)}) collective-permute-start(bf16[2,2,256,128]{3,2,1,0:T(8,128)(2,1)} %pad_maximum_fusion.22), channel_id=1, source_target_pairs={{0,4},{4,0},{8,12},{12,8},{16,20},{20,16},{24,28},{28,24},{1,5},{5... | collective-permute-start | bytes 786440 | tf_op jit(solution)/shard_map/ppermute | solution.py:52
  62.9 12.2 %collective-permute-start.28 = (bf16[2,64,1024]{2,1,0:T(8,128)(2,1)S(1)}, bf16[2,64,1024]{2,1,0:T(8,128)(2,1)}, u32[]{:S(2)}, u32[]{:S(2)}) collective-permute-start(bf16[2,64,1024]{2,1,0:T(8,128)(2,1)S(1)} %fusion.165), channel_id=1, source_target_pairs={{0,2},{1,3},{2,0},{3,1},{4,6},{5,7},{6,4},{7,5},{8,10},{9,11},{10,... | collective-permute-start | bytes 786440 | tf_op jit(solution)/shard_map/ppermute | solution.py:52
  86.6 52.1 %collective-permute-start.15 = (bf16[2,2,128,512]{3,2,1,0:T(8,128)(2,1)}, bf16[2,2,128,512]{3,2,1,0:T(8,128)(2,1)}, u32[]{:S(2)}, u32[]{:S(2)}) collective-permute-start(bf16[2,2,128,512]{3,2,1,0:T(8,128)(2,1)} %pad_maximum_fusion.5), channel_id=1, source_target_pairs={{0,4},{4,0},{8,12},{12,8},{16,20},{20,16},{24,28},{28,24},{1,5},{5... | collective-permute-start | bytes 1572872 | tf_op jit(solution)/shard_map/ppermute | solution.py:52
  170.2 10.2 %collective-permute-start.37 = (bf16[2,64,1024]{2,1,0:T(8,128)(2,1)}, bf16[2,64,1024]{2,1,0:T(8,128)(2,1)}, u32[]{:S(2)}, u32[]{:S(2)}) collective-permute-start(bf16[2,64,1024]{2,1,0:T(8,128)(2,1)} %fusion.163), channel_id=1, source_target_pairs={{0,2},{1,3},{2,0},{3,1},{4,6},{5,7},{6,4},{7,5},{8,10},{9,11},{10,... | collective-permute-start | bytes 786440 | tf_op jit(solution)/shard_map/ppermute | solution.py:52
  205.7 11.5 %collective-permute-start.26 = (bf16[2,64,1024]{2,1,0:T(8,128)(2,1)S(1)}, bf16[2,64,1024]{2,1,0:T(8,128)(2,1)}, u32[]{:S(2)}, u32[]{:S(2)}) collective-permute-start(bf16[2,64,1024]{2,1,0:T(8,128)(2,1)S(1)} %fusion.168), channel_id=1, source_target_pairs={{0,2},{1,3},{2,0},{3,1},{4,6},{5,7},{6,4},{7,5},{8,10},{9,11},{10,... | collective-permute-start | bytes 786440 | tf_op jit(solution)/shard_map/ppermute | solution.py:52
  252.7 20.0 %collective-permute-start.43 = (bf16[2,64,1024]{2,1,0:T(8,128)(2,1)}, bf16[2,64,1024]{2,1,0:T(8,128)(2,1)}, u32[]{:S(2)}, u32[]{:S(2)}) collective-permute-start(bf16[2,64,1024]{2,1,0:T(8,128)(2,1)} %fusion.184), channel_id=1, source_target_pairs={{0,1},{1,0},{2,3},{3,2},{4,5},{5,4},{6,7},{7,6},{8,9},{9,8},{10,11... | collective-permute-start | bytes 786440 | tf_op jit(solution)/shard_map/ppermute | solution.py:52
  253.6 22.8 %collective-permute-start.58 = (bf16[2,64,1024]{2,1,0:T(8,128)(2,1)}, bf16[2,64,1024]{2,1,0:T(8,128)(2,1)}, u32[]{:S(2)}, u32[]{:S(2)}) collective-permute-start(bf16[2,64,1024]{2,1,0:T(8,128)(2,1)} %fusion.188), channel_id=1, source_target_pairs={{0,1},{1,0},{2,3},{3,2},{4,5},{5,4},{6,7},{7,6},{8,9},{9,8},{10,11... | collective-permute-start | bytes 786440 | tf_op jit(solution)/shard_map/ppermute | solution.py:52
  264.2 89.4 %collective-permute-start.98 = (bf16[2,2,128,1024]{2,3,0,1:T(8,128)(2,1)}, bf16[2,2,128,1024]{2,3,0,1:T(8,128)(2,1)}, u32[]{:S(2)}, u32[]{:S(2)}) collective-permute-start(bf16[2,2,128,1024]{2,3,0,1:T(8,128)(2,1)} %fusion.20), channel_id=1, source_target_pairs={{0,4},{4,0},{8,12},{12,8},{16,20},{20,16},{24,28},{28,24},{1,5},{5... | collective-permute-start | bytes 3145736 | tf_op jit(solution)/shard_map/ppermute | solution.py:52
  277.9 10.8 %collective-permute-start.59 = (bf16[2,64,1024]{2,1,0:T(8,128)(2,1)S(1)}, bf16[2,64,1024]{2,1,0:T(8,128)(2,1)S(1)}, u32[]{:S(2)}, u32[]{:S(2)}) collective-permute-start(bf16[2,64,1024]{2,1,0:T(8,128)(2,1)S(1)} %fusion.127), channel_id=1, source_target_pairs={{0,2},{1,3},{2,0},{3,1},{4,6},{5,7},{6,4},{7,5},{8,10},{9,11},{10,... | collective-permute-start | bytes 786440 | tf_op jit(solution)/shard_map/ppermute | solution.py:52
  280.9 75.7 %collective-permute-start.101 = (bf16[2,2,128,1024]{2,3,0,1:T(8,128)(2,1)}, bf16[2,2,128,1024]{2,3,0,1:T(8,128)(2,1)}, u32[]{:S(2)}, u32[]{:S(2)}) collective-permute-start(bf16[2,2,128,1024]{2,3,0,1:T(8,128)(2,1)} %fusion.21), channel_id=1, source_target_pairs={{0,4},{4,0},{8,12},{12,8},{16,20},{20,16},{24,28},{28,24},{1,5},{5... | collective-permute-start | bytes 3145736 | tf_op jit(solution)/shard_map/ppermute | solution.py:52
  314.3 12.1 %collective-permute-start.61 = (f32[2,256]{1,0:T(2,128)}, f32[2,256]{1,0:T(2,128)}, u32[]{:S(2)}, u32[]{:S(2)}) collective-permute-start(f32[2,256]{1,0:T(2,128)} %pad_maximum_fusion.39), channel_id=1, source_target_pairs={{0,4},{4,0},{8,12},{12,8},{16,20},{20,16},{24,28},{28,24},{1,5},{5... | collective-permute-start | bytes 6152 | tf_op jit(solution)/shard_map/ppermute | solution.py:52
  324.6 35.5 %collective-permute-start.95 = (bf16[2,2,128,256]{2,3,0,1:T(8,128)(2,1)}, bf16[2,2,128,256]{2,3,0,1:T(8,128)(2,1)}, u32[]{:S(2)}, u32[]{:S(2)}) collective-permute-start(bf16[2,2,128,256]{2,3,0,1:T(8,128)(2,1)} %fusion.196), channel_id=1, source_target_pairs={{0,4},{4,0},{8,12},{12,8},{16,20},{20,16},{24,28},{28,24},{1,5},{5... | collective-permute-start | bytes 786440 | tf_op jit(solution)/shard_map/ppermute | solution.py:52
  347.1 15.2 %collective-permute-start.49 = (bf16[2,64,1024]{2,1,0:T(8,128)(2,1)}, bf16[2,64,1024]{2,1,0:T(8,128)(2,1)}, u32[]{:S(2)}, u32[]{:S(2)}) collective-permute-start(bf16[2,64,1024]{2,1,0:T(8,128)(2,1)} %fusion.185), channel_id=1, source_target_pairs={{0,1},{1,0},{2,3},{3,2},{4,5},{5,4},{6,7},{7,6},{8,9},{9,8},{10,11... | collective-permute-start | bytes 786440 | tf_op jit(solution)/shard_map/ppermute | solution.py:52
  348.8 37.7 %collective-permute-start.64 = (bf16[2,64,1024]{2,1,0:T(8,128)(2,1)S(1)}, bf16[2,64,1024]{2,1,0:T(8,128)(2,1)S(1)}, u32[]{:S(2)}, u32[]{:S(2)}) collective-permute-start(bf16[2,64,1024]{2,1,0:T(8,128)(2,1)S(1)} %fusion.189), channel_id=1, source_target_pairs={{0,1},{1,0},{2,3},{3,2},{4,5},{5,4},{6,7},{7,6},{8,9},{9,8},{10,11... | collective-permute-start | bytes 786440 | tf_op jit(solution)/shard_map/ppermute | solution.py:52
  353.6 39.8 %collective-permute-start.92 = (bf16[2,2,128,512]{3,2,1,0:T(8,128)(2,1)S(1)}, bf16[2,2,128,512]{3,2,1,0:T(8,128)(2,1)S(1)}, u32[]{:S(2)}, u32[]{:S(2)}) collective-permute-start(bf16[2,2,128,512]{3,2,1,0:T(8,128)(2,1)S(1)} %fusion.90), channel_id=1, source_target_pairs={{0,4},{4,0},{8,12},{12,8},{16,20},{20,16},{24,28},{28,24},{1,5},{5... | collective-permute-start | bytes 1572872 | tf_op jit(solution)/shard_map/ppermute | solution.py:52
  356.7 57.7 %collective-permute-start.99 = (bf16[2,128,1024]{1,2,0:T(8,128)(2,1)}, bf16[2,128,1024]{1,2,0:T(8,128)(2,1)}, u32[]{:S(2)}, u32[]{:S(2)}) collective-permute-start(bf16[2,128,1024]{1,2,0:T(8,128)(2,1)} %fusion.91), channel_id=1, source_target_pairs={{0,8},{4,12},{8,0},{12,4},{16,24},{20,28},{24,16},{28,20},{1,9},{5... | collective-permute-start | bytes 1572872 | tf_op jit(solution)/shard_map/ppermute | solution.py:52
  360.1 57.3 %collective-permute-start.102 = (bf16[2,128,1024]{1,2,0:T(8,128)(2,1)}, bf16[2,128,1024]{1,2,0:T(8,128)(2,1)}, u32[]{:S(2)}, u32[]{:S(2)}) collective-permute-start(bf16[2,128,1024]{1,2,0:T(8,128)(2,1)} %fusion.92), channel_id=1, source_target_pairs={{0,8},{4,12},{8,0},{12,4},{16,24},{20,28},{24,16},{28,20},{1,9},{5... | collective-permute-start | bytes 1572872 | tf_op jit(solution)/shard_map/ppermute | solution.py:52
  362.3 22.4 %collective-permute-start.96 = (bf16[2,128,256]{1,2,0:T(8,128)(2,1)S(1)}, bf16[2,128,256]{1,2,0:T(8,128)(2,1)S(1)}, u32[]{:S(2)}, u32[]{:S(2)}) collective-permute-start(bf16[2,128,256]{1,2,0:T(8,128)(2,1)S(1)} %fusion.254), channel_id=1, source_target_pairs={{0,8},{4,12},{8,0},{12,4},{16,24},{20,28},{24,16},{28,20},{1,9},{5... | collective-permute-start | bytes 393224 | tf_op jit(solution)/shard_map/ppermute | solution.py:52
  384.6 10.1 %collective-permute-start.50 = (bf16[2,64,1024]{2,1,0:T(8,128)(2,1)S(1)}, bf16[2,64,1024]{2,1,0:T(8,128)(2,1)S(1)}, u32[]{:S(2)}, u32[]{:S(2)}) collective-permute-start(bf16[2,64,1024]{2,1,0:T(8,128)(2,1)S(1)} %fusion.146), channel_id=1, source_target_pairs={{0,2},{1,3},{2,0},{3,1},{4,6},{5,7},{6,4},{7,5},{8,10},{9,11},{10,... | collective-permute-start | bytes 786440 | tf_op jit(solution)/shard_map/ppermute | solution.py:52
  394.4 27.2 %collective-permute-start.93 = (bf16[2,128,512]{2,1,0:T(8,128)(2,1)}, bf16[2,128,512]{2,1,0:T(8,128)(2,1)}, u32[]{:S(2)}, u32[]{:S(2)}) collective-permute-start(bf16[2,128,512]{2,1,0:T(8,128)(2,1)} %fusion.195), channel_id=1, source_target_pairs={{0,8},{4,12},{8,0},{12,4},{16,24},{20,28},{24,16},{28,20},{1,9},{5... | collective-permute-start | bytes 786440 | tf_op jit(solution)/shard_map/ppermute | solution.py:52
  413.3 10.9 %collective-permute-start.66 = (bf16[128,1024]{1,0:T(8,128)(2,1)S(1)}, bf16[128,1024]{1,0:T(8,128)(2,1)S(1)}, u32[]{:S(2)}, u32[]{:S(2)}) collective-permute-start(bf16[128,1024]{1,0:T(8,128)(2,1)S(1)} %get-tuple-element.221), channel_id=1, source_target_pairs={{0,1},{1,0},{2,3},{3,2},{4,5},{5,4},{6,7},{7,6},{8,9},{9,8},{10,11... | collective-permute-start | bytes 786440 | tf_op jit(solution)/shard_map/ppermute | solution.py:52
  413.3 18.0 %collective-permute-start.51 = (bf16[128,1024]{1,0:T(8,128)(2,1)}, bf16[128,1024]{1,0:T(8,128)(2,1)}, u32[]{:S(2)}, u32[]{:S(2)}) collective-permute-start(bf16[128,1024]{1,0:T(8,128)(2,1)} %get-tuple-element.389), channel_id=1, source_target_pairs={{0,1},{1,0},{2,3},{3,2},{4,5},{5,4},{6,7},{7,6},{8,9},{9,8},{10,11... | collective-permute-start | bytes 786440 | tf_op jit(solution)/shard_map/ppermute | solution.py:52
  416.6 44.8 %collective-permute-start.100 = (bf16[128,1024]{0,1:T(8,128)(2,1)}, bf16[128,1024]{0,1:T(8,128)(2,1)}, u32[]{:S(2)}, u32[]{:S(2)}) collective-permute-start(bf16[128,1024]{0,1:T(8,128)(2,1)} %fusion.197), channel_id=1, source_target_pairs={{0,16},{4,20},{8,24},{12,28},{16,0},{20,4},{24,8},{28,12},{1,17},{... | collective-permute-start | bytes 786440 | tf_op jit(solution)/shard_map/ppermute | solution.py:52
  419.4 54.7 %collective-permute-start.103 = (bf16[128,1024]{0,1:T(8,128)(2,1)}, bf16[128,1024]{0,1:T(8,128)(2,1)}, u32[]{:S(2)}, u32[]{:S(2)}) collective-permute-start(bf16[128,1024]{0,1:T(8,128)(2,1)} %fusion.198), channel_id=1, source_target_pairs={{0,16},{4,20},{8,24},{12,28},{16,0},{20,4},{24,8},{28,12},{1,17},{... | collective-permute-start | bytes 786440 | tf_op jit(solution)/shard_map/ppermute | solution.py:52
  423.4 35.7 %collective-permute-start.94 = (bf16[128,512]{1,0:T(8,128)(2,1)}, bf16[128,512]{1,0:T(8,128)(2,1)}, u32[]{:S(2)}, u32[]{:S(2)}) collective-permute-start(bf16[128,512]{1,0:T(8,128)(2,1)} %fusion.253), channel_id=1, source_target_pairs={{0,16},{4,20},{8,24},{12,28},{16,0},{20,4},{24,8},{28,12},{1,17},{... | collective-permute-start | bytes 393224 | tf_op jit(solution)/shard_map/ppermute | solution.py:52
  443.6 21.7 %collective-permute-start.86 = (bf16[2,2,128,256]{2,3,0,1:T(8,128)(2,1)}, bf16[2,2,128,256]{2,3,0,1:T(8,128)(2,1)}, u32[]{:S(2)}, u32[]{:S(2)}) collective-permute-start(bf16[2,2,128,256]{2,3,0,1:T(8,128)(2,1)} %fusion.194), channel_id=1, source_target_pairs={{0,4},{4,0},{8,12},{12,8},{16,20},{20,16},{24,28},{28,24},{1,5},{5... | collective-permute-start | bytes 786440 | tf_op jit(solution)/shard_map/ppermute | solution.py:52
  458.6 10.0 %collective-permute-start.67 = (bf16[2,64,1024]{2,1,0:T(8,128)(2,1)S(1)}, bf16[2,64,1024]{2,1,0:T(8,128)(2,1)}, u32[]{:S(2)}, u32[]{:S(2)}) collective-permute-start(bf16[2,64,1024]{2,1,0:T(8,128)(2,1)S(1)} %fusion.190), channel_id=1, source_target_pairs={{0,1},{1,0},{2,3},{3,2},{4,5},{5,4},{6,7},{7,6},{8,9},{9,8},{10,11... | collective-permute-start | bytes 786440 | tf_op jit(solution)/shard_map/ppermute | solution.py:52
  459.1 11.7 %collective-permute-start.52 = (bf16[2,64,1024]{2,1,0:T(8,128)(2,1)}, bf16[2,64,1024]{2,1,0:T(8,128)(2,1)}, u32[]{:S(2)}, u32[]{:S(2)}) collective-permute-start(bf16[2,64,1024]{2,1,0:T(8,128)(2,1)} %fusion.186), channel_id=1, source_target_pairs={{0,1},{1,0},{2,3},{3,2},{4,5},{5,4},{6,7},{7,6},{8,9},{9,8},{10,11... | collective-permute-start | bytes 786440 | tf_op jit(solution)/shard_map/ppermute | solution.py:52
  461.4 29.9 %collective-permute-start.83 = (bf16[2,2,128,768]{3,2,0,1:T(8,128)(2,1)}, bf16[2,2,128,768]{3,2,0,1:T(8,128)(2,1)}, u32[]{:S(2)}, u32[]{:S(2)}) collective-permute-start(bf16[2,2,128,768]{3,2,0,1:T(8,128)(2,1)} %fusion.76), channel_id=1, source_target_pairs={{0,4},{4,0},{8,12},{12,8},{16,20},{20,16},{24,28},{28,24},{1,5},{5... | collective-permute-start | bytes 2359304 | tf_op jit(solution)/shard_map/ppermute | solution.py:52
  470.3 10.5 %collective-permute-start.68 = (bf16[2,64,1024]{2,1,0:T(8,128)(2,1)}, bf16[2,64,1024]{2,1,0:T(8,128)(2,1)}, u32[]{:S(2)}, u32[]{:S(2)}) collective-permute-start(bf16[2,64,1024]{2,1,0:T(8,128)(2,1)} %fusion.117), channel_id=1, source_target_pairs={{0,2},{1,3},{2,0},{3,1},{4,6},{5,7},{6,4},{7,5},{8,10},{9,11},{10,... | collective-permute-start | bytes 786440 | tf_op jit(solution)/shard_map/ppermute | solution.py:52
  471.9 12.1 %collective-permute-start.53 = (bf16[2,64,1024]{2,1,0:T(8,128)(2,1)S(1)}, bf16[2,64,1024]{2,1,0:T(8,128)(2,1)}, u32[]{:S(2)}, u32[]{:S(2)}) collective-permute-start(bf16[2,64,1024]{2,1,0:T(8,128)(2,1)S(1)} %fusion.141), channel_id=1, source_target_pairs={{0,2},{1,3},{2,0},{3,1},{4,6},{5,7},{6,4},{7,5},{8,10},{9,11},{10,... | collective-permute-start | bytes 786440 | tf_op jit(solution)/shard_map/ppermute | solution.py:52
  493.8 45.0 %collective-permute-start.84 = (bf16[2,128,768]{2,1,0:T(8,128)(2,1)}, bf16[2,128,768]{2,1,0:T(8,128)(2,1)}, u32[]{:S(2)}, u32[]{:S(2)}) collective-permute-start(bf16[2,128,768]{2,1,0:T(8,128)(2,1)} %fusion.175), channel_id=1, source_target_pairs={{0,8},{4,12},{8,0},{12,4},{16,24},{20,28},{24,16},{28,20},{1,9},{5... | collective-permute-start | bytes 1179656 | tf_op jit(solution)/shard_map/ppermute | solution.py:52
  508.0 19.8 %collective-permute-start.55 = (bf16[2,64,1024]{2,1,0:T(8,128)(2,1)}, bf16[2,64,1024]{2,1,0:T(8,128)(2,1)}, u32[]{:S(2)}, u32[]{:S(2)}) collective-permute-start(bf16[2,64,1024]{2,1,0:T(8,128)(2,1)} %fusion.187), channel_id=1, source_target_pairs={{0,1},{1,0},{2,3},{3,2},{4,5},{5,4},{6,7},{7,6},{8,9},{9,8},{10,11... | collective-permute-start | bytes 786440 | tf_op jit(solution)/shard_map/ppermute | solution.py:52
  508.7 21.2 %collective-permute-start.70 = (bf16[2,64,1024]{2,1,0:T(8,128)(2,1)}, bf16[2,64,1024]{2,1,0:T(8,128)(2,1)S(1)}, u32[]{:S(2)}, u32[]{:S(2)}) collective-permute-start(bf16[2,64,1024]{2,1,0:T(8,128)(2,1)} %fusion.191), channel_id=1, source_target_pairs={{0,1},{1,0},{2,3},{3,2},{4,5},{5,4},{6,7},{7,6},{8,9},{9,8},{10,11... | collective-permute-start | bytes 786440 | tf_op jit(solution)/shard_map/ppermute | solution.py:52
  519.4 63.1 %collective-permute-start.77 = (bf16[2,2,128,1024]{2,3,0,1:T(8,128)(2,1)}, bf16[2,2,128,1024]{2,3,0,1:T(8,128)(2,1)}, u32[]{:S(2)}, u32[]{:S(2)}) collective-permute-start(bf16[2,2,128,1024]{2,3,0,1:T(8,128)(2,1)} %fusion.18), channel_id=1, source_target_pairs={{0,4},{4,0},{8,12},{12,8},{16,20},{20,16},{24,28},{28,24},{1,5},{5... | collective-permute-start | bytes 3145736 | tf_op jit(solution)/shard_map/ppermute | solution.py:52
  534.5 49.8 %collective-permute-start.80 = (bf16[2,2,128,1024]{2,3,0,1:T(8,128)(2,1)}, bf16[2,2,128,1024]{2,3,0,1:T(8,128)(2,1)}, u32[]{:S(2)}, u32[]{:S(2)}) collective-permute-start(bf16[2,2,128,1024]{2,3,0,1:T(8,128)(2,1)} %fusion.19), channel_id=1, source_target_pairs={{0,4},{4,0},{8,12},{12,8},{16,20},{20,16},{24,28},{28,24},{1,5},{5... | collective-permute-start | bytes 3145736 | tf_op jit(solution)/shard_map/ppermute | solution.py:52
  544.4 23.4 %collective-permute-start.74 = (f32[6,1024]{1,0:T(8,128)S(1)}, f32[6,1024]{1,0:T(8,128)S(1)}, u32[]{:S(2)}, u32[]{:S(2)}) collective-permute-start(f32[6,1024]{1,0:T(8,128)S(1)} %add.1226), channel_id=1, source_target_pairs={{0,4},{4,0},{8,12},{12,8},{16,20},{20,16},{24,28},{28,24},{1,5},{5... | collective-permute-start | bytes 73736 | tf_op jit(solution)/shard_map/ppermute | solution.py:52
  569.6 12.8 %collective-permute-start.85 = (bf16[128,768]{1,0:T(8,128)(2,1)S(1)}, bf16[128,768]{1,0:T(8,128)(2,1)S(1)}, u32[]{:S(2)}, u32[]{:S(2)}) collective-permute-start(bf16[128,768]{1,0:T(8,128)(2,1)S(1)} %fusion.251), channel_id=1, source_target_pairs={{0,16},{4,20},{8,24},{12,28},{16,0},{20,4},{24,8},{28,12},{1,17},{... | collective-permute-start | bytes 589832 | tf_op jit(solution)/shard_map/ppermute | solution.py:52
  571.8 10.0 %collective-permute-start.76 = (f32[6,1024]{1,0:T(8,128)S(1)}, f32[6,1024]{1,0:T(8,128)S(1)}, u32[]{:S(2)}, u32[]{:S(2)}) collective-permute-start(f32[6,1024]{1,0:T(8,128)S(1)} %add.1228), channel_id=1, source_target_pairs={{0,16},{4,20},{8,24},{12,28},{16,0},{20,4},{24,8},{28,12},{1,17},{... | collective-permute-start | bytes 73736 | tf_op jit(solution)/shard_map/ppermute | solution.py:52
  584.3 14.9 %collective-permute-start.78 = (bf16[2,128,1024]{1,2,0:T(8,128)(2,1)S(1)}, bf16[2,128,1024]{1,2,0:T(8,128)(2,1)S(1)}, u32[]{:S(2)}, u32[]{:S(2)}) collective-permute-start(bf16[2,128,1024]{1,2,0:T(8,128)(2,1)S(1)} %fusion.88), channel_id=1, source_target_pairs={{0,8},{4,12},{8,0},{12,4},{16,24},{20,28},{24,16},{28,20},{1,9},{5... | collective-permute-start | bytes 1572872 | tf_op jit(solution)/shard_map/ppermute | solution.py:52
  586.6 28.1 %collective-permute-start.81 = (bf16[2,128,1024]{1,2,0:T(8,128)(2,1)S(1)}, bf16[2,128,1024]{1,2,0:T(8,128)(2,1)S(1)}, u32[]{:S(2)}, u32[]{:S(2)}) collective-permute-start(bf16[2,128,1024]{1,2,0:T(8,128)(2,1)S(1)} %fusion.89), channel_id=1, source_target_pairs={{0,8},{4,12},{8,0},{12,4},{16,24},{20,28},{24,16},{28,20},{1,9},{5... | collective-permute-start | bytes 1572872 | tf_op jit(solution)/shard_map/ppermute | solution.py:52
  599.4 17.1 %collective-permute-start.79 = (bf16[128,1024]{0,1:T(8,128)(2,1)S(1)}, bf16[128,1024]{0,1:T(8,128)(2,1)S(1)}, u32[]{:S(2)}, u32[]{:S(2)}) collective-permute-start(bf16[128,1024]{0,1:T(8,128)(2,1)S(1)} %fusion.192), channel_id=1, source_target_pairs={{0,16},{4,20},{8,24},{12,28},{16,0},{20,4},{24,8},{28,12},{1,17},{... | collective-permute-start | bytes 786440 | tf_op jit(solution)/shard_map/ppermute | solution.py:52
  615.7 12.7 %collective-permute-start.82 = (bf16[128,1024]{0,1:T(8,128)(2,1)}, bf16[128,1024]{0,1:T(8,128)(2,1)S(1)}, u32[]{:S(2)}, u32[]{:S(2)}) collective-permute-start(bf16[128,1024]{0,1:T(8,128)(2,1)} %fusion.193), channel_id=1, source_target_pairs={{0,16},{4,20},{8,24},{12,28},{16,0},{20,4},{24,8},{28,12},{1,17},{... | collective-permute-start | bytes 786440 | tf_op jit(solution)/shard_map/ppermute | solution.py:52
  (411 other events, 2535.4 us)

commit v2 on v1

v2 whole, which is shorter than its diff:
```python
import functools

import jax
import jax.numpy as jnp
from jax import lax
from jax.experimental import pallas as pl
from jax.experimental.pallas import tpu as pltpu
from jax.sharding import PartitionSpec as P

DH = 128
KW = 5
SPAN = 10
REACH = 128
EPSILON = 1e-05
MASKED_SCORE = -1000000000.0
BF = jnp.bfloat16
F32 = jnp.float32
STEP = 32
TILE = 256
EDGE = 8
MIB = 1024 * 1024
COST = 30_000_000

VMEM_SPEC = pl.BlockSpec(memory_space=pltpu.VMEM)
SMEM_SPEC = pl.BlockSpec(memory_space=pltpu.SMEM)


def product(left, right):
    return jnp.dot(left, right, preferred_element_type=F32)


def inner_rows(left, right):
    return lax.dot_general(left, right, (((0,), (0,)), ((), ())), preferred_element_type=F32)


def times_back(left, right):
    return lax.dot_general(left, right, (((1,), (1,)), ((), ())), preferred_element_type=F32)


def sigmoid(values):
    return 0.5 * jnp.tanh(0.5 * values) + 0.5


def norm_unit(values):
    centre = jnp.mean(values, axis=-1, keepdims=True)
    centred = values - centre
    inverse = lax.rsqrt(jnp.mean(centred * centred, axis=-1, keepdims=True) + EPSILON)
    return centred * inverse, inverse


def norm_back(grad_out, unit_rows, inverse, norm_gain):
    grad_unit = grad_out * norm_gain
    first_mean = jnp.mean(grad_unit, axis=-1, keepdims=True)
    second_mean = jnp.mean(grad_unit * unit_rows, axis=-1, keepdims=True)
    return (
        inverse * (grad_unit - first_mean - unit_rows * second_mean),
        jnp.sum(grad_out * unit_rows, axis=0, keepdims=True),
    )


def silu_slope(values):
    gate_value = sigmoid(values)
    return gate_value * (1.0 + values * (1.0 - gate_value))


def over_rows(count, body, init=0, step=STEP):
    def one(index, carry):
        return body(pl.ds(pl.multiple_of(index * step, step), step), index * step, carry)

    return lax.fori_loop(0, count // step, one, init)


def row_iota(first, rows, columns):
    return first + lax.broadcasted_iota(jnp.int32, (rows, columns), 0)


def mask_col(starts_ref, first, rows, length):
    starts = starts_ref[...]
    at = row_iota(first, rows, starts.shape[1])
    hit = (starts <= at) & (at < starts + SPAN) & (at < length)
    return jnp.max(jnp.where(hit, 1.0, 0.0), axis=1, keepdims=True)


def valid_col(first, rows, columns, length):
    return jnp.where(row_iota(first, rows, columns) < length, 1.0, 0.0)


def masked_rows(frame_rows, mask, mask_row):
    return jnp.where(
        jnp.broadcast_to(mask, frame_rows.shape) > 0.5, mask_row, frame_rows.astype(F32)
    )


def pair_sum(mine, theirs, rows):
    return mine[rows, :].astype(F32) + theirs[rows, :].astype(F32)


class Late:
    def __init__(self, source, held, semaphore):
        self.copy = pltpu.make_async_copy(source, held, semaphore)
        self.copy.start()
        self.held, self.shape, self.dtype, self.waited = held, held.shape, held.dtype, False

    def arrive(self):
        if not self.waited:
            self.copy.wait()
            self.waited = True

    def __getitem__(self, index):
        assert self.waited
        return self.held[index]


class Leaving:
    def __init__(self, target, held, semaphore):
        self.copy = pltpu.make_async_copy(held, target, semaphore)
        self.held, self.shape, self.dtype, self.started = held, held.shape, held.dtype, False

    def leave(self):
        if not self.started:
            self.copy.start()
            self.started = True

    def finish(self):
        self.leave()
        self.copy.wait()

    def __getitem__(self, index):
        return self.held[index]

    def __setitem__(self, index, value):
        assert not self.started
        self.held[index] = value


def arrive(*refs):
    for ref in refs:
        if isinstance(ref, Late):
            ref.arrive()


def leave(*refs):
    for ref in refs:
        if isinstance(ref, Leaving):
            ref.leave()


def columns(index, size=TILE):
    return slice(index * size, (index + 1) * size)


def ffn_up(branch, ups, hidden, active_own, active_cross):
    normed = branch[...]
    for shard, weight in enumerate(ups):
        arrive(weight)
        tiles = weight.shape[1] // TILE
        for index in range(tiles):
            at = columns(index)
            values = product(normed, weight[:, at])
            hidden[:, columns(index + shard * tiles)] = values
            (active_own, active_cross)[shard][:, at] = (values * sigmoid(values)).astype(BF)


def ffn_down(active_own, active_cross, downs, part):
    width = downs[0].shape[1]
    own, cross = active_own[...], active_cross[...]
    arrive(*downs)
    for index in range(width // TILE):
        at = columns(index)
        part[:, at] = (product(own, downs[0][:, at]) + product(cross, downs[1][:, at])).astype(BF)


def ffn_grad_hidden(branch, downs, hidden, grad_own, grad_cross):
    grad_branch = branch[...]
    for shard, weight in enumerate(downs):
        arrive(weight)
        tiles = weight.shape[0] // TILE
        for index in range(tiles):
            at = columns(index)
            slope = silu_slope(hidden[:, columns(index + shard * tiles)])
            grad = (times_back(grad_branch, weight[at, :]) * slope).astype(BF)
            (grad_own, grad_cross)[shard][:, at] = grad


def ffn_grad_input(grad_own, grad_cross, ups, store):
    own, cross = grad_own[...], grad_cross[...]
    arrive(*ups)
    for index in range(ups[0].shape[0] // TILE):
        at = columns(index)
        store(at, times_back(own, ups[0][at, :]) + times_back(cross, ups[1][at, :]))


def k_pick(info, block, across_block, sent):
    core = info[0]
    sent[0] = block[pl.ds(1 - core, 1)][0]
    sent[1] = across_block[pl.ds(1 - core, 1)][0]


def place_rows(info, block, across_block, arrived, whole):
    core, high = info[0], info[1]
    rows = block.shape[1]
    places = (
        (2 * high + core, block[pl.ds(core, 1)][0]),
        (2 * (1 - high) + core, across_block[pl.ds(core, 1)][0]),
        (2 * high + 1 - core, arrived[0]),
        (2 * (1 - high) + 1 - core, arrived[1]),
    )
    for place, value in places:
        whole[pl.ds(pl.multiple_of(place * rows, rows), rows), :] = value


def k_ffn_one(
    info, starts, block, across_block, arrived, small, up_o, up_t, down_o, down_t,
    frames, branch, active_cross, active_own, hidden, part, whole,
):
    length = info[2]
    rows, width = whole.shape
    place_rows(info, block, across_block, arrived, whole)
    frames[...] = whole[...]

    def normalise(at, first, carry):
        mask = mask_col(starts, first, STEP, length)
        unit_rows, _ = norm_unit(masked_rows(whole[at, :], mask, small[0:1, :]))
        branch[at, :] = (unit_rows * small[1:2, :]).astype(BF)
        return carry

    over_rows(rows, normalise)
    ffn_up(branch, (up_o, up_t), hidden, active_own, active_cross)
    ffn_down(active_own, active_cross, (down_o, down_t), part)


def k_attn(
    info, starts, slopes, mine, theirs, frames, small, qkv_o, qkv_t, out_o, out_t,
    stream, branch, context_cross, context_own, qkv, weights, part,
):
    length = info[2]
    rows, width = frames.shape
    arrive(frames)

    def normalise(at, first, carry):
        mask = mask_col(starts, first, STEP, length)
        inputs = masked_rows(frames[at, :], mask, small[0:1, :])
        values = inputs + 0.5 * pair_sum(mine, theirs, at)
        stream[at, :] = values
        unit_rows, _ = norm_unit(values)
        branch[at, :] = (unit_rows * small[2:3, :]).astype(BF)
        return carry

    over_rows(rows, normalise)
    normed = branch[...]
    third = qkv_o.shape[1] // 3
    for shard, weight in enumerate((qkv_o, qkv_t)):
        arrive(weight)
        for index in range(3):
            at = columns(index, third)
            qkv[:, columns(3 * shard + index, third)] = product(normed, weight[:, at]).astype(BF)
    heads = third // DH
    span = rows // 2
    for shard in range(2):
        base = 3 * third * shard
        for head in range(heads):
            place = shard * heads + head
            key = qkv[:, base + third + head * DH : base + third + (head + 1) * DH]
            value = qkv[:, base + 2 * third + head * DH : base + 2 * third + (head + 1) * DH]
            for part_index in range(2):
                at = columns(part_index, span)
                query = qkv[at, base + head * DH : base + (head + 1) * DH]
                scores = times_back(query, key) * DH ** (-0.5)
                key_place = lax.broadcasted_iota(jnp.int32, (span, rows), 1)
                away = key_place - row_iota(part_index * span, span, rows)
                relative = jnp.clip(away, -REACH, REACH).astype(F32) * (1.0 / REACH)
                scores = scores + slopes[place] * relative
                scores = jnp.where(key_place < length, scores, MASKED_SCORE)
                raised = jnp.exp(scores - jnp.max(scores, axis=-1, keepdims=True))
                soft = raised * (1.0 / jnp.sum(raised, axis=-1, keepdims=True))
                weights[place, at, :] = soft
                context = product(soft.astype(BF), value).astype(BF)
                if shard == 0:
                    context_own[at, columns(head, DH)] = context
                else:
                    context_cross[at, columns(head, DH)] = context
    arrive(out_o, out_t)
    own = context_own[...]
    other = context_cross[...]
    for index in range(width // TILE):
        at = columns(index)
        part[:, at] = (product(own, out_o[:, at]) + product(other, out_t[:, at])).astype(BF)


def k_conv_front(
    info, mine, theirs, stream_in, small, params, conv_o, conv_t,
    stream, normed, value, gate, padded, convolved, stats,
):
    length = info[2]
    rows, width = stream_in.shape
    channels = params.shape[1] // 2
    arrive(stream_in)

    def normalise(at, first, carry):
        values = stream_in[at, :] + pair_sum(mine, theirs, at)
        stream[at, :] = values
        unit_rows, _ = norm_unit(values)
        normed[at, :] = (unit_rows * small[3:4, :]).astype(BF)
        return carry

    over_rows(rows, normalise)
    normed_rows = normed[...]
    edge = jnp.zeros((EDGE, 2 * channels), F32)
    padded[:EDGE, :] = edge
    padded[EDGE + rows :, :] = edge
    for shard, weight in enumerate((conv_o, conv_t)):
        arrive(weight)
        at = columns(shard, channels)
        value_rows = product(normed_rows, weight[:, :channels])
        value[:, at] = value_rows
        gate_rows = sigmoid(product(normed_rows, weight[:, channels : 2 * channels]))
        gate[:, at] = gate_rows
        padded[EDGE : EDGE + rows, at] = (
            value_rows * gate_rows * valid_col(0, rows, channels, length)
        )
    count = length.astype(F32)
    for tile in range(2 * channels // DH):
        at = columns(tile, DH)
        total = params[0:1, at] * padded[EDGE - 2 : EDGE - 2 + rows, at]
        for offset in range(1, KW):
            begin = EDGE - 2 + offset
            total = total + params[offset : offset + 1, at] * padded[begin : begin + rows, at]
        convolved[:, at] = total
        keep = valid_col(0, rows, DH, length)
        mean = jnp.sum(total * keep, axis=0, keepdims=True) / count
        centred = (total - mean) * keep
        stats[0:1, at] = jnp.full((1, DH), count, F32)
        stats[1:2, at] = mean
        stats[2:3, at] = jnp.sum(centred * centred, axis=0, keepdims=True)
        stats[3:8, at] = jnp.zeros((5, DH), F32)


def merged(mine, theirs):
    total = mine[0:1, :] + theirs[0:1, :]
    apart = mine[1:2, :] - theirs[1:2, :]
    mean = (mine[0:1, :] * mine[1:2, :] + theirs[0:1, :] * theirs[1:2, :]) / total
    share = mine[0:1, :] * theirs[0:1, :] / total
    spread = mine[2:3, :] + theirs[2:3, :] + apart * apart * share
    return total, mean, spread


def k_merge(mine, theirs, result):
    total, mean, spread = merged(mine, theirs)
    result[0:1, :] = total
    result[1:2, :] = mean
    result[2:3, :] = spread
    result[3:8, :] = jnp.zeros((5, result.shape[1]), F32)


def k_add(mine, theirs, result):
    result[...] = mine[...] + theirs[...]


def shaped_rows(convolved, stats, params, at):
    unit_bn = (convolved[at, :] - stats[1:2, :]) * stats[2:3, :]
    return unit_bn, unit_bn * params[5:6, :] + params[6:7, :]


def k_conv_rear(
    mine, theirs, convolved, params, normed, conv_o, conv_t,
    stats, active_own, active_cross, part,
):
    rows, width = normed.shape
    channels = params.shape[1] // 2
    total, mean, spread = merged(mine, theirs)
    arrive(convolved)
    stats[0:1, :] = total
    stats[1:2, :] = mean
    stats[2:3, :] = lax.rsqrt(spread / total + EPSILON)
    stats[3:8, :] = jnp.zeros((5, stats.shape[1]), F32)

    def activate(at, first, carry):
        _, shaped = shaped_rows(convolved, stats, params, at)
        active = (shaped * sigmoid(shaped)).astype(BF)
        active_own[at, :] = active[:, :channels]
        active_cross[at, :] = active[:, channels:]
        return carry

    over_rows(rows, activate)
    arrive(conv_o, conv_t)
    own = active_own[...]
    other = active_cross[...]
    for index in range(width // TILE):
        at = columns(index)
        part[:, at] = (
            times_back(own, conv_o[at, 2 * channels :])
            + times_back(other, conv_t[at, 2 * channels :])
        ).astype(BF)


def k_ffn_two(
    mine, theirs, stream_in, small, up_o, up_t, down_o, down_t,
    stream, branch, active_cross, active_own, hidden, part,
):
    rows, width = stream_in.shape
    arrive(stream_in)

    def normalise(at, first, carry):
        values = stream_in[at, :] + pair_sum(mine, theirs, at)
        stream[at, :] = values
        unit_rows, _ = norm_unit(values)
        branch[at, :] = (unit_rows * small[4:5, :]).astype(BF)
        return carry

    over_rows(rows, normalise)
    ffn_up(branch, (up_o, up_t), hidden, active_own, active_cross)
    ffn_down(active_own, active_cross, (down_o, down_t), part)


def split_blocks(info, rows, source, own, sent):
    core, high = info[0], info[1]
    own[...] = source[pl.ds((2 * high + core) * rows, rows), :]
    sent[...] = source[pl.ds((2 * high + 1 - core) * rows, rows), :]


def k_ffn_two_back(
    info, mine, theirs, stream, small, block, across_block, arrived, hidden,
    up_o, up_t, down_o, down_t,
    out_own, out_sent, grad_four, gain_sum, branch, grad_cross, grad_own, part, out_rows, grads,
):
    rows, width = stream.shape
    arrive(block, across_block, arrived)
    place_rows(info, block, across_block, arrived, grads)
    arrive(stream)

    def pass_back(at, first, carry):
        values = stream[at, :] + 0.5 * pair_sum(mine, theirs, at)
        unit_rows, inverse = norm_unit(values)
        out_rows[at, :] = (unit_rows * small[5:6, :]).astype(BF)
        grad, fresh = norm_back(grads[at, :].astype(F32), unit_rows, inverse, small[5:6, :])
        grad_four[at, :] = grad
        branch[at, :] = (0.5 * grad).astype(BF)
        return carry + fresh

    gain_sum[...] = over_rows(rows, pass_back, jnp.zeros((1, width), F32))
    split_blocks(info, rows // 4, out_rows, out_own, out_sent)
    ffn_grad_hidden(branch, (down_o, down_t), hidden, grad_own, grad_cross)

    def store(at, values):
        part[:, at] = values.astype(BF)

    ffn_grad_input(grad_own, grad_cross, (up_o, up_t), store)


def k_conv_back_front(
    mine, theirs, stream, small, grad_in, convolved, stats, params, conv_o, conv_t,
    grad_out, gain_sum, branch, grad_shaped, sums,
):
    rows, width = stream.shape
    channels = params.shape[1] // 2
    arrive(stream)

    def pass_back(at, first, carry):
        unit_rows, inverse = norm_unit(stream[at, :])
        grad, fresh = norm_back(pair_sum(mine, theirs, at), unit_rows, inverse, small[4:5, :])
        grad = grad_in[at, :] + grad
        grad_out[at, :] = grad
        branch[at, :] = grad.astype(BF)
        return carry + fresh

    gain_sum[...] = over_rows(rows, pass_back, jnp.zeros((1, width), F32))
    branch_rows = branch[...]
    arrive(convolved)
    for shard, weight in enumerate((conv_o, conv_t)):
        arrive(weight)
        grad_shaped[:, columns(shard, channels)] = product(branch_rows, weight[:, 2 * channels :])

    def slope(at, first, carry):
        unit_bn, shaped = shaped_rows(convolved, stats, params, at)
        grad = grad_shaped[at, :] * silu_slope(shaped)
        grad_shaped[at, :] = grad
        return (
            carry[0] + jnp.sum(grad, axis=0, keepdims=True),
            carry[1] + jnp.sum(grad * unit_bn, axis=0, keepdims=True),
        )

    zero = jnp.zeros((1, 2 * channels), F32)
    shift_sum, scale_sum = over_rows(rows, slope, (zero, zero))
    sums[0:1, :] = shift_sum
    sums[1:2, :] = scale_sum
    sums[2:8, :] = jnp.zeros((6, 2 * channels), F32)


def k_conv_back_rear(
    info, sums_mine, sums_theirs, grad_shaped, convolved, stats, params, padded, value, gate, branch,
    conv_o, conv_t,
    small_sums, mixed_own, mixed_cross, part, grad_padded,
):
    length = info[2]
    rows, width = branch.shape
    channels = params.shape[1] // 2
    sums = sums_mine[0:2, :] + sums_theirs[0:2, :]
    small_sums[5:6, :] = sums[0:1, :]
    small_sums[6:7, :] = sums[1:2, :]
    small_sums[7:8, :] = jnp.zeros((1, 2 * channels), F32)
    edge = jnp.zeros((EDGE, 2 * channels), F32)
    grad_padded[:EDGE, :] = edge
    grad_padded[EDGE + rows :, :] = edge
    arrive(convolved)
    count, bn_inverse, scale_row = stats[0:1, :], stats[2:3, :], params[5:6, :]
    grad_centre = -bn_inverse * scale_row * sums[0:1, :]
    grad_spread = -bn_inverse * bn_inverse * scale_row * sums[1:2, :]

    def spread(at, first, carry):
        centred = convolved[at, :] - stats[1:2, :]
        keep = valid_col(first, STEP, 2 * channels, length)
        grad = grad_shaped[at, :] * scale_row * bn_inverse + keep * (
            grad_centre + grad_spread * centred
        ) * (1.0 / count)
        grad_padded[pl.ds(pl.multiple_of(EDGE + first, EDGE), STEP), :] = grad
        return carry

    over_rows(rows, spread)
    arrive(padded, gate, value)
    for tile in range(2 * channels // DH):
        at = columns(tile, DH)
        grad = grad_padded[EDGE : EDGE + rows, at]
        back = None
        for offset in range(KW):
            begin = EDGE + 2 - offset
            term = params[offset : offset + 1, at] * grad_padded[begin : begin + rows, at]
            back = term if back is None else back + term
            begin = EDGE - 2 + offset
            small_sums[offset : offset + 1, at] = jnp.sum(
                grad * padded[begin : begin + rows, at], axis=0, keepdims=True
            )
        back = back * valid_col(0, rows, DH, length)
        gate_rows = gate[:, at]
        first_grad = (back * gate_rows).astype(BF)
        second_grad = (back * value[:, at] * gate_rows * (1.0 - gate_rows)).astype(BF)
        inner = (tile * DH) % channels
        if tile * DH < channels:
            mixed_own[:, inner : inner + DH] = first_grad
            mixed_own[:, channels + inner : channels + inner + DH] = second_grad
        else:
            mixed_cross[:, inner : inner + DH] = first_grad
            mixed_cross[:, channels + inner : channels + inner + DH] = second_grad
    arrive(conv_o, conv_t)
    own = mixed_own[...]
    other = mixed_cross[...]
    for index in range(width // TILE):
        at = columns(index)
        part[:, at] = (
            times_back(own, conv_o[at, : 2 * channels])
            + times_back(other, conv_t[at, : 2 * channels])
        ).astype(BF)


def k_attn_back(
    mine, theirs, stream, small, grad_in, sums_in, qkv, weights, qkv_o, qkv_t, out_o, out_t,
    grad_out, gain_sum, branch, three_cross, three_own, small_sums, part, grad_context,
):
    rows, width = stream.shape
    arrive(stream)
    third = qkv_o.shape[1] // 3
    heads = third // DH

    def pass_back(at, first, carry):
        unit_rows, inverse = norm_unit(stream[at, :])
        grad, fresh = norm_back(pair_sum(mine, theirs, at), unit_rows, inverse, small[3:4, :])
        grad = grad_in[at, :] + grad
        grad_out[at, :] = grad
        branch[at, :] = grad.astype(BF)
        return carry + fresh

    gain_sum[...] = over_rows(rows, pass_back, jnp.zeros((1, width), F32))
    branch_rows = branch[...]
    for shard, weight in enumerate((out_o, out_t)):
        arrive(weight)
        grad_context[:, columns(shard, third)] = times_back(branch_rows, weight[...]).astype(BF)
    away = lax.broadcasted_iota(jnp.int32, (rows, rows), 1) - row_iota(0, rows, rows)
    relative = jnp.clip(away, -REACH, REACH).astype(F32) * (1.0 / REACH)
    scale = DH ** (-0.5)
    arrive(qkv, weights)
    lanes = small_sums.shape[1]
    lane = lax.broadcasted_iota(jnp.int32, (1, lanes), 1)
    slope_row = jnp.zeros((1, lanes), F32)
    for shard in range(2):
        base = 3 * third * shard
        for head in range(heads):
            place = shard * heads + head
            query = qkv[:, base + head * DH : base + (head + 1) * DH]
            key = qkv[:, base + third + head * DH : base + third + (head + 1) * DH]
            value = qkv[:, base + 2 * third + head * DH : base + 2 * third + (head + 1) * DH]
            grad_head = grad_context[:, place * DH : (place + 1) * DH]
            soft = weights[place]
            grad_soft = times_back(grad_head, value)
            grad_value = inner_rows(soft.astype(BF), grad_head)
            dots = jnp.sum(soft * grad_soft, axis=-1, keepdims=True)
            grad_scores = (soft * (grad_soft - dots)).astype(BF)
            tilted = jnp.sum(grad_scores.astype(F32) * relative, axis=0, keepdims=True)
            slope = jnp.broadcast_to(jnp.sum(tilted, axis=1, keepdims=True), (1, lanes))
            slope_row = jnp.where(lane == shard * (lanes // 2) + head, slope, slope_row)
            grads = (
                product(grad_scores, key) * scale,
                inner_rows(grad_scores, query) * scale,
                grad_value,
            )
            for index, grad in enumerate(grads):
                begin = index * third + head * DH
                if shard == 0:
                    three_own[:, begin : begin + DH] = grad.astype(BF)
                else:
                    three_cross[:, begin : begin + DH] = grad.astype(BF)
    small_sums[:7, :] = sums_in[:7, :]
    small_sums[7:8, :] = slope_row
    arrive(qkv_o, qkv_t)
    own = three_own[...]
    other = three_cross[...]
    for index in range(width // TILE):
        at = columns(index)
        part[:, at] = (times_back(own, qkv_o[at, :]) + times_back(other, qkv_t[at, :])).astype(BF)


def k_ffn_one_back(
    info, mine, theirs, stream, small, grad_in, hidden, up_o, up_t, down_o, down_t,
    grad_out, gain_sum, branch, grad_cross, grad_own, part_own, part_sent, whole,
):
    high = info[1]
    rows, width = stream.shape
    span = rows // 2
    arrive(stream)

    def pass_back(at, first, carry):
        unit_rows, inverse = norm_unit(stream[at, :])
        grad, fresh = norm_back(pair_sum(mine, theirs, at), unit_rows, inverse, small[2:3, :])
        grad = grad_in[at, :] + grad
        grad_out[at, :] = grad
        branch[at, :] = (0.5 * grad).astype(BF)
        return carry + fresh

    gain_sum[...] = over_rows(rows, pass_back, jnp.zeros((1, width), F32))
    ffn_grad_hidden(branch, (down_o, down_t), hidden, grad_own, grad_cross)

    def store(at, values):
        whole[:, at] = values

    ffn_grad_input(grad_own, grad_cross, (up_o, up_t), store)
    part_own[...] = whole[pl.ds(high * span, span), :]
    part_sent[...] = whole[pl.ds((1 - high) * span, span), :].astype(BF)


def k_last(
    info, starts, part_own, arrived, frames, small, grad_in,
    grad_own, grad_sent, sums, grads,
):
    core, high, length = info[0], info[1], info[2]
    span, width = part_own.shape
    arrive(frames)

    def pass_back(at, first, carry):
        begin = pl.multiple_of(high * span + first, STEP)
        mask = mask_col(starts, begin, STEP, length)
        unit_rows, inverse = norm_unit(
            masked_rows(frames[pl.ds(begin, STEP), :], mask, small[0:1, :])
        )
        grad_normed = part_own[at, :] + arrived[at, :].astype(F32)
        grad, fresh = norm_back(grad_normed, unit_rows, inverse, small[1:2, :])
        grad = grad_in[pl.ds(begin, STEP), :] + grad
        hit = jnp.broadcast_to(mask, grad.shape) > 0.5
        grads[at, :] = jnp.where(hit, 0.0, grad)
        masked_part = jnp.sum(jnp.where(hit, grad, 0.0), axis=0, keepdims=True)
        return carry[0] + masked_part, carry[1] + fresh

    zero = jnp.zeros((1, width), F32)
    mask_sum, gain_sum = over_rows(span, pass_back, (zero, zero))
    sums[0:1, :] = mask_sum
    sums[1:2, :] = gain_sum
    rows = span // 2
    grad_own[...] = grads[pl.ds(core * rows, rows), :]
    grad_sent[...] = grads[pl.ds((1 - core) * rows, rows), :]


def k_weights(pairs, bit, tiles, info, *refs):
    count = 1 + max(max(pair[place] for place in (0, 1, 2, 4)) for pair in pairs)
    inputs, kept, sent = refs[:count], refs[count], refs[count + 1 :]
    mine = (info[3] >> bit) & 1
    low = bit - tiles
    rows = kept.shape[1]
    cut = sent[0].shape[2]
    for index in range(kept.shape[0]):
        high_part, low_part = index >> low, index & ((1 << low) - 1)
        for side in range(2):
            tile = (high_part * 2 + (mine ^ side)) * (1 << low) + low_part
            at = pl.ds(pl.multiple_of(tile * rows, rows), rows)
            begin = 0
            for left, left_too, right, shift, right_too, shift_too, size in pairs:
                for piece in range(0, size, TILE):
                    grad = inner_rows(
                        inputs[left][:, at],
                        inputs[right][:, shift + piece : shift + piece + TILE],
                    ) + inner_rows(
                        inputs[left_too][:, at],
                        inputs[right_too][:, shift_too + piece : shift_too + piece + TILE],
                    )
                    place = begin + piece
                    if side == 0:
                        kept[index, :, place : place + TILE] = grad
                    else:
                        inside = place % cut
                        sent[place // cut][index, :, inside : inside + TILE] = grad.astype(BF)
                begin += size


def k_fold(bit, count, info, held, *refs):
    arrivals, kept, sent = refs[:count], refs[count], refs[count + 1 :]
    mine = (info[3] >> bit) & 1
    cut_in, cut_out = arrivals[0].shape[3], sent[0].shape[2]
    size = min(cut_in, cut_out)
    for index in range(held.shape[0]):
        for side in range(2):
            at = pl.ds(mine ^ side, 1)
            for begin in range(0, held.shape[3], size):
                spot = slice(begin, begin + size)
                inside = slice(begin % cut_in, begin % cut_in + size)
                total = held[index, at, :, spot][0]
                total = total + arrivals[begin // cut_in][index, at, :, inside][0].astype(F32)
                if side == 0:
                    kept[index, :, spot] = total
                else:
                    inside = slice(begin % cut_out, begin % cut_out + size)
                    sent[begin // cut_out][index, :, inside] = total.astype(BF)


def k_finish(turned, count, info, kept, *refs):
    arrivals, results = refs[:count], refs[count:]
    cut = arrivals[0].shape[1]
    begin = 0
    for result, turn in zip(results, turned):
        size = result.shape[0] if turn else result.size // result.shape[0]
        for piece in range(begin, begin + size, DH):
            spot = slice(piece, piece + DH)
            at = piece - begin
            inside = slice(piece % cut, piece % cut + DH)
            total = kept[:, spot] + arrivals[piece // cut][:, inside].astype(F32)
            if turn:
                result[at : at + DH, :] = total.T
            elif len(result.shape) == 3:
                result[:, at // result.shape[2], pl.ds(at % result.shape[2], DH)] = total
            else:
                result[:, at : at + DH] = total
        begin += size


def k_in_order(info, own, other, result):
    core = info[0]
    result[pl.ds(core, 1)] = own[...][None]
    result[pl.ds(1 - core, 1)] = other[...][None]


def k_gather(bit, info, held, arrived, result):
    mine = (info[3] >> bit) & 1
    result[:, pl.ds(mine, 1)] = held[...][:, None]
    result[:, pl.ds(1 - mine, 1)] = arrived[...][:, None]


def k_smalls(last, attn, conv, two, final, channel_sums, result):
    width = attn.shape[1]
    result[0:2, :width] = last[...]
    for place, entry in enumerate((attn, conv, two, final), 2):
        result[place : place + 1, :width] = 0.5 * entry[...]
    result[6:8, :width] = jnp.zeros((2, width), F32)
    result[:, width:] = channel_sums[...]


def k_smalls_cross(smalls, result):
    width = smalls.shape[1] - 2 * (smalls.shape[1] - result.shape[1])
    channels = result.shape[1] - width
    result[:, :width] = smalls[:, :width]
    result[:, width:] = smalls[:, width + channels :]


def k_gains(mine, theirs, channel_sums, result):
    width = mine.shape[1]
    result[:, :width] = mine[...] + theirs[...]
    result[:, width:] = channel_sums[...]


def k_smalls_add(smalls, arrived, result):
    size = result.shape[1]
    result[...] = smalls[:, :size] + arrived[...]


def run(kernel, results, arguments, scalars=1, scratch=(), late=(), leaving=(), cost=1):
    given, made = len(arguments), len(results)
    hbm_shapes = [(arguments[place].shape, arguments[place].dtype) for place in late]
    hbm_shapes += [results[place] for place in leaving]
    buffers = [pltpu.VMEM(shape, kind) for shape, kind in hbm_shapes]
    own = [pltpu.VMEM(shape, kind) for shape, kind in scratch]
    hbm = pl.BlockSpec(memory_space=pltpu.HBM)

    def body(*refs):
        ins, outs = list(refs[:given]), list(refs[given : given + made])
        rest = refs[given + made :]
        extra, held, semaphores = rest[: len(own)], rest[len(own) : -1], rest[-1]
        for index, place in enumerate(late):
            ins[place] = Late(ins[place], held[index], semaphores.at[index])
        for index, place in enumerate(leaving, len(late)):
            outs[place] = Leaving(outs[place], held[index], semaphores.at[index])
        kernel(*ins, *outs, *extra)
        arrive(*ins)
        for place in leaving:
            outs[place].finish()

    def plain(*refs):
        kernel(*refs)

    held_bytes = sum(
        functools.reduce(lambda a, b: a * b, shape) * jnp.dtype(kind).itemsize
        for shape, kind in [*scratch, *hbm_shapes]
    )
    specs = [SMEM_SPEC] * scalars + [VMEM_SPEC] * (given - scalars)
    out_specs = [VMEM_SPEC] * made
    for place in late:
        specs[place] = hbm
    for place in leaving:
        out_specs[place] = hbm
    many = len(hbm_shapes)
    return pl.pallas_call(
        body if many else plain,
        out_shape=[
            pltpu.HBM(shape, kind) if place in leaving else pltpu.VMEM(shape, kind)
            for place, (shape, kind) in enumerate(results)
        ],
        in_specs=specs,
        out_specs=out_specs,
        scratch_shapes=own + buffers + ([pltpu.SemaphoreType.DMA((many,))] if many else []),
        compiler_params=pltpu.CompilerParams(vmem_limit_bytes=held_bytes + 8 * MIB),
        cost_estimate=pl.CostEstimate(flops=cost, bytes_accessed=cost, transcendentals=0),
    )(*(
        entry if place < scalars else pltpu.with_memory_space_constraint(
            entry, pltpu.HBM if place in late else pltpu.VMEM
        )
        for place, entry in enumerate(arguments)
    ))


def swap(value, axis, bit):
    size = lax.axis_size(axis)
    return lax.ppermute(value, axis, [(place, place ^ bit) for place in range(size)])


def across(value):
    return swap(value, "tensor", 2)


def beside(value):
    return swap(value, "tensor", 1)


def bit_of(axis, bit):
    return (lax.axis_index(axis) & bit) != 0


def tie(*values):
    return lax.optimization_barrier(values)


class RowSum:
    def __init__(self, info, inputs, pairs, width, first_bits, cuts=1, cost=1):
        size = lax.axis_size("dp")
        levels = size.bit_length() - 1
        tiles = max(levels - 3, 0)
        order = [tiles + bit for bit in first_bits]
        self.order = order + [bit for bit in range(levels - 1, -1, -1) if bit not in order]
        self.left = list(range(levels - 1, -1, -1))
        self.total = sum(pair[-1] for pair in pairs)
        self.block = width // size
        self.info = info
        count = size >> tiles
        shape = (count // 2, width // count)
        self.kept, *self.sent = run(
            functools.partial(k_weights, pairs, self.order[0], tiles),
            [((*shape, self.total), F32)] + [((*shape, self.total // cuts), BF)] * cuts,
            [info] + inputs,
            cost=cost,
        )
        self.begin()

    def begin(self):
        self.bit = self.order.pop(0)
        self.left.remove(self.bit)
        self.arrived = []

    def send(self, chain=None):
        piece = self.sent.pop(0)
        if chain is not None:
            (piece,) = chain.after(piece)
        self.arrived.append(swap(piece, "dp", 1 << self.bit))

    def here(self, chain):
        (self.arrived[-1],) = chain.after(self.arrived[-1])

    def fold(self, chain, cuts=1):
        bit = self.order[0]
        place = self.left.index(bit)
        inner = self.block << (len(self.left) - 1 - place)
        outer = 1 << place
        kept, *arrived = chain.after(self.kept, *self.arrived)
        self.kept, *self.sent = run(
            functools.partial(k_fold, bit, len(arrived)),
            [((outer, inner, self.total), F32)] + [((outer, inner, self.total // cuts), BF)] * cuts,
            [self.info, kept.reshape(outer, 2, inner, self.total)]
            + [entry.reshape(outer, 2, inner, -1) for entry in arrived],
        )
        self.kept, chain.last = tie(self.kept, chain.last)
        self.begin()

    def step(self, chain):
        self.fold(chain)
        self.send()

    def finish(self, chain, *results):
        while self.order:
            self.step(chain)
        shape = (self.block, self.total)
        kept, *arrived = chain.after(
            self.kept.reshape(shape), *(entry.reshape(self.block, -1) for entry in self.arrived)
        )
        sums = run(
            functools.partial(k_finish, tuple(turn for _, turn in results), len(arrived)),
            [(size, F32) for size, _ in results],
            [self.info, kept, *arrived],
        )
        *sums, chain.last = tie(*sums, chain.last)
        return sums


class Chain:
    def __init__(self, last):
        self.last = last

    def after(self, *values):
        *values, self.last = tie(*values, self.last)
        return values


class Gather:
    def __init__(self, info, block):
        self.info, self.held = info, block.reshape(1, *block.shape)
        self.bit = lax.axis_size("dp") // 2
        self.shape = (lax.axis_size("dp") * block.shape[0], block.shape[1])

    def send(self):
        self.arrived = swap(self.held, "dp", self.bit)

    def take(self):
        outer, rows, width = self.held.shape
        (held,) = run(
            functools.partial(k_gather, self.bit.bit_length() - 1),
            [((outer, 2, rows, width), self.held.dtype)],
            [self.info, self.held, self.arrived],
        )
        self.held = held.reshape(outer * 2, rows, width)
        self.bit //= 2

    def whole(self):
        while self.bit:
            self.send()
            self.take()
        return self.held.reshape(self.shape)


def sum_pair(value, axis, merge=None):
    bit, size = 1, lax.axis_size(axis)
    while bit * 2 < size:
        (value,) = run(
            merge or k_add, [(value.shape, F32)], [value, swap(value, axis, bit)], scalars=0
        )
        bit *= 2
    return value, swap(value, axis, bit)


def per_device(
    frames,
    lengths,
    span_starts,
    mask_vector,
    ffn1_gain,
    ffn1_up,
    ffn1_down,
    attn_gain,
    query_weight,
    key_weight,
    value_weight,
    output_weight,
    rel_slope,
    conv_gain,
    conv_up,
    conv_depth,
    bn_scale,
    bn_shift,
    conv_down,
    ffn2_gain,
    ffn2_up,
    ffn2_down,
    final_gain,
    cotangent,
):
    batches, row_count, width = frames.shape
    length = row_count * lax.axis_size("tensor")
    span = 2 * row_count
    channels = conv_depth.shape[1]
    hidden_width = ffn1_up.shape[1]
    heads = rel_slope.shape[0]
    third = query_weight.shape[1]
    core = lax.axis_index("tensor") & 1
    high = (lax.axis_index("tensor") >> 1) & 1
    group = lax.axis_index("dp")
    on_first = core == 0
    own_length = jnp.where(on_first, lengths[0], lengths[1])
    info = jnp.stack([core, high, own_length, group]).astype(jnp.int32)
    starts = jnp.where(on_first, span_starts[0:1], span_starts[1:2])

    def gather_rows(block):
        across_block = across(block)
        (sent,) = run(k_pick, [(block.shape, BF)], [info, block, across_block])
        return [block, across_block, beside(sent)]

    conv_block = jnp.concatenate(
        [conv_up.reshape(conv_up.shape[0], 2 * channels), conv_down.T], axis=1
    )
    conv_weights = Gather(info, conv_block)
    conv_weights.send()
    frame_parts = gather_rows(frames)
    part = mask_vector.shape[0]
    place = (group * lax.axis_size("tensor") + lax.axis_index("tensor")) * part
    vectors = jnp.stack(
        [mask_vector.astype(F32), ffn1_gain, attn_gain, conv_gain, ffn2_gain, final_gain,
         jnp.zeros_like(ffn1_gain), jnp.zeros_like(ffn1_gain)]
    )
    small = lax.dynamic_update_slice(jnp.zeros((8, width), F32), vectors, (0, place))
    hops = [("tensor", 1), ("dp", 2), ("dp", 1), ("tensor", 2)]
    bit = 4
    while bit < lax.axis_size("dp"):
        hops.append(("dp", bit))
        bit *= 2
    for step, (axis, bit) in enumerate(hops):
        if step == 3:
            conv_weights.arrived, small = tie(conv_weights.arrived, small)
            conv_weights.take()
            if conv_weights.bit:
                conv_weights.send()
        if bit < lax.axis_size(axis):
            (small,) = run(
                k_add, [(small.shape, F32)], [small, swap(small, axis, bit)], scalars=0
            )
    if conv_weights.bit:
        conv_weights.arrived, small = tie(conv_weights.arrived, small)
        conv_weights.take()
    conv_weights.held, small = tie(conv_weights.held, small)
    if conv_weights.bit:
        conv_weights.send()
    up_one, down_one = beside(ffn1_up), beside(ffn1_down)

    wide = (length, width)
    ffn_outs = [
        (wide, BF),
        ((length, hidden_width), BF),
        ((length, hidden_width), BF),
        ((length, 2 * hidden_width), F32),
        (wide, BF),
    ]
    whole, norm_one, cross_one, active_one, hidden_one, partial = run(
        k_ffn_one,
        [(wide, BF)] + ffn_outs,
        [info, starts, *frame_parts, small, ffn1_up, up_one, ffn1_down, down_one],
        scratch=[(wide, BF)], late=(6, 7, 8, 9),
    )
    query_weight, key_weight, value_weight, output_weight, rel_slope, active_one = tie(
        query_weight, key_weight, value_weight, output_weight, rel_slope, active_one
    )
    own_qkv = jnp.concatenate([query_weight, key_weight, value_weight], axis=1)
    other_qkv, other_out = beside(own_qkv), beside(output_weight)
    slope_row = jnp.pad(rel_slope[None], ((0, 0), (0, channels - heads)))
    own_params = jnp.concatenate([conv_depth, bn_scale[None], bn_shift[None], slope_row])
    other_params = beside(own_params)
    params = jnp.concatenate([own_params, other_params], axis=1)
    slopes = jnp.concatenate([rel_slope, other_params[KW + 2, :heads]])
    stream_one, norm_attn, context_cross, context_own, qkv, weights, partial = run(
        k_attn_wrapped,
        [
            (wide, F32),
            (wide, BF),
            ((length, third), BF),
            ((length, third), BF),
            ((length, 6 * third), BF),
            ((2 * heads, length, length), F32),
            (wide, BF),
        ],
        [info, slopes, starts, partial, across(partial), whole, small, own_qkv, other_qkv,
         output_weight, other_out],
        scalars=2, late=(7, 8, 9, 10),
    )
    conv_weights.arrived, norm_one, cross_one, context_own = tie(
        conv_weights.arrived, norm_one, cross_one, context_own
    )
    conv_weights.take()
    own_conv = conv_weights.whole()
    other_conv = beside(own_conv)
    norm_one_too, cross_one_too = beside(norm_one), beside(cross_one)
    norm_one_too, cross_one_too, params = tie(norm_one_too, cross_one_too, params)
    both_channels = (length, 2 * channels)
    stat_shape = ((8, 2 * channels), F32)
    stream_two, norm_conv, value, gate, padded, convolved, stats = run(
        k_conv_front,
        [
            (wide, F32),
            (wide, BF),
            (both_channels, F32),
            (both_channels, F32),
            ((length + 2 * EDGE, 2 * channels), F32),
            (both_channels, F32),
            stat_shape,
        ],
        [info, partial, across(partial), stream_one, small, params, own_conv, other_conv],
        late=(6, 7),
    )
    norm_attn, context_cross, cotangent, ffn2_up, ffn2_down, value = tie(
        norm_attn, context_cross, cotangent, ffn2_up, ffn2_down, value
    )
    stats, stats_too = sum_pair(stats, "dp", k_merge)
    grad_across = across(cotangent)
    up_two, down_two = beside(ffn2_up), beside(ffn2_down)
    norm_attn_too, context_cross_too = beside(norm_attn), beside(context_cross)
    norm_attn_too, context_cross_too, params, grad_across = tie(
        norm_attn_too, context_cross_too, params, grad_across
    )
    stats, active_conv, cross_conv, partial = run(
        k_conv_rear,
        [stat_shape, ((length, channels), BF), ((length, channels), BF), (wide, BF)],
        [stats, stats_too, convolved, params, norm_conv, own_conv, other_conv],
        scalars=0, late=(5, 6),
    )
    grad_across, active_conv = tie(grad_across, active_conv)
    (sent,) = run(k_pick, [(cotangent.shape, BF)], [info, cotangent, grad_across])
    grad_parts = [cotangent, grad_across, beside(sent)]
    grad_parts[2], small = tie(grad_parts[2], small)
    stream_three, norm_two, cross_two, active_two, hidden_two, partial = run(
        k_ffn_two,
        [(wide, F32)] + ffn_outs,
        [partial, across(partial), stream_two, small, ffn2_up, up_two, ffn2_down, down_two],
        scalars=0, late=(4, 5, 6, 7),
    )
    norm_two, cross_two, norm_conv, cross_conv, active_two = tie(
        norm_two, cross_two, norm_conv, cross_conv, active_two
    )
    norm_two_too, cross_two_too = beside(norm_two), beside(cross_two)
    norm_conv_too, cross_conv_too = beside(norm_conv), beside(cross_conv)
    norm_two_too, cross_two_too, norm_conv_too, cross_conv_too, small = tie(
        norm_two_too, cross_two_too, norm_conv_too, cross_conv_too, small
    )

    row_shape = ((1, width), F32)
    block_shape = (row_count, width)
    out_own, out_sent, grad_four, sum_final, back_two, hid_cross_two, hid_two, partial = run(
        k_ffn_two_back,
        [
            (block_shape, BF),
            (block_shape, BF),
            (wide, F32),
            row_shape,
            (wide, BF),
            ((length, hidden_width), BF),
            ((length, hidden_width), BF),
            (wide, BF),
        ],
        [info, partial, across(partial), stream_three, small, *grad_parts, hidden_two,
         ffn2_up, up_two, ffn2_down, down_two],
        scratch=[(wide, BF), (wide, BF)], late=(9, 10, 11, 12),
    )
    back_two_too, hid_cross_two_too = beside(back_two), beside(hid_cross_two)
    ffn_pair = ((0, 1, 2, 0, 3, 0, hidden_width),)
    two_up = RowSum(
        info, [norm_two, norm_two_too, hid_two, hid_cross_two_too], ffn_pair, width, (0, 1, 2)
    )
    two_down = RowSum(
        info, [back_two, back_two_too, active_two, cross_two_too], ffn_pair, width, (1, 2, 0)
    )
    grad_four, two_up.sent[0], two_down.sent[0] = tie(
        grad_four, two_up.sent[0], two_down.sent[0]
    )
    grad_three, sum_two, back_conv, grad_shaped, sums = run(
        k_conv_back_front,
        [(wide, F32), row_shape, (wide, BF), (both_channels, F32), stat_shape],
        [partial, across(partial), stream_three, small, grad_four, convolved, stats, params,
         own_conv, other_conv],
        scalars=0, late=(8, 9),
    )
    out_sent, sum_two, back_conv = tie(out_sent, sum_two, back_conv)
    out_other, back_conv_too = beside(out_sent), beside(back_conv)
    sums, sums_too = sum_pair(sums, "dp")
    sums_too, out_other, back_conv_too = tie(sums_too, out_other, back_conv_too)
    chain = Chain(sums_too)
    two_up.send(chain)
    two_down.send(chain)
    sums_too = chain.last
    small_sums, mixed_own, mixed_cross, partial = run(
        k_conv_back_rear,
        [
            stat_shape,
            ((length, 2 * channels), BF),
            ((length, 2 * channels), BF),
            (wide, BF),
        ],
        [info, sums, sums_too, grad_shaped, convolved, stats, params, padded, value, gate,
         back_conv, own_conv, other_conv],
        scratch=[((length + 2 * EDGE, 2 * channels), F32)], late=(11, 12),
    )
    mixed_cross_too = beside(mixed_cross)
    mixed_cross_too, grad_three = tie(mixed_cross_too, grad_three)
    grad_two, sum_conv, back_attn, three_cross, three_own, small_sums, partial = run(
        k_attn_back,
        [
            (wide, F32),
            row_shape,
            (wide, BF),
            ((length, 3 * third), BF),
            ((length, 3 * third), BF),
            stat_shape,
            (wide, BF),
        ],
        [partial, across(partial), stream_two, small, grad_three, small_sums, qkv, weights,
         own_qkv, other_qkv, output_weight, other_out],
        scalars=0,
        scratch=[((length, 2 * third), BF)], late=(8, 9, 10, 11),
    )
    back_attn_too, three_cross_too = beside(back_attn), beside(three_cross)
    chain = Chain(small_sums)
    for entry in (two_up, two_down):
        entry.step(chain)
    back_attn, three_own = chain.after(back_attn, three_own)
    small_sums = chain.last
    middle = RowSum(
        info,
        [norm_conv, norm_conv_too, mixed_own, mixed_cross_too,
         back_conv, back_conv_too, active_conv, cross_conv_too,
         norm_attn, norm_attn_too, three_own, three_cross_too,
         back_attn, back_attn_too, context_own, context_cross_too],
        (
            (0, 1, 2, 0, 3, 0, 2 * channels),
            (4, 5, 6, 0, 7, 0, channels),
            (8, 9, 10, 0, 11, 0, 3 * third),
            (12, 13, 14, 0, 15, 0, third),
        ),
        width, (0, 1, 2),
    )
    middle.send()
    middle.kept, grad_two = tie(middle.kept, grad_two)
    grad_one, sum_attn, back_one, hid_cross_one, hid_one, last_own, last_sent = run(
        k_ffn_one_back,
        [
            (wide, F32),
            row_shape,
            (wide, BF),
            ((length, hidden_width), BF),
            ((length, hidden_width), BF),
            ((span, width), F32),
            ((span, width), BF),
        ],
        [info, partial, across(partial), stream_one, small, grad_two, hidden_one,
         ffn1_up, up_one, ffn1_down, down_one],
        scratch=[(wide, F32)], late=(7, 8, 9, 10),
    )
    back_one_too, hid_cross_one_too = beside(back_one), beside(hid_cross_one)
    one_up = RowSum(
        info, [norm_one, norm_one_too, hid_one, hid_cross_one_too], ffn_pair, width, (0, 1, 2),
        cost=COST,
    )
    one_down = RowSum(
        info, [back_one, back_one_too, active_one, cross_one_too], ffn_pair, width, (0, 1, 2),
        cost=COST,
    )
    chain = Chain(sum_attn)
    for entry in (one_up, one_down):
        entry.send(chain)
        entry.kept, chain.last = tie(entry.kept, chain.last)
    for entry in (middle, two_up, two_down):
        entry.step(chain)
    (starts,) = chain.after(starts)
    sum_attn = chain.last
    frames_own, frames_sent, last_sums = run(
        k_last,
        [(block_shape, F32), (block_shape, F32), ((2, width), F32)],
        [info, starts, last_own, across(last_sent), whole, small, grad_one],
        scratch=[((span, width), F32)],
    )
    frames_other = beside(frames_sent)
    (smalls,) = run(
        k_smalls, [((8, width + 2 * channels), F32)],
        [last_sums, sum_attn, sum_conv, sum_two, sum_final, small_sums], scalars=0,
    )
    (smalls_sent,) = run(k_smalls_cross, [((8, width + channels), F32)], [smalls], scalars=0)
    (smalls,) = run(
        k_smalls_add, [((8, width + channels), F32)], [smalls, beside(smalls_sent)], scalars=0
    )
    gains, gains_too = smalls[:, :width], across(smalls[:, :width])
    block = width // lax.axis_size("dp")
    (gains,) = run(
        k_gains, [(smalls.shape, F32)], [gains, gains_too, smalls[:, width:]], scalars=0
    )
    chain = Chain(frames_own)
    one_up.step(chain)
    (two_up,) = two_up.finish(chain, ((block, hidden_width), False))
    middle.step(chain)
    one_up.step(chain)
    one_down.step(chain)
    (gains,) = chain.after(gains)
    gains_too = swap(gains, "dp", 1)
    conv_up_grad, conv_down_grad, query_grad, key_grad, value_grad, output_grad = middle.finish(
        chain,
        (conv_up.shape, False), ((channels, block), True),
        *[((block, third), False)] * 3, ((third, block), True),
    )
    (two_down,) = two_down.finish(chain, ((hidden_width, block), True))
    one_down.step(chain)
    (one_up,) = one_up.finish(chain, ((block, hidden_width), False))
    gains, gains_too = chain.after(gains, gains_too)
    (gains,) = run(k_add, [(gains.shape, F32)], [gains, gains_too], scalars=0)
    bit = 2
    while bit < lax.axis_size("dp"):
        (gains,) = run(
            k_add, [(gains.shape, F32)], [gains, swap(gains, "dp", bit)], scalars=0
        )
        bit *= 2
    (one_down,) = one_down.finish(chain, ((hidden_width, block), True))
    frames_own = chain.last

    channel_sums = gains[:, width:]
    scale_grad = channel_sums[KW + 1] * (1.0 / lax.axis_size("dp"))
    shift_grad = channel_sums[KW] * (1.0 / lax.axis_size("dp"))
    gains = lax.dynamic_slice_in_dim(gains, place, part, axis=1)

    def in_order(own, other):
        return run(k_in_order, [((2, *own.shape), own.dtype)], [info, own, other])[0]

    return (
        in_order(out_own, out_other),
        in_order(frames_own, frames_other),
        gains[0],
        gains[1],
        one_up,
        one_down,
        gains[2],
        query_grad,
        key_grad,
        value_grad,
        output_grad,
        channel_sums[KW + 2, :heads],
        gains[3],
        conv_up_grad,
        channel_sums[:KW],
        scale_grad,
        shift_grad,
        conv_down_grad,
        gains[4],
        two_up,
        two_down,
        gains[5],
    )


def k_attn_wrapped(info, slopes, starts, *refs):
    k_attn(info, starts, slopes, *refs)


def solution(mesh):
    every, split, by_column = P(("dp", "tensor")), P("tensor"), P(None, "tensor")
    rows_by = P("dp", "tensor", None)
    return jax.shard_map(
        per_device,
        mesh=mesh,
        in_specs=(
            rows_by,
            P("dp"),
            P("dp", None),
            every,
            every,
            by_column,
            P("tensor", None),
            every,
            by_column,
            by_column,
            by_column,
            P("tensor", None),
            split,
            every,
            P("dp", None, "tensor"),
            by_column,
            split,
            split,
            P("tensor", "dp"),
            every,
            by_column,
            P("tensor", None),
            every,
            rows_by,
        ),
        out_specs=(
            rows_by,
            rows_by,
            every,
            every,
            P("dp", "tensor"),
            P("tensor", "dp"),
            every,
            P("dp", "tensor"),
            P("dp", "tensor"),
            P("dp", "tensor"),
            P("tensor", "dp"),
            split,
            every,
            P("dp", None, "tensor"),
            by_column,
            split,
            split,
            P("tensor", "dp"),
            every,
            P("dp", "tensor"),
            P("tensor", "dp"),
            every,
        ),
        check_vma=False,
    )
```

time: 642 us -> 357 us (0.56); the launches traced: 630 us -> 357 us
  other arithmetic: 202 us -> 1.42 us
  local copies, waits for them, and re-layouts: 119 us -> 22.2 us
  Pallas kernels: 0 us -> 75.1 us
  matrix products: 61.3 us -> 0 us
  waiting for transfers between devices: 151 us -> 192 us
  starting transfers between devices: 88.9 us -> 63.5 us
    pallas_call x0 -> x54, Pallas kernels: none -> 75.1 us  [run(): pl.pallas_call(body if many else plain, out_shape=[pltpu.HBM(shape, kind)...]
    convert_element_type x66 -> x0, other arithmetic: 66.6 us -> none  [the longest x24 22.7 us: scatter_rows(): sent = pick(held, axis, jnp.logical_not(mine)).astype(BF)]
    dot_general x58 -> x0, matrix products: 56.8 us -> none  [the longest x20 17.1 us: product(): return jnp.dot(left, right, preferred_element_type=F32)]
    ppermute x104 -> x72, waiting for transfers between devices: 151 us -> 192 us  [swap(): lax.ppermute(value, axis, [(place, place ^ bit) for place in range(size)])]
    reduce_sum x35 -> x0, other arithmetic: 39.7 us -> none  [the longest x10 14.6 us: norm_unit(): centre = jnp.mean(values, axis=-1, keepdims=True)]
    unnamed x725 -> x68, local copies, waits for them, and re-layouts: 54.4 us -> 18.1 us
    ppermute x104 -> x72, starting transfers between devices: 88.9 us -> 63.5 us  [swap(): lax.ppermute(value, axis, [(place, place ^ bit) for place in range(size)])]
    add x43 -> x0, other arithmetic: 25.2 us -> none  [the longest x20 20.1 us: scatter_rows(): held = pick(held, axis, mine) + swap(sent, 'dp', 1 << level).astype(F32)]
  transfers between devices with their start and end apart: 104 -> 72, of which waited for: 38 -> 39; matrix products, arithmetic and copies ran while one was open for 52% -> 4% of each run, Pallas kernels for 0% -> 13%
where the time goes in v2:
time: 357 us
  waiting for transfers between devices  192 us (54%)
  Pallas kernels  75.1 us (21%)
  starting transfers between devices  63.5 us (18%)
  local copies, waits for them, and re-layouts  22.2 us (6%)
    ppermute x72, waiting for transfers between devices, swap(): lax.ppermute(value, axis, [(place, place ^ bit) for place in range(size)])  192 us
    pallas_call x54, Pallas kernels, run(): pl.pallas_call(body if many else plain, out_shape=[pltpu.HBM(shape, kind)...  75.1 us
    ppermute x72, starting transfers between devices, swap(): lax.ppermute(value, axis, [(place, place ^ bit) for place in range(size)])  63.5 us
    unnamed x68, local copies, waits for them, and re-layouts  18.1 us
  transfers between devices with their start and end apart: 72, of which 39 were waited for; matrix products, arithmetic and copies ran while one was open for 4% of the time, Pallas kernels for 13%

profile of v2, /device:TPU:0, one launch (start us, length us, event | category | flops | bytes accessed | tf_op | source)
XLA Modules:
  0.0 356.7 jit_solution(18427559056337654579)
XLA Ops:
  5.4 3.7 %collective-permute-start.2 = (bf16[1,128,768]{2,1,0:T(8,128)(2,1)S(1)}, bf16[1,128,768]{2,1,0:T(8,128)(2,1)S(1)}, u32[]{:S(2)}, u32[]{:S(2)}) collective-permute-start(bf16[1,128,768]{2,1,0:T(8,128)(2,1)S(1)} %maximum_bitcast_fusion.refs_1_), channel_id=1, source_target_pairs={{0,16},{4,20},{8,24},{12,28},{16,0},{20,4},{24,8},{28,12},{1,17},{... | collective-permute-start | bytes 589832 | tf_op jit(solution)/shard_map/ppermute | solution.py:845
  16.5 2.4 collective-permute-done.5.refs_1_
  19.4 2.2 collective-permute-start.6
  23.9 2.4 collective-permute-done.7.refs_1_
  28.2 2.9 collective-permute-done.8.refs_1_
  33.1 5.7 %shard_map.407 = (bf16[256,1024]{1,0:T(8,128)(2,1)S(1)}, bf16[256,1024]{1,0:T(8,128)(2,1)S(1)}, bf16[256,1024]{1,0:T(8,128)(2,1)S(1)}, bf16[256,1024]{1,0:T(8,12...) custom-call(s32[4]{0:T(128)S(1)} %pad_add_fusion.refs_0_, ...), custom_call_target="tpu_custom_call" | custom-call | flops 1 | bytes 1 | tf_op jit(solution)/shard_map/pallas_call | solution.py:824
  44.6 11.3 %collective-permute-done.12.refs_4_ = bf16[256,1024]{1,0:T(8,128)(2,1)S(1)} collective-permute-done((bf16[256,1024]{1,0:T(8,128)(2,1)S(1)}, bf16[256,1024]{1,0:T(8,128)(2,1)S(1)}, u32[]{:S(2)}, u32[]{:S(2)}) %collective-permute-start.12) | collective-permute-done | bytes 524320 | tf_op jit(solution)/shard_map/ppermute | solution.py:845
  57.1 5.2 %shard_map.408 = (f32[256,1024]{1,0:T(8,128)S(1)}, bf16[256,1024]{1,0:T(8,128)(2,1)S(1)}, bf16[256,256]{1,0:T(8,128)(2,1)S(1)}, bf16[256,256]{1,0:T(8,128)(2,1)S...) custom-call(s32[4]{0:T(128)S(1)} %pad_add_fusion.refs_0_, ...), custom_call_target="tpu_custom_call" | custom-call | flops 1 | bytes 1 | tf_op jit(solution)/shard_map/pallas_call | solution.py:824
  65.2 2.0 collective-permute-done.18.refs_4_
  68.0 10.0 %collective-permute-done.15.refs_2_ = bf16[256,1024]{1,0:T(8,128)(2,1)S(1)} collective-permute-done((bf16[256,1024]{1,0:T(8,128)(2,1)S(1)}, bf16[256,1024]{1,0:T(8,128)(2,1)S(1)}, u32[]{:S(2)}, u32[]{:S(2)}) %collective-permute-start.15) | collective-permute-done | bytes 524320 | tf_op jit(solution)/shard_map/ppermute | solution.py:845
  79.2 3.7 %shard_map.410 = (f32[256,1024]{1,0:T(8,128)S(1)}, bf16[256,1024]{1,0:T(8,128)(2,1)S(1)}, f32[256,512]{1,0:T(8,128)S(1)}, f32[256,512]{1,0:T(8,128)S(1)}, f32[27...) custom-call(s32[4]{0:T(128)S(1)} %pad_add_fusion.refs_0_, ...), custom_call_target="tpu_custom_call" | custom-call | flops 1 | bytes 1 | tf_op jit(solution)/shard_map/pallas_call | solution.py:824
  85.6 3.2 collective-permute-done.20.refs_1_
  88.8 2.6 collective-permute-start.21
  96.2 2.9 collective-permute-done.22.refs_1_
  99.1 2.4 shard_map.413
  104.2 10.1 %collective-permute-done.26.refs_1_ = bf16[256,1024]{1,0:T(8,128)(2,1)S(1)} collective-permute-done((bf16[256,1024]{1,0:T(8,128)(2,1)S(1)}, bf16[256,1024]{1,0:T(8,128)(2,1)S(1)}, u32[]{:S(2)}, u32[]{:S(2)}) %collective-permute-start.26) | collective-permute-done | bytes 524320 | tf_op jit(solution)/shard_map/ppermute | solution.py:845
  116.4 4.8 %shard_map.415 = (f32[256,1024]{1,0:T(8,128)S(1)}, bf16[256,1024]{1,0:T(8,128)(2,1)S(1)}, bf16[256,1024]{1,0:T(8,128)(2,1)S(1)}, bf16[256,1024]{1,0:T(8,128)(2,1...) custom-call(bf16[256,1024]{1,0:T(8,128)(2,1)S(1)} %get-tuple-element.313.refs_0_, ...), custom_call_target="tpu_custom_call" | custom-call | flops 1 | bytes 1 | tf_op jit(solution)/shard_map/pallas_call | solution.py:824
  122.5 2.3 collective-permute-done.34.refs_8_
  124.9 11.3 %collective-permute-done.30.refs_2_ = bf16[256,1024]{1,0:T(8,128)(2,1)S(1)} collective-permute-done((bf16[256,1024]{1,0:T(8,128)(2,1)S(1)}, bf16[256,1024]{1,0:T(8,128)(2,1)S(1)}, u32[]{:S(2)}, u32[]{:S(2)}) %collective-permute-start.30) | collective-permute-done | bytes 524320 | tf_op jit(solution)/shard_map/ppermute | solution.py:845
  136.1 6.5 %shard_map.416 = (bf16[64,1024]{1,0:T(8,128)(2,1)S(1)}, bf16[64,1024]{1,0:T(8,128)(2,1)S(1)}, f32[256,1024]{1,0:T(8,128)S(1)}, f32[1,1024]{1,0:T(1,128)S(1)}, bf...) custom-call(s32[4]{0:T(128)S(1)} %pad_add_fusion.refs_0_, ...), custom_call_target="tpu_custom_call" | custom-call | flops 1 | bytes 1 | tf_op jit(solution)/shard_map/pallas_call | solution.py:824
  144.6 1.9 shard_map.418
  146.5 1.9 shard_map.417
  148.5 8.6 %collective-permute-done.35.refs_1_ = bf16[256,1024]{1,0:T(8,128)(2,1)S(1)} collective-permute-done((bf16[256,1024]{1,0:T(8,128)(2,1)S(1)}, bf16[256,1024]{1,0:T(8,128)(2,1)S(1)}, u32[]{:S(2)}, u32[]{:S(2)}) %collective-permute-start.35) | collective-permute-done | bytes 524320 | tf_op jit(solution)/shard_map/ppermute | solution.py:845
  157.1 3.7 %shard_map.419 = (f32[256,1024]{1,0:T(8,128)S(1)}, f32[1,1024]{1,0:T(1,128)S(1)}, bf16[256,1024]{1,0:T(8,128)(2,1)S(1)}, f32[256,512]{1,0:T(8,128)S(1)}, f32[8,512]{1,0:T(8,128)S(1)}) custom-call(bf16[256,1024]{1,0:T(8,128)(2,1)S(1)} %get-tuple-element.335.refs_0_, bf16[256,1024]{1,0:T(8,128)(2,1)S(1)} %collective-permute-done.35.refs_1_, ...), custom_call_target="tpu_custom_call" | custom-call | flops 1 | bytes 1 | tf_op jit(solution)/shard_map/pallas_call | solution.py:824
  161.8 3.2 collective-permute-done.38.refs_1_
  165.1 2.0 collective-permute-start.39
  170.5 3.0 collective-permute-done.40.refs_2_
  174.0 2.0 collective-permute-start.46
  176.1 3.2 shard_map.423
  181.4 7.8 %collective-permute-done.43.refs_1_ = bf16[256,1024]{1,0:T(8,128)(2,1)S(1)} collective-permute-done((bf16[256,1024]{1,0:T(8,128)(2,1)S(1)}, bf16[256,1024]{1,0:T(8,128)(2,1)S(1)}, u32[]{:S(2)}, u32[]{:S(2)}) %collective-permute-start.43) | collective-permute-done | bytes 524320 | tf_op jit(solution)/shard_map/ppermute | solution.py:845
  189.2 5.5 %shard_map.424 = (f32[256,1024]{1,0:T(8,128)S(1)}, f32[1,1024]{1,0:T(1,128)S(1)}, bf16[256,1024]{1,0:T(8,128)(2,1)S(1)}, bf16[256,768]{1,0:T(8,128)(2,1)S(1)}, b...) custom-call(bf16[256,1024]{1,0:T(8,128)(2,1)S(1)} %get-tuple-element.363.refs_0_, ...), custom_call_target="tpu_custom_call" | custom-call | flops 1 | bytes 1 | tf_op jit(solution)/shard_map/pallas_call | solution.py:824
  197.3 3.1 shard_map.427
  202.4 13.2 %collective-permute-done.45.refs_2_ = bf16[256,1024]{1,0:T(8,128)(2,1)S(1)} collective-permute-done((bf16[256,1024]{1,0:T(8,128)(2,1)S(1)}, bf16[256,1024]{1,0:T(8,128)(2,1)S(1)}, u32[]{:S(2)}, u32[]{:S(2)}) %collective-permute-start.45) | collective-permute-done | bytes 524320 | tf_op jit(solution)/shard_map/ppermute | solution.py:845
  215.6 6.5 %shard_map.428 = (f32[256,1024]{1,0:T(8,128)S(1)}, f32[1,1024]{1,0:T(1,128)S(1)}, bf16[256,1024]{1,0:T(8,128)(2,1)S(1)}, bf16[256,1024]{1,0:T(8,128)(2,1)S(1)}, ...) custom-call(s32[4]{0:T(128)S(1)} %pad_add_fusion.refs_0_, ...), custom_call_target="tpu_custom_call" | custom-call | flops 1 | bytes 1 | tf_op jit(solution)/shard_map/pallas_call | solution.py:824
  228.6 1.9 shard_map.429
  232.2 11.1 %collective-permute-done.56 = bf16[4,128,1792]{2,1,0:T(8,128)(2,1)S(1)} collective-permute-done((bf16[4,128,1792]{2,1,0:T(8,128)(2,1)S(1)}, bf16[4,128,1792]{2,1,0:T(8,128)(2,1)S(1)}, u32[]{:S(2)}, u32[]{:S(2)}) %collective-permute-start.56) | collective-permute-done | bytes 1835040 | tf_op jit(solution)/shard_map/ppermute | solution.py:845
  245.7 6.8 %collective-permute-done.55 = bf16[2,128,1024]{2,1,0:T(8,128)(2,1)S(1)} collective-permute-done((bf16[2,128,1024]{2,1,0:T(8,128)(2,1)S(1)}, bf16[2,128,1024]{2,1,0:T(8,128)(2,1)S(1)}, u32[]{:S(2)}, u32[]{:S(2)}) %collective-permute-start.55) | collective-permute-done | bytes 524320 | tf_op jit(solution)/shard_map/ppermute | solution.py:845
  254.4 4.5 %collective-permute-done.57.refs_3_ = bf16[128,1024]{1,0:T(8,128)(2,1)S(1)} collective-permute-done((bf16[128,1024]{1,0:T(8,128)(2,1)S(1)}, bf16[128,1024]{1,0:T(8,128)(2,1)S(1)}, u32[]{:S(2)}, u32[]{:S(2)}) %collective-permute-start.57) | collective-permute-done | bytes 262176 | tf_op jit(solution)/shard_map/ppermute | solution.py:845
  258.9 2.4 shard_map.434
  261.3 4.4 %collective-permute-done.53 = bf16[4,128,1024]{2,1,0:T(8,128)(2,1)S(1)} collective-permute-done((bf16[4,128,1024]{2,1,0:T(8,128)(2,1)S(1)}, bf16[4,128,1024]{2,1,0:T(8,128)(2,1)S(1)}, u32[]{:S(2)}, u32[]{:S(2)}) %collective-permute-start.53) | collective-permute-done | bytes 1048608 | tf_op jit(solution)/shard_map/ppermute | solution.py:845
  269.9 16.0 %collective-permute-done.60 = bf16[1,128,1024]{2,1,0:T(8,128)(2,1)S(1)} collective-permute-done((bf16[1,128,1024]{2,1,0:T(8,128)(2,1)S(1)}, bf16[1,128,1024]{2,1,0:T(8,128)(2,1)S(1)}, u32[]{:S(2)}, u32[]{:S(2)}) %collective-permute-start.60) | collective-permute-done | bytes 262176 | tf_op jit(solution)/shard_map/ppermute | solution.py:845
  289.5 3.1 collective-permute-start.61
  294.2 2.9 collective-permute-start.68
  299.0 3.4 collective-permute-done.65.refs_1_
  302.9 19.5 %collective-permute-done.63 = bf16[1,128,1792]{2,1,0:T(8,128)(2,1)S(1)} collective-permute-done((bf16[1,128,1792]{2,1,0:T(8,128)(2,1)S(1)}, bf16[1,128,1792]{2,1,0:T(8,128)(2,1)S(1)}, u32[]{:S(2)}, u32[]{:S(2)}) %collective-permute-start.63) | collective-permute-done | bytes 458784 | tf_op jit(solution)/shard_map/ppermute | solution.py:845
  326.5 4.0 %collective-permute-done.70.refs_1_ = f32[8,1280]{1,0:T(8,128)S(1)} collective-permute-done((f32[8,1280]{1,0:T(8,128)S(1)}, f32[8,1280]{1,0:T(8,128)S(1)}, u32[]{:S(2)}, u32[]{:S(2)}) %collective-permute-start.70) | collective-permute-done | bytes 40992 | tf_op jit(solution)/shard_map/ppermute | solution.py:845
  338.3 2.9 collective-permute-start.66
  344.3 9.5 %collective-permute-done.66 = bf16[1,128,1024]{2,1,0:T(8,128)(2,1)S(1)} collective-permute-done((bf16[1,128,1024]{2,1,0:T(8,128)(2,1)S(1)}, bf16[1,128,1024]{2,1,0:T(8,128)(2,1)S(1)}, u32[]{:S(2)}, u32[]{:S(2)}) %collective-permute-start.66) | collective-permute-done | bytes 262176 | tf_op jit(solution)/shard_map/ppermute | solution.py:845
  (240 shorter events, 98.1 us)
Async XLA Ops:
  0.7 31.1 %collective-permute-start.9 = (bf16[1024,1024]{1,0:T(8,128)(2,1)}, bf16[1024,1024]{1,0:T(8,128)(2,1)S(1)}, u32[]{:S(2)}, u32[]{:S(2)}) collective-permute-start(bf16[1024,1024]{1,0:T(8,128)(2,1)} %refs_7_.1), channel_id=1, source_target_pairs={{0,1},{1,0},{2,3},{3,2},{4,5},{5,4},{6,7},{7,6},{8,9},{9,8},{10,11... | collective-permute-start | bytes 6291464 | tf_op jit(solution)/shard_map/ppermute | solution.py:845
  1.2 30.6 %collective-permute-start.10 = (bf16[1024,1024]{1,0:T(8,128)(2,1)}, bf16[1024,1024]{1,0:T(8,128)(2,1)}, u32[]{:S(2)}, u32[]{:S(2)}) collective-permute-start(bf16[1024,1024]{1,0:T(8,128)(2,1)} %refs_9_.3), channel_id=1, source_target_pairs={{0,1},{1,0},{2,3},{3,2},{4,5},{5,4},{6,7},{7,6},{8,9},{9,8},{10,11... | collective-permute-start | bytes 6291464 | tf_op jit(solution)/shard_map/ppermute | solution.py:845
  2.9 7.6 %collective-permute-start.3 = (f32[8,1024]{1,0:T(8,128)S(1)}, f32[8,1024]{1,0:T(8,128)S(1)}, u32[]{:S(2)}, u32[]{:S(2)}) collective-permute-start(f32[8,1024]{1,0:T(8,128)S(1)} %dynamic_update_slice.3.refs_0_), channel_id=1, source_target_pairs={{0,1},{1,0},{2,3},{3,2},{4,5},{5,4},{6,7},{7,6},{8,9},{9,8},{10,11... | collective-permute-start | bytes 98312 | tf_op jit(solution)/shard_map/ppermute | solution.py:845
  5.4 13.5 %collective-permute-start.2 = (bf16[1,128,768]{2,1,0:T(8,128)(2,1)S(1)}, bf16[1,128,768]{2,1,0:T(8,128)(2,1)S(1)}, u32[]{:S(2)}, u32[]{:S(2)}) collective-permute-start(bf16[1,128,768]{2,1,0:T(8,128)(2,1)S(1)} %maximum_bitcast_fusion.refs_1_), channel_id=1, source_target_pairs={{0,16},{4,20},{8,24},{12,28},{16,0},{20,4},{24,8},{28,12},{1,17},{... | collective-permute-start | bytes 589832 | tf_op jit(solution)/shard_map/ppermute | solution.py:845
  9.1 12.6 %collective-permute-start = (bf16[2,64,1024]{2,1,0:T(8,128)(2,1)}, bf16[2,64,1024]{2,1,0:T(8,128)(2,1)S(1)}, u32[]{:S(2)}, u32[]{:S(2)}) collective-permute-start(bf16[2,64,1024]{2,1,0:T(8,128)(2,1)} %refs_2_.1), channel_id=1, source_target_pairs={{0,2},{1,3},{2,0},{3,1},{4,6},{5,7},{6,4},{7,5},{8,10},{9,11},{10,... | collective-permute-start | bytes 786440 | tf_op jit(solution)/shard_map/ppermute | solution.py:845
  19.4 11.7 %collective-permute-start.6 = (bf16[2,128,768]{2,1,0:T(8,128)(2,1)S(1)}, bf16[2,128,768]{2,1,0:T(8,128)(2,1)S(1)}, u32[]{:S(2)}, u32[]{:S(2)}) collective-permute-start(bf16[2,128,768]{2,1,0:T(8,128)(2,1)S(1)} %bitcast.87), channel_id=1, source_target_pairs={{0,8},{4,12},{8,0},{12,4},{16,24},{20,28},{24,16},{28,20},{1,9},{5... | collective-permute-start | bytes 1179656 | tf_op jit(solution)/shard_map/ppermute | solution.py:845
  22.2 9.5 %collective-permute-start.1 = (bf16[2,64,1024]{2,1,0:T(8,128)(2,1)S(1)}, bf16[2,64,1024]{2,1,0:T(8,128)(2,1)S(1)}, u32[]{:S(2)}, u32[]{:S(2)}) collective-permute-start(bf16[2,64,1024]{2,1,0:T(8,128)(2,1)S(1)} %shard_map.399), channel_id=1, source_target_pairs={{0,1},{1,0},{2,3},{3,2},{4,5},{5,4},{6,7},{7,6},{8,9},{9,8},{10,11... | collective-permute-start | bytes 786440 | tf_op jit(solution)/shard_map/ppermute | solution.py:845
  26.3 4.8 %collective-permute-start.8 = (f32[8,1024]{1,0:T(8,128)S(1)}, f32[8,1024]{1,0:T(8,128)S(1)}, u32[]{:S(2)}, u32[]{:S(2)}) collective-permute-start(f32[8,1024]{1,0:T(8,128)S(1)} %shard_map.404.refs_0_), channel_id=1, source_target_pairs={{0,16},{4,20},{8,24},{12,28},{16,0},{20,4},{24,8},{28,12},{1,17},{... | collective-permute-start | bytes 98312 | tf_op jit(solution)/shard_map/ppermute | solution.py:845
  39.9 16.0 %collective-permute-start.13 = (bf16[1024,768]{1,0:T(8,128)(2,1)S(1)}, bf16[1024,768]{1,0:T(8,128)(2,1)S(1)}, u32[]{:S(2)}, u32[]{:S(2)}) collective-permute-start(bf16[1024,768]{1,0:T(8,128)(2,1)S(1)} %constant_dynamic-update-slice_fusion.refs_7_.refs_8_), channel_id=1, source_target_pairs={{0,1},{1,0},{2,3},{3,2},{4,5},{5,4},{6,7},{7,6},{8,9},{9,8},{10,11... | collective-permute-start | bytes 4718600 | tf_op jit(solution)/shard_map/ppermute | solution.py:845
  40.0 22.4 %collective-permute-start.16 = (bf16[4,128,768]{2,1,0:T(8,128)(2,1)S(1)}, bf16[4,128,768]{2,1,0:T(8,128)(2,1)S(1)}, u32[]{:S(2)}, u32[]{:S(2)}) collective-permute-start(bf16[4,128,768]{2,1,0:T(8,128)(2,1)S(1)} %bitcast.79), channel_id=1, source_target_pairs={{0,4},{4,0},{8,12},{12,8},{16,20},{20,16},{24,28},{28,24},{1,5},{5... | collective-permute-start | bytes 2359304 | tf_op jit(solution)/shard_map/ppermute | solution.py:845
  41.7 14.2 %collective-permute-start.12 = (bf16[256,1024]{1,0:T(8,128)(2,1)S(1)}, bf16[256,1024]{1,0:T(8,128)(2,1)S(1)}, u32[]{:S(2)}, u32[]{:S(2)}) collective-permute-start(bf16[256,1024]{1,0:T(8,128)(2,1)S(1)} %get-tuple-element.287.refs_3_), channel_id=1, source_target_pairs={{0,2},{1,3},{2,0},{3,1},{4,6},{5,7},{6,4},{7,5},{8,10},{9,11},{10,... | collective-permute-start | bytes 1572872 | tf_op jit(solution)/shard_map/ppermute | solution.py:845
  63.1 14.9 %collective-permute-start.19 = (bf16[1024,768]{1,0:T(8,128)(2,1)S(1)}, bf16[1024,768]{1,0:T(8,128)(2,1)S(1)}, u32[]{:S(2)}, u32[]{:S(2)}) collective-permute-start(bf16[1024,768]{1,0:T(8,128)(2,1)S(1)} %bitcast.73), channel_id=1, source_target_pairs={{0,1},{1,0},{2,3},{3,2},{4,5},{5,4},{6,7},{7,6},{8,9},{9,8},{10,11... | collective-permute-start | bytes 4718600 | tf_op jit(solution)/shard_map/ppermute | solution.py:845
  63.6 4.4 %collective-permute-start.17 = (bf16[256,1024]{1,0:T(8,128)(2,1)S(1)}, bf16[256,1024]{1,0:T(8,128)(2,1)S(1)}, u32[]{:S(2)}, u32[]{:S(2)}) collective-permute-start(bf16[256,1024]{1,0:T(8,128)(2,1)S(1)} %get-tuple-element.299.refs_1_), channel_id=1, source_target_pairs={{0,1},{1,0},{2,3},{3,2},{4,5},{5,4},{6,7},{7,6},{8,9},{9,8},{10,11... | collective-permute-start | bytes 1572872 | tf_op jit(solution)/shard_map/ppermute | solution.py:845
  63.7 14.3 %collective-permute-start.15 = (bf16[256,1024]{1,0:T(8,128)(2,1)S(1)}, bf16[256,1024]{1,0:T(8,128)(2,1)S(1)}, u32[]{:S(2)}, u32[]{:S(2)}) collective-permute-start(bf16[256,1024]{1,0:T(8,128)(2,1)S(1)} %get-tuple-element.293.refs_1_), channel_id=1, source_target_pairs={{0,2},{1,3},{2,0},{3,1},{4,6},{5,7},{6,4},{7,5},{8,10},{9,11},{10,... | collective-permute-start | bytes 1572872 | tf_op jit(solution)/shard_map/ppermute | solution.py:845
  82.9 31.5 %collective-permute-start.28 = (bf16[1024,1024]{1,0:T(8,128)(2,1)S(1)}, bf16[1024,1024]{1,0:T(8,128)(2,1)S(1)}, u32[]{:S(2)}, u32[]{:S(2)}) collective-permute-start(bf16[1024,1024]{1,0:T(8,128)(2,1)S(1)} %copy-done.10), channel_id=1, source_target_pairs={{0,1},{1,0},{2,3},{3,2},{4,5},{5,4},{6,7},{7,6},{8,9},{9,8},{10,11... | collective-permute-start | bytes 6291464 | tf_op jit(solution)/shard_map/ppermute | solution.py:845
  83.0 31.4 %collective-permute-start.29 = (bf16[1024,1024]{1,0:T(8,128)(2,1)S(1)}, bf16[1024,1024]{1,0:T(8,128)(2,1)S(1)}, u32[]{:S(2)}, u32[]{:S(2)}) collective-permute-start(bf16[1024,1024]{1,0:T(8,128)(2,1)S(1)} %copy-done.11), channel_id=1, source_target_pairs={{0,1},{1,0},{2,3},{3,2},{4,5},{5,4},{6,7},{7,6},{8,9},{9,8},{10,11... | collective-permute-start | bytes 6291464 | tf_op jit(solution)/shard_map/ppermute | solution.py:845
  83.5 12.7 %collective-permute-start.23 = (bf16[256,1024]{1,0:T(8,128)(2,1)S(1)}, bf16[256,1024]{1,0:T(8,128)(2,1)S(1)}, u32[]{:S(2)}, u32[]{:S(2)}) collective-permute-start(bf16[256,1024]{1,0:T(8,128)(2,1)S(1)} %get-tuple-element.308.refs_9_), channel_id=1, source_target_pairs={{0,1},{1,0},{2,3},{3,2},{4,5},{5,4},{6,7},{7,6},{8,9},{9,8},{10,11... | collective-permute-start | bytes 1572872 | tf_op jit(solution)/shard_map/ppermute | solution.py:845
  83.6 12.6 %collective-permute-start.25 = (bf16[2,64,1024]{2,1,0:T(8,128)(2,1)S(1)}, bf16[2,64,1024]{2,1,0:T(8,128)(2,1)S(1)}, u32[]{:S(2)}, u32[]{:S(2)}) collective-permute-start(bf16[2,64,1024]{2,1,0:T(8,128)(2,1)S(1)} %copy-done.2), channel_id=1, source_target_pairs={{0,2},{1,3},{2,0},{3,1},{4,6},{5,7},{6,4},{7,5},{8,10},{9,11},{10,... | collective-permute-start | bytes 786440 | tf_op jit(solution)/shard_map/ppermute | solution.py:845
  88.8 4.3 %collective-permute-start.21 = (f32[8,512]{1,0:T(8,128)S(1)}, f32[8,512]{1,0:T(8,128)S(1)}, u32[]{:S(2)}, u32[]{:S(2)}) collective-permute-start(f32[8,512]{1,0:T(8,128)S(1)} %shard_map.411.refs_0_), channel_id=1, source_target_pairs={{0,8},{4,12},{8,0},{12,4},{16,24},{20,28},{24,16},{28,20},{1,9},{5... | collective-permute-start | bytes 49160 | tf_op jit(solution)/shard_map/ppermute | solution.py:845
  94.5 4.6 %collective-permute-start.22 = (f32[8,512]{1,0:T(8,128)S(1)}, f32[8,512]{1,0:T(8,128)S(1)}, u32[]{:S(2)}, u32[]{:S(2)}) collective-permute-start(f32[8,512]{1,0:T(8,128)S(1)} %shard_map.412.refs_0_), channel_id=1, source_target_pairs={{0,16},{4,20},{8,24},{12,28},{16,0},{20,4},{24,8},{28,12},{1,17},{... | collective-permute-start | bytes 49160 | tf_op jit(solution)/shard_map/ppermute | solution.py:845
  101.5 12.9 %collective-permute-start.26 = (bf16[256,1024]{1,0:T(8,128)(2,1)S(1)}, bf16[256,1024]{1,0:T(8,128)(2,1)S(1)}, u32[]{:S(2)}, u32[]{:S(2)}) collective-permute-start(bf16[256,1024]{1,0:T(8,128)(2,1)S(1)} %get-tuple-element.313.refs_0_), channel_id=1, source_target_pairs={{0,2},{1,3},{2,0},{3,1},{4,6},{5,7},{6,4},{7,5},{8,10},{9,11},{10,... | collective-permute-start | bytes 1572872 | tf_op jit(solution)/shard_map/ppermute | solution.py:845
  121.8 14.3 %collective-permute-start.30 = (bf16[256,1024]{1,0:T(8,128)(2,1)S(1)}, bf16[256,1024]{1,0:T(8,128)(2,1)S(1)}, u32[]{:S(2)}, u32[]{:S(2)}) collective-permute-start(bf16[256,1024]{1,0:T(8,128)(2,1)S(1)} %get-tuple-element.321.refs_1_), channel_id=1, source_target_pairs={{0,2},{1,3},{2,0},{3,1},{4,6},{5,7},{6,4},{7,5},{8,10},{9,11},{10,... | collective-permute-start | bytes 1572872 | tf_op jit(solution)/shard_map/ppermute | solution.py:845
  143.2 13.9 %collective-permute-start.35 = (bf16[256,1024]{1,0:T(8,128)(2,1)S(1)}, bf16[256,1024]{1,0:T(8,128)(2,1)S(1)}, u32[]{:S(2)}, u32[]{:S(2)}) collective-permute-start(bf16[256,1024]{1,0:T(8,128)(2,1)S(1)} %get-tuple-element.335.refs_0_), channel_id=1, source_target_pairs={{0,2},{1,3},{2,0},{3,1},{4,6},{5,7},{6,4},{7,5},{8,10},{9,11},{10,... | collective-permute-start | bytes 1572872 | tf_op jit(solution)/shard_map/ppermute | solution.py:845
  160.8 12.8 %collective-permute-start.42 = (bf16[256,1024]{1,0:T(8,128)(2,1)S(1)}, bf16[256,1024]{1,0:T(8,128)(2,1)S(1)}, u32[]{:S(2)}, u32[]{:S(2)}) collective-permute-start(bf16[256,1024]{1,0:T(8,128)(2,1)S(1)} %get-tuple-element.352.refs_10_.refs_5_), channel_id=1, source_target_pairs={{0,1},{1,0},{2,3},{3,2},{4,5},{5,4},{6,7},{7,6},{8,9},{9,8},{10,11... | collective-permute-start | bytes 1572872 | tf_op jit(solution)/shard_map/ppermute | solution.py:845
  160.8 12.7 %collective-permute-start.41 = (bf16[64,1024]{1,0:T(8,128)(2,1)S(1)}, bf16[64,1024]{1,0:T(8,128)(2,1)S(1)}, u32[]{:S(2)}, u32[]{:S(2)}) collective-permute-start(bf16[64,1024]{1,0:T(8,128)(2,1)S(1)} %get-tuple-element.351), channel_id=1, source_target_pairs={{0,1},{1,0},{2,3},{3,2},{4,5},{5,4},{6,7},{7,6},{8,9},{9,8},{10,11... | collective-permute-start | bytes 393224 | tf_op jit(solution)/shard_map/ppermute | solution.py:845
  168.8 4.7 %collective-permute-start.40 = (f32[8,512]{1,0:T(8,128)S(1)}, f32[8,512]{1,0:T(8,128)S(1)}, u32[]{:S(2)}, u32[]{:S(2)}) collective-permute-start(f32[8,512]{1,0:T(8,128)S(1)} %shard_map.421.refs_1_), channel_id=1, source_target_pairs={{0,16},{4,20},{8,24},{12,28},{16,0},{20,4},{24,8},{28,12},{1,17},{... | collective-permute-start | bytes 49160 | tf_op jit(solution)/shard_map/ppermute | solution.py:845
  173.6 21.9 %collective-permute-start.47 = (bf16[4,128,1024]{2,1,0:T(8,128)(2,1)S(1)}, bf16[4,128,1024]{2,1,0:T(8,128)(2,1)S(1)}, u32[]{:S(2)}, u32[]{:S(2)}) collective-permute-start(bf16[4,128,1024]{2,1,0:T(8,128)(2,1)S(1)} %get-tuple-element.383), channel_id=1, source_target_pairs={{0,4},{4,0},{8,12},{12,8},{16,20},{20,16},{24,28},{28,24},{1,5},{5... | collective-permute-start | bytes 3145736 | tf_op jit(solution)/shard_map/ppermute | solution.py:845
  174.0 22.2 %collective-permute-start.46 = (bf16[4,128,1024]{2,1,0:T(8,128)(2,1)S(1)}, bf16[4,128,1024]{2,1,0:T(8,128)(2,1)S(1)}, u32[]{:S(2)}, u32[]{:S(2)}) collective-permute-start(bf16[4,128,1024]{2,1,0:T(8,128)(2,1)S(1)} %get-tuple-element.381), channel_id=1, source_target_pairs={{0,8},{4,12},{8,0},{12,4},{16,24},{20,28},{24,16},{28,20},{1,9},{5... | collective-permute-start | bytes 3145736 | tf_op jit(solution)/shard_map/ppermute | solution.py:845
  179.3 10.0 %collective-permute-start.43 = (bf16[256,1024]{1,0:T(8,128)(2,1)S(1)}, bf16[256,1024]{1,0:T(8,128)(2,1)S(1)}, u32[]{:S(2)}, u32[]{:S(2)}) collective-permute-start(bf16[256,1024]{1,0:T(8,128)(2,1)S(1)} %get-tuple-element.363.refs_0_), channel_id=1, source_target_pairs={{0,2},{1,3},{2,0},{3,1},{4,6},{5,7},{6,4},{7,5},{8,10},{9,11},{10,... | collective-permute-start | bytes 1572872 | tf_op jit(solution)/shard_map/ppermute | solution.py:845
  200.3 42.9 %collective-permute-start.56 = (bf16[4,128,1792]{2,1,0:T(8,128)(2,1)S(1)}, bf16[4,128,1792]{2,1,0:T(8,128)(2,1)S(1)}, u32[]{:S(2)}, u32[]{:S(2)}) collective-permute-start(bf16[4,128,1792]{2,1,0:T(8,128)(2,1)S(1)} %get-tuple-element.427), channel_id=1, source_target_pairs={{0,4},{4,0},{8,12},{12,8},{16,20},{20,16},{24,28},{28,24},{1,5},{5... | collective-permute-start | bytes 5505032 | tf_op jit(solution)/shard_map/ppermute | solution.py:845
  201.9 13.7 %collective-permute-start.45 = (bf16[256,1024]{1,0:T(8,128)(2,1)S(1)}, bf16[256,1024]{1,0:T(8,128)(2,1)S(1)}, u32[]{:S(2)}, u32[]{:S(2)}) collective-permute-start(bf16[256,1024]{1,0:T(8,128)(2,1)S(1)} %get-tuple-element.370.refs_1_), channel_id=1, source_target_pairs={{0,2},{1,3},{2,0},{3,1},{4,6},{5,7},{6,4},{7,5},{8,10},{9,11},{10,... | collective-permute-start | bytes 1572872 | tf_op jit(solution)/shard_map/ppermute | solution.py:845
  222.2 6.4 %collective-permute-start.50 = (bf16[256,1024]{1,0:T(8,128)(2,1)S(1)}, bf16[256,1024]{1,0:T(8,128)(2,1)S(1)}, u32[]{:S(2)}, u32[]{:S(2)}) collective-permute-start(bf16[256,1024]{1,0:T(8,128)(2,1)S(1)} %get-tuple-element.404.refs_1_), channel_id=1, source_target_pairs={{0,1},{1,0},{2,3},{3,2},{4,5},{5,4},{6,7},{7,6},{8,9},{9,8},{10,11... | collective-permute-start | bytes 1572872 | tf_op jit(solution)/shard_map/ppermute | solution.py:845
  226.1 39.7 %collective-permute-start.53 = (bf16[4,128,1024]{2,1,0:T(8,128)(2,1)S(1)}, bf16[4,128,1024]{2,1,0:T(8,128)(2,1)S(1)}, u32[]{:S(2)}, u32[]{:S(2)}) collective-permute-start(bf16[4,128,1024]{2,1,0:T(8,128)(2,1)S(1)} %get-tuple-element.421), channel_id=1, source_target_pairs={{0,4},{4,0},{8,12},{12,8},{16,20},{20,16},{24,28},{28,24},{1,5},{5... | collective-permute-start | bytes 3145736 | tf_op jit(solution)/shard_map/ppermute | solution.py:845
  226.6 25.9 %collective-permute-start.55 = (bf16[2,128,1024]{2,1,0:T(8,128)(2,1)S(1)}, bf16[2,128,1024]{2,1,0:T(8,128)(2,1)S(1)}, u32[]{:S(2)}, u32[]{:S(2)}) collective-permute-start(bf16[2,128,1024]{2,1,0:T(8,128)(2,1)S(1)} %get-tuple-element.425), channel_id=1, source_target_pairs={{0,8},{4,12},{8,0},{12,4},{16,24},{20,28},{24,16},{28,20},{1,9},{5... | collective-permute-start | bytes 1572872 | tf_op jit(solution)/shard_map/ppermute | solution.py:845
  226.9 26.8 %collective-permute-start.54 = (bf16[1,256,1024]{2,1,0:T(8,128)(2,1)S(1)}, bf16[1,256,1024]{2,1,0:T(8,128)(2,1)S(1)}, u32[]{:S(2)}, u32[]{:S(2)}) collective-permute-start(bf16[1,256,1024]{2,1,0:T(8,128)(2,1)S(1)} %get-tuple-element.423), channel_id=1, source_target_pairs={{0,16},{4,20},{8,24},{12,28},{16,0},{20,4},{24,8},{28,12},{1,17},{... | collective-permute-start | bytes 1572872 | tf_op jit(solution)/shard_map/ppermute | solution.py:845
  230.6 58.1 %collective-permute-start.52 = (bf16[4,128,1024]{2,1,0:T(8,128)(2,1)S(1)}, bf16[4,128,1024]{2,1,0:T(8,128)(2,1)S(1)}, u32[]{:S(2)}, u32[]{:S(2)}) collective-permute-start(bf16[4,128,1024]{2,1,0:T(8,128)(2,1)S(1)} %get-tuple-element.419), channel_id=1, source_target_pairs={{0,4},{4,0},{8,12},{12,8},{16,20},{20,16},{24,28},{28,24},{1,5},{5... | collective-permute-start | bytes 3145736 | tf_op jit(solution)/shard_map/ppermute | solution.py:845
  244.1 42.4 %collective-permute-start.59 = (bf16[2,128,1792]{2,1,0:T(8,128)(2,1)S(1)}, bf16[2,128,1792]{2,1,0:T(8,128)(2,1)S(1)}, u32[]{:S(2)}, u32[]{:S(2)}) collective-permute-start(bf16[2,128,1792]{2,1,0:T(8,128)(2,1)S(1)} %get-tuple-element.456), channel_id=1, source_target_pairs={{0,8},{4,12},{8,0},{12,4},{16,24},{20,28},{24,16},{28,20},{1,9},{5... | collective-permute-start | bytes 2752520 | tf_op jit(solution)/shard_map/ppermute | solution.py:845
  252.5 6.4 %collective-permute-start.57 = (bf16[128,1024]{1,0:T(8,128)(2,1)S(1)}, bf16[128,1024]{1,0:T(8,128)(2,1)S(1)}, u32[]{:S(2)}, u32[]{:S(2)}) collective-permute-start(bf16[128,1024]{1,0:T(8,128)(2,1)S(1)} %get-tuple-element.446), channel_id=1, source_target_pairs={{0,2},{1,3},{2,0},{3,1},{4,6},{5,7},{6,4},{7,5},{8,10},{9,11},{10,... | collective-permute-start | bytes 786440 | tf_op jit(solution)/shard_map/ppermute | solution.py:845
  266.5 21.5 %collective-permute-start.58 = (bf16[2,128,1024]{2,1,0:T(8,128)(2,1)S(1)}, bf16[2,128,1024]{2,1,0:T(8,128)(2,1)S(1)}, u32[]{:S(2)}, u32[]{:S(2)}) collective-permute-start(bf16[2,128,1024]{2,1,0:T(8,128)(2,1)S(1)} %get-tuple-element.454), channel_id=1, source_target_pairs={{0,8},{4,12},{8,0},{12,4},{16,24},{20,28},{24,16},{28,20},{1,9},{5... | collective-permute-start | bytes 1572872 | tf_op jit(solution)/shard_map/ppermute | solution.py:845
  268.1 17.7 %collective-permute-start.60 = (bf16[1,128,1024]{2,1,0:T(8,128)(2,1)S(1)}, bf16[1,128,1024]{2,1,0:T(8,128)(2,1)S(1)}, u32[]{:S(2)}, u32[]{:S(2)}) collective-permute-start(bf16[1,128,1024]{2,1,0:T(8,128)(2,1)S(1)} %get-tuple-element.458), channel_id=1, source_target_pairs={{0,16},{4,20},{8,24},{12,28},{16,0},{20,4},{24,8},{28,12},{1,17},{... | collective-permute-start | bytes 786440 | tf_op jit(solution)/shard_map/ppermute | solution.py:845
  289.5 34.5 %collective-permute-start.61 = (bf16[2,128,1024]{2,1,0:T(8,128)(2,1)S(1)}, bf16[2,128,1024]{2,1,0:T(8,128)(2,1)S(1)}, u32[]{:S(2)}, u32[]{:S(2)}) collective-permute-start(bf16[2,128,1024]{2,1,0:T(8,128)(2,1)S(1)} %get-tuple-element.479), channel_id=1, source_target_pairs={{0,8},{4,12},{8,0},{12,4},{16,24},{20,28},{24,16},{28,20},{1,9},{5... | collective-permute-start | bytes 1572872 | tf_op jit(solution)/shard_map/ppermute | solution.py:845
  292.6 29.8 %collective-permute-start.63 = (bf16[1,128,1792]{2,1,0:T(8,128)(2,1)S(1)}, bf16[1,128,1792]{2,1,0:T(8,128)(2,1)S(1)}, u32[]{:S(2)}, u32[]{:S(2)}) collective-permute-start(bf16[1,128,1792]{2,1,0:T(8,128)(2,1)S(1)} %get-tuple-element.483), channel_id=1, source_target_pairs={{0,16},{4,20},{8,24},{12,28},{16,0},{20,4},{24,8},{28,12},{1,17},{... | collective-permute-start | bytes 1376264 | tf_op jit(solution)/shard_map/ppermute | solution.py:845
  292.6 30.6 %collective-permute-start.62 = (bf16[1,128,1024]{2,1,0:T(8,128)(2,1)S(1)}, bf16[1,128,1024]{2,1,0:T(8,128)(2,1)S(1)}, u32[]{:S(2)}, u32[]{:S(2)}) collective-permute-start(bf16[1,128,1024]{2,1,0:T(8,128)(2,1)S(1)} %get-tuple-element.481), channel_id=1, source_target_pairs={{0,4},{4,0},{8,12},{12,8},{16,20},{20,16},{24,28},{28,24},{1,5},{5... | collective-permute-start | bytes 786440 | tf_op jit(solution)/shard_map/ppermute | solution.py:845
  294.2 31.6 %collective-permute-start.68 = (bf16[1,128,1024]{2,1,0:T(8,128)(2,1)S(1)}, bf16[1,128,1024]{2,1,0:T(8,128)(2,1)S(1)}, u32[]{:S(2)}, u32[]{:S(2)}) collective-permute-start(bf16[1,128,1024]{2,1,0:T(8,128)(2,1)S(1)} %get-tuple-element.514), channel_id=1, source_target_pairs={{0,16},{4,20},{8,24},{12,28},{16,0},{20,4},{24,8},{28,12},{1,17},{... | collective-permute-start | bytes 786440 | tf_op jit(solution)/shard_map/ppermute | solution.py:845
  302.4 24.0 %collective-permute-start.67 = (f32[8,1280]{1,0:T(8,128)S(1)}, f32[8,1280]{1,0:T(8,128)S(1)}, u32[]{:S(2)}, u32[]{:S(2)}) collective-permute-start(f32[8,1280]{1,0:T(8,128)S(1)} %shard_map.443.refs_0_), channel_id=1, source_target_pairs={{0,4},{4,0},{8,12},{12,8},{16,20},{20,16},{24,28},{28,24},{1,5},{5... | collective-permute-start | bytes 122888 | tf_op jit(solution)/shard_map/ppermute | solution.py:845
  330.5 11.5 %collective-permute-start.71 = (f32[8,1280]{1,0:T(8,128)S(1)}, f32[8,1280]{1,0:T(8,128)S(1)}, u32[]{:S(2)}, u32[]{:S(2)}) collective-permute-start(f32[8,1280]{1,0:T(8,128)S(1)} %shard_map.451.refs_0_), channel_id=1, source_target_pairs={{0,16},{4,20},{8,24},{12,28},{16,0},{20,4},{24,8},{28,12},{1,17},{... | collective-permute-start | bytes 122888 | tf_op jit(solution)/shard_map/ppermute | solution.py:845
  332.7 21.8 %collective-permute-start.69 = (f32[64,1024]{1,0:T(8,128)}, f32[64,1024]{1,0:T(8,128)S(1)}, u32[]{:S(2)}, u32[]{:S(2)}) collective-permute-start(f32[64,1024]{1,0:T(8,128)} %copy-done.5), channel_id=1, source_target_pairs={{0,1},{1,0},{2,3},{3,2},{4,5},{5,4},{6,7},{7,6},{8,9},{9,8},{10,11... | collective-permute-start | bytes 786440 | tf_op jit(solution)/shard_map/ppermute | solution.py:845
  338.3 15.5 %collective-permute-start.66 = (bf16[1,128,1024]{2,1,0:T(8,128)(2,1)S(1)}, bf16[1,128,1024]{2,1,0:T(8,128)(2,1)S(1)}, u32[]{:S(2)}, u32[]{:S(2)}) collective-permute-start(bf16[1,128,1024]{2,1,0:T(8,128)(2,1)S(1)} %copy-done.7), channel_id=1, source_target_pairs={{0,16},{4,20},{8,24},{12,28},{16,0},{20,4},{24,8},{28,12},{1,17},{... | collective-permute-start | bytes 786440 | tf_op jit(solution)/shard_map/ppermute | solution.py:845
  (50 other events, 260.2 us)

commit v3 on v2

--- a/solution.py
+++ b/solution.py
@@ -896,7 +896,7 @@
     def here(self, chain):
         (self.arrived[-1],) = chain.after(self.arrived[-1])
 
-    def fold(self, chain, cuts=1):
+    def fold(self, chain, cuts=1, cost=1):
         bit = self.order[0]
         place = self.left.index(bit)
         inner = self.block << (len(self.left) - 1 - place)
@@ -907,12 +907,13 @@
             [((outer, inner, self.total), F32)] + [((outer, inner, self.total // cuts), BF)] * cuts,
             [self.info, kept.reshape(outer, 2, inner, self.total)]
             + [entry.reshape(outer, 2, inner, -1) for entry in arrived],
+            cost=cost,
         )
         self.kept, chain.last = tie(self.kept, chain.last)
         self.begin()
 
-    def step(self, chain):
-        self.fold(chain)
+    def step(self, chain, cost=1):
+        self.fold(chain, cost=cost)
         self.send()
 
     def finish(self, chain, *results):
@@ -1017,17 +1018,13 @@
     info = jnp.stack([core, high, own_length, group]).astype(jnp.int32)
     starts = jnp.where(on_first, span_starts[0:1], span_starts[1:2])
 
-    def gather_rows(block):
-        across_block = across(block)
-        (sent,) = run(k_pick, [(block.shape, BF)], [info, block, across_block])
-        return [block, across_block, beside(sent)]
-
+    frames_across = across(frames)
     conv_block = jnp.concatenate(
         [conv_up.reshape(conv_up.shape[0], 2 * channels), conv_down.T], axis=1
     )
     conv_weights = Gather(info, conv_block)
     conv_weights.send()
-    frame_parts = gather_rows(frames)
+
     part = mask_vector.shape[0]
     place = (group * lax.axis_size("tensor") + lax.axis_index("tensor")) * part
     vectors = jnp.stack(
@@ -1041,7 +1038,17 @@
         hops.append(("dp", bit))
         bit *= 2
     for step, (axis, bit) in enumerate(hops):
+        if step == 4:
+            (sent,) = run(k_pick, [(frames.shape, BF)], [info, frames, frames_across])
+            sent, small = tie(sent, small)
         if step == 3:
+            query_weight, key_weight, conv_depth, rel_slope, small = tie(
+                query_weight, key_weight, conv_depth, rel_slope, small
+            )
+            own_qkv = jnp.concatenate([query_weight, key_weight, value_weight], axis=1)
+            slope_row = jnp.pad(rel_slope[None], ((0, 0), (0, channels - heads)))
+            own_params = jnp.concatenate([conv_depth, bn_scale[None], bn_shift[None], slope_row])
+            other_params = beside(own_params)
             conv_weights.arrived, small = tie(conv_weights.arrived, small)
             conv_weights.take()
             if conv_weights.bit:
@@ -1053,7 +1060,12 @@
     if conv_weights.bit:
         conv_weights.arrived, small = tie(conv_weights.arrived, small)
         conv_weights.take()
-    conv_weights.held, small = tie(conv_weights.held, small)
+    frame_parts = [frames, frames_across, beside(sent)]
+    own_qkv, other_params, conv_weights.held, small = tie(
+        own_qkv, other_params, conv_weights.held, small
+    )
+    params = jnp.concatenate([own_params, other_params], axis=1)
+    slopes = jnp.concatenate([rel_slope, other_params[KW + 2, :heads]])
     if conv_weights.bit:
         conv_weights.send()
     up_one, down_one = beside(ffn1_up), beside(ffn1_down)
@@ -1070,18 +1082,10 @@
         k_ffn_one,
         [(wide, BF)] + ffn_outs,
         [info, starts, *frame_parts, small, ffn1_up, up_one, ffn1_down, down_one],
-        scratch=[(wide, BF)], late=(6, 7, 8, 9),
-    )
-    query_weight, key_weight, value_weight, output_weight, rel_slope, active_one = tie(
-        query_weight, key_weight, value_weight, output_weight, rel_slope, active_one
-    )
-    own_qkv = jnp.concatenate([query_weight, key_weight, value_weight], axis=1)
+        scratch=[(wide, BF)], late=(6, 8),
+    )
+    output_weight, active_one = tie(output_weight, active_one)
     other_qkv, other_out = beside(own_qkv), beside(output_weight)
-    slope_row = jnp.pad(rel_slope[None], ((0, 0), (0, channels - heads)))
-    own_params = jnp.concatenate([conv_depth, bn_scale[None], bn_shift[None], slope_row])
-    other_params = beside(own_params)
-    params = jnp.concatenate([own_params, other_params], axis=1)
-    slopes = jnp.concatenate([rel_slope, other_params[KW + 2, :heads]])
     stream_one, norm_attn, context_cross, context_own, qkv, weights, partial = run(
         k_attn_wrapped,
         [
@@ -1095,7 +1099,7 @@
         ],
         [info, slopes, starts, partial, across(partial), whole, small, own_qkv, other_qkv,
          output_weight, other_out],
-        scalars=2, late=(7, 8, 9, 10),
+        scalars=2, late=(7, 9),
     )
     conv_weights.arrived, norm_one, cross_one, context_own = tie(
         conv_weights.arrived, norm_one, cross_one, context_own
@@ -1119,7 +1123,7 @@
             stat_shape,
         ],
         [info, partial, across(partial), stream_one, small, params, own_conv, other_conv],
-        late=(6, 7),
+        late=(6,),
     )
     norm_attn, context_cross, cotangent, ffn2_up, ffn2_down, value = tie(
         norm_attn, context_cross, cotangent, ffn2_up, ffn2_down, value
@@ -1135,7 +1139,7 @@
         k_conv_rear,
         [stat_shape, ((length, channels), BF), ((length, channels), BF), (wide, BF)],
         [stats, stats_too, convolved, params, norm_conv, own_conv, other_conv],
-        scalars=0, late=(5, 6),
+        scalars=0, late=(5,),
     )
     grad_across, active_conv = tie(grad_across, active_conv)
     (sent,) = run(k_pick, [(cotangent.shape, BF)], [info, cotangent, grad_across])
@@ -1145,7 +1149,7 @@
         k_ffn_two,
         [(wide, F32)] + ffn_outs,
         [partial, across(partial), stream_two, small, ffn2_up, up_two, ffn2_down, down_two],
-        scalars=0, late=(4, 5, 6, 7),
+        scalars=0, late=(4, 6),
     )
     norm_two, cross_two, norm_conv, cross_conv, active_two = tie(
         norm_two, cross_two, norm_conv, cross_conv, active_two
@@ -1172,7 +1176,7 @@
         ],
         [info, partial, across(partial), stream_three, small, *grad_parts, hidden_two,
          ffn2_up, up_two, ffn2_down, down_two],
-        scratch=[(wide, BF), (wide, BF)], late=(9, 10, 11, 12),
+        scratch=[(wide, BF), (wide, BF)], late=(9, 11),
     )
     back_two_too, hid_cross_two_too = beside(back_two), beside(hid_cross_two)
     ffn_pair = ((0, 1, 2, 0, 3, 0, hidden_width),)
@@ -1190,7 +1194,7 @@
         [(wide, F32), row_shape, (wide, BF), (both_channels, F32), stat_shape],
         [partial, across(partial), stream_three, small, grad_four, convolved, stats, params,
          own_conv, other_conv],
-        scalars=0, late=(8, 9),
+        scalars=0, late=(8,),
     )
     out_sent, sum_two, back_conv = tie(out_sent, sum_two, back_conv)
     out_other, back_conv_too = beside(out_sent), beside(back_conv)
@@ -1210,7 +1214,7 @@
         ],
         [info, sums, sums_too, grad_shaped, convolved, stats, params, padded, value, gate,
          back_conv, own_conv, other_conv],
-        scratch=[((length + 2 * EDGE, 2 * channels), F32)], late=(11, 12),
+        scratch=[((length + 2 * EDGE, 2 * channels), F32)], late=(11,),
     )
     mixed_cross_too = beside(mixed_cross)
     mixed_cross_too, grad_three = tie(mixed_cross_too, grad_three)
@@ -1228,7 +1232,7 @@
         [partial, across(partial), stream_two, small, grad_three, small_sums, qkv, weights,
          own_qkv, other_qkv, output_weight, other_out],
         scalars=0,
-        scratch=[((length, 2 * third), BF)], late=(8, 9, 10, 11),
+        scratch=[((length, 2 * third), BF)], late=(8, 10),
     )
     back_attn_too, three_cross_too = beside(back_attn), beside(three_cross)
     chain = Chain(small_sums)
@@ -1265,9 +1269,13 @@
         ],
         [info, partial, across(partial), stream_one, small, grad_two, hidden_one,
          ffn1_up, up_one, ffn1_down, down_one],
-        scratch=[(wide, F32)], late=(7, 8, 9, 10),
+        scratch=[(wide, F32)], late=(7, 9),
     )
     back_one_too, hid_cross_one_too = beside(back_one), beside(hid_cross_one)
+    chain = Chain(sum_attn)
+    for entry in (two_up, two_down):
+        entry.step(chain, cost=COST)
+    hid_one, active_one = chain.after(hid_one, active_one)
     one_up = RowSum(
         info, [norm_one, norm_one_too, hid_one, hid_cross_one_too], ffn_pair, width, (0, 1, 2),
         cost=COST,
@@ -1276,12 +1284,11 @@
         info, [back_one, back_one_too, active_one, cross_one_too], ffn_pair, width, (0, 1, 2),
         cost=COST,
     )
-    chain = Chain(sum_attn)
-    for entry in (one_up, one_down):
-        entry.send(chain)
-        entry.kept, chain.last = tie(entry.kept, chain.last)
-    for entry in (middle, two_up, two_down):
-        entry.step(chain)
+    one_up.send(chain)
+    one_up.kept, chain.last = tie(one_up.kept, chain.last)
+    one_down.send(chain)
+    one_down.kept, chain.last = tie(one_down.kept, chain.last)
+    block = width // lax.axis_size("dp")
     (starts,) = chain.after(starts)
     sum_attn = chain.last
     frames_own, frames_sent, last_sums = run(
@@ -1300,68 +1307,84 @@
         k_smalls_add, [((8, width + channels), F32)], [smalls, beside(smalls_sent)], scalars=0
     )
     gains, gains_too = smalls[:, :width], across(smalls[:, :width])
-    block = width // lax.axis_size("dp")
     (gains,) = run(
         k_gains, [(smalls.shape, F32)], [gains, gains_too, smalls[:, width:]], scalars=0
     )
-    chain = Chain(frames_own)
-    one_up.step(chain)
+
+    def in_order(own, other):
+        return run(k_in_order, [((2, *own.shape), own.dtype)], [info, own, other])[0]
+
+    chain = Chain(in_order(out_own, out_other))
+
+    def hop(value, bit):
+        (value,) = chain.after(value)
+        return value, swap(value, "dp", bit)
+
+    def add(value, other):
+        (total,) = run(k_add, [(value.shape, F32)], chain.after(value, other), scalars=0)
+        return total
+
+    first, *between = [1 << level for level in range(1, lax.axis_size("dp").bit_length() - 1)]
+    gains = add(*hop(gains, first))
+    gains, chain.last = tie(gains, chain.last)
     (two_up,) = two_up.finish(chain, ((block, hidden_width), False))
+    middle.step(chain)
+    for bit in between:
+        gains = add(*hop(gains, bit))
+    gains, chain.last = tie(gains, chain.last)
     middle.step(chain)
     one_up.step(chain)
     one_down.step(chain)
-    (gains,) = chain.after(gains)
-    gains_too = swap(gains, "dp", 1)
+    one_up.step(chain)
     conv_up_grad, conv_down_grad, query_grad, key_grad, value_grad, output_grad = middle.finish(
         chain,
         (conv_up.shape, False), ((channels, block), True),
         *[((block, third), False)] * 3, ((third, block), True),
     )
+    gains, gains_too = hop(gains, 1)
+    (one_up,) = one_up.finish(chain, ((block, hidden_width), False))
+    gains = add(gains, gains_too)
+    one_down.step(chain)
     (two_down,) = two_down.finish(chain, ((hidden_width, block), True))
-    one_down.step(chain)
-    (one_up,) = one_up.finish(chain, ((block, hidden_width), False))
-    gains, gains_too = chain.after(gains, gains_too)
-    (gains,) = run(k_add, [(gains.shape, F32)], [gains, gains_too], scalars=0)
-    bit = 2
-    while bit < lax.axis_size("dp"):
-        (gains,) = run(
-            k_add, [(gains.shape, F32)], [gains, swap(gains, "dp", bit)], scalars=0
-        )
-        bit *= 2
-    (one_down,) = one_down.finish(chain, ((hidden_width, block), True))
-    frames_own = chain.last
-
     channel_sums = gains[:, width:]
     scale_grad = channel_sums[KW + 1] * (1.0 / lax.axis_size("dp"))
     shift_grad = channel_sums[KW] * (1.0 / lax.axis_size("dp"))
     gains = lax.dynamic_slice_in_dim(gains, place, part, axis=1)
 
-    def in_order(own, other):
-        return run(k_in_order, [((2, *own.shape), own.dtype)], [info, own, other])[0]
+    frames_grad = in_order(frames_own, frames_other)
+    smallest = [
+        *(gains[index] for index in range(6)),
+        channel_sums[KW + 2, :heads],
+        channel_sums[:KW],
+        scale_grad,
+        shift_grad,
+    ]
+    frames_grad, *smallest = chain.after(frames_grad, *smallest)
+    (one_down,) = one_down.finish(chain, ((hidden_width, block), True))
 
     return (
-        in_order(out_own, out_other),
-        in_order(frames_own, frames_other),
-        gains[0],
-        gains[1],
+        chain.last,
+        frames_grad,
+        smallest[0],
+        smallest[1],
         one_up,
         one_down,
-        gains[2],
+        smallest[2],
         query_grad,
         key_grad,
         value_grad,
         output_grad,
-        channel_sums[KW + 2, :heads],
-        gains[3],
+        smallest[6],
+        smallest[3],
         conv_up_grad,
-        channel_sums[:KW],
-        scale_grad,
-        shift_grad,
+        smallest[7],
+        smallest[8],
+        smallest[9],
         conv_down_grad,
-        gains[4],
+        smallest[4],
         two_up,
         two_down,
-        gains[5],
+        smallest[5],
     )
 
 

time: 357 us -> 324 us (0.908)
  waiting for transfers between devices: 192 us -> 159 us
  local copies, waits for them, and re-layouts: 22.2 us -> 17 us
    ppermute x72, waiting for transfers between devices: 192 us -> 159 us  [swap(): lax.ppermute(value, axis, [(place, place ^ bit) for place in range(size)])]
    unnamed x68 -> x54, local copies, waits for them, and re-layouts: 18.1 us -> 12.3 us
  transfers between devices with their start and end apart: 72 -> 72, of which waited for: 39 -> 38; matrix products, arithmetic and copies ran while one was open for 4% -> 5% of each run, Pallas kernels for 13% -> 17%
where the time goes in v3:
time: 324 us; the launch traced here: 323 us
  waiting for transfers between devices  159 us (49%)
  Pallas kernels  77.4 us (24%)
  starting transfers between devices  65.1 us (20%)
  local copies, waits for them, and re-layouts  17 us (5%)
    ppermute x72, waiting for transfers between devices, swap(): lax.ppermute(value, axis, [(place, place ^ bit) for place in range(size)])  159 us
    pallas_call x54, Pallas kernels, run(): pl.pallas_call(body if many else plain, out_shape=[pltpu.HBM(shape, kind)...  77.4 us
    ppermute x72, starting transfers between devices, swap(): lax.ppermute(value, axis, [(place, place ^ bit) for place in range(size)])  65.1 us
    unnamed x54, local copies, waits for them, and re-layouts  12.3 us
  transfers between devices with their start and end apart: 72, of which 38 were waited for; matrix products, arithmetic and copies ran while one was open for 5% of the time, Pallas kernels for 17%

profile of v3, /device:TPU:0, one launch (start us, length us, event | category | flops | bytes accessed | tf_op | source)
XLA Modules:
  0.0 323.2 jit_solution(912025241519745962)
XLA Ops:
  5.4 3.7 %collective-permute-start.4 = (bf16[1,128,768]{2,1,0:T(8,128)(2,1)S(1)}, bf16[1,128,768]{2,1,0:T(8,128)(2,1)S(1)}, u32[]{:S(2)}, u32[]{:S(2)}) collective-permute-start(bf16[1,128,768]{2,1,0:T(8,128)(2,1)S(1)} %maximum_bitcast_fusion.refs_1_), channel_id=1, source_target_pairs={{0,16},{4,20},{8,24},{12,28},{16,0},{20,4},{24,8},{28,12},{1,17},{... | collective-permute-start | bytes 589832 | tf_op jit(solution)/shard_map/ppermute | solution.py:845
  16.5 2.4 collective-permute-done.2.refs_1_
  19.5 2.2 collective-permute-start.5
  26.8 2.0 collective-permute-start.8
  28.9 2.8 collective-permute-done.8.refs_1_
  36.2 6.6 %shard_map.407 = (bf16[256,1024]{1,0:T(8,128)(2,1)S(1)}, bf16[256,1024]{1,0:T(8,128)(2,1)S(1)}, bf16[256,1024]{1,0:T(8,128)(2,1)S(1)}, bf16[256,1024]{1,0:T(8,12...) custom-call(s32[4]{0:T(128)S(1)} %pad_add_fusion.refs_0_, ...), custom_call_target="tpu_custom_call" | custom-call | flops 1 | bytes 1 | tf_op jit(solution)/shard_map/pallas_call | solution.py:824
  44.8 12.4 %collective-permute-done.12.refs_4_ = bf16[256,1024]{1,0:T(8,128)(2,1)S(1)} collective-permute-done((bf16[256,1024]{1,0:T(8,128)(2,1)S(1)}, bf16[256,1024]{1,0:T(8,128)(2,1)S(1)}, u32[]{:S(2)}, u32[]{:S(2)}) %collective-permute-start.12) | collective-permute-done | bytes 524320 | tf_op jit(solution)/shard_map/ppermute | solution.py:845
  57.2 5.1 %shard_map.408 = (f32[256,1024]{1,0:T(8,128)S(1)}, bf16[256,1024]{1,0:T(8,128)(2,1)S(1)}, bf16[256,256]{1,0:T(8,128)(2,1)S(1)}, bf16[256,256]{1,0:T(8,128)(2,1)S...) custom-call(s32[4]{0:T(128)S(1)} %pad_add_fusion.refs_0_, ...), custom_call_target="tpu_custom_call" | custom-call | flops 1 | bytes 1 | tf_op jit(solution)/shard_map/pallas_call | solution.py:824
  65.2 2.0 collective-permute-done.18.refs_4_
  68.0 10.0 %collective-permute-done.15.refs_2_ = bf16[256,1024]{1,0:T(8,128)(2,1)S(1)} collective-permute-done((bf16[256,1024]{1,0:T(8,128)(2,1)S(1)}, bf16[256,1024]{1,0:T(8,128)(2,1)S(1)}, u32[]{:S(2)}, u32[]{:S(2)}) %collective-permute-start.15) | collective-permute-done | bytes 524320 | tf_op jit(solution)/shard_map/ppermute | solution.py:845
  78.0 3.5 %shard_map.410 = (f32[256,1024]{1,0:T(8,128)S(1)}, bf16[256,1024]{1,0:T(8,128)(2,1)S(1)}, f32[256,512]{1,0:T(8,128)S(1)}, f32[256,512]{1,0:T(8,128)S(1)}, f32[27...) custom-call(s32[4]{0:T(128)S(1)} %pad_add_fusion.refs_0_, ...), custom_call_target="tpu_custom_call" | custom-call | flops 1 | bytes 1 | tf_op jit(solution)/shard_map/pallas_call | solution.py:824
  85.2 2.2 collective-permute-done.20.refs_1_
  87.4 1.9 collective-permute-start.21
  92.6 1.9 collective-permute-start.22
  94.5 2.7 collective-permute-done.22.refs_1_
  101.8 10.1 %collective-permute-done.26.refs_1_ = bf16[256,1024]{1,0:T(8,128)(2,1)S(1)} collective-permute-done((bf16[256,1024]{1,0:T(8,128)(2,1)S(1)}, bf16[256,1024]{1,0:T(8,128)(2,1)S(1)}, u32[]{:S(2)}, u32[]{:S(2)}) %collective-permute-start.26) | collective-permute-done | bytes 524320 | tf_op jit(solution)/shard_map/ppermute | solution.py:845
  112.0 4.4 %shard_map.415 = (f32[256,1024]{1,0:T(8,128)S(1)}, bf16[256,1024]{1,0:T(8,128)(2,1)S(1)}, bf16[256,1024]{1,0:T(8,128)(2,1)S(1)}, bf16[256,1024]{1,0:T(8,128)(2,1...) custom-call(bf16[256,1024]{1,0:T(8,128)(2,1)S(1)} %get-tuple-element.352.refs_0_, ...), custom_call_target="tpu_custom_call" | custom-call | flops 1 | bytes 1 | tf_op jit(solution)/shard_map/pallas_call | solution.py:824
  117.7 2.3 collective-permute-done.34.refs_8_
  120.0 11.3 %collective-permute-done.30.refs_2_ = bf16[256,1024]{1,0:T(8,128)(2,1)S(1)} collective-permute-done((bf16[256,1024]{1,0:T(8,128)(2,1)S(1)}, bf16[256,1024]{1,0:T(8,128)(2,1)S(1)}, u32[]{:S(2)}, u32[]{:S(2)}) %collective-permute-start.30) | collective-permute-done | bytes 524320 | tf_op jit(solution)/shard_map/ppermute | solution.py:845
  131.3 6.2 %shard_map.416 = (bf16[64,1024]{1,0:T(8,128)(2,1)S(1)}, bf16[64,1024]{1,0:T(8,128)(2,1)S(1)}, f32[256,1024]{1,0:T(8,128)S(1)}, f32[1,1024]{1,0:T(1,128)S(1)}, bf...) custom-call(s32[4]{0:T(128)S(1)} %pad_add_fusion.refs_0_, ...), custom_call_target="tpu_custom_call" | custom-call | flops 1 | bytes 1 | tf_op jit(solution)/shard_map/pallas_call | solution.py:824
  139.5 1.9 shard_map.418
  141.5 1.9 shard_map.417
  143.4 8.6 %collective-permute-done.35.refs_1_ = bf16[256,1024]{1,0:T(8,128)(2,1)S(1)} collective-permute-done((bf16[256,1024]{1,0:T(8,128)(2,1)S(1)}, bf16[256,1024]{1,0:T(8,128)(2,1)S(1)}, u32[]{:S(2)}, u32[]{:S(2)}) %collective-permute-start.35) | collective-permute-done | bytes 524320 | tf_op jit(solution)/shard_map/ppermute | solution.py:845
  152.0 3.3 %shard_map.419 = (f32[256,1024]{1,0:T(8,128)S(1)}, f32[1,1024]{1,0:T(1,128)S(1)}, bf16[256,1024]{1,0:T(8,128)(2,1)S(1)}, f32[256,512]{1,0:T(8,128)S(1)}, f32[8,512]{1,0:T(8,128)S(1)}) custom-call(bf16[256,1024]{1,0:T(8,128)(2,1)S(1)} %get-tuple-element.373.refs_0_, bf16[256,1024]{1,0:T(8,128)(2,1)S(1)} %collective-permute-done.35.refs_1_, ...), custom_call_target="tpu_custom_call" | custom-call | flops 1 | bytes 1 | tf_op jit(solution)/shard_map/pallas_call | solution.py:824
  157.4 2.2 collective-permute-done.38.refs_1_
  165.2 2.7 collective-permute-done.40.refs_2_
  169.6 1.9 collective-permute-start.46
  171.6 2.7 shard_map.422
  176.4 7.7 %collective-permute-done.43.refs_1_ = bf16[256,1024]{1,0:T(8,128)(2,1)S(1)} collective-permute-done((bf16[256,1024]{1,0:T(8,128)(2,1)S(1)}, bf16[256,1024]{1,0:T(8,128)(2,1)S(1)}, u32[]{:S(2)}, u32[]{:S(2)}) %collective-permute-start.43) | collective-permute-done | bytes 524320 | tf_op jit(solution)/shard_map/ppermute | solution.py:845
  184.1 5.4 %shard_map.423 = (f32[256,1024]{1,0:T(8,128)S(1)}, f32[1,1024]{1,0:T(1,128)S(1)}, bf16[256,1024]{1,0:T(8,128)(2,1)S(1)}, bf16[256,768]{1,0:T(8,128)(2,1)S(1)}, b...) custom-call(bf16[256,1024]{1,0:T(8,128)(2,1)S(1)} %get-tuple-element.400.refs_0_, ...), custom_call_target="tpu_custom_call" | custom-call | flops 1 | bytes 1 | tf_op jit(solution)/shard_map/pallas_call | solution.py:824
  192.0 3.1 shard_map.426
  200.0 9.3 %collective-permute-done.45.refs_2_ = bf16[256,1024]{1,0:T(8,128)(2,1)S(1)} collective-permute-done((bf16[256,1024]{1,0:T(8,128)(2,1)S(1)}, bf16[256,1024]{1,0:T(8,128)(2,1)S(1)}, u32[]{:S(2)}, u32[]{:S(2)}) %collective-permute-start.45) | collective-permute-done | bytes 524320 | tf_op jit(solution)/shard_map/ppermute | solution.py:845
  209.3 6.9 %shard_map.427 = (f32[256,1024]{1,0:T(8,128)S(1)}, f32[1,1024]{1,0:T(1,128)S(1)}, bf16[256,1024]{1,0:T(8,128)(2,1)S(1)}, bf16[256,1024]{1,0:T(8,128)(2,1)S(1)}, ...) custom-call(s32[4]{0:T(128)S(1)} %pad_add_fusion.refs_0_, ...), custom_call_target="tpu_custom_call" | custom-call | flops 1 | bytes 1 | tf_op jit(solution)/shard_map/pallas_call | solution.py:824
  216.9 4.0 %collective-permute-done.52 = bf16[2,128,1024]{2,1,0:T(8,128)(2,1)S(1)} collective-permute-done((bf16[2,128,1024]{2,1,0:T(8,128)(2,1)S(1)}, bf16[2,128,1024]{2,1,0:T(8,128)(2,1)S(1)}, u32[]{:S(2)}, u32[]{:S(2)}) %collective-permute-start.52) | collective-permute-done | bytes 524320 | tf_op jit(solution)/shard_map/ppermute | solution.py:845
  223.7 1.9 shard_map.431
  227.3 1.9 shard_map.430
  229.2 3.1 shard_map.432
  235.5 2.8 collective-permute-done.60.refs_1_
  238.3 2.2 collective-permute-start.61
  240.5 2.0 collective-permute-done.61.refs_1_
  244.1 2.1 collective-permute-start.62
  247.5 17.8 %collective-permute-done.63.refs_1_ = f32[8,1280]{1,0:T(8,128)S(1)} collective-permute-done((f32[8,1280]{1,0:T(8,128)S(1)}, f32[8,1280]{1,0:T(8,128)S(1)}, u32[]{:S(2)}, u32[]{:S(2)}) %collective-permute-start.63) | collective-permute-done | bytes 40992 | tf_op jit(solution)/shard_map/ppermute | solution.py:845
  267.5 2.5 collective-permute-start.66
  270.3 11.8 %collective-permute-done.54 = bf16[4,128,1024]{2,1,0:T(8,128)(2,1)S(1)} collective-permute-done((bf16[4,128,1024]{2,1,0:T(8,128)(2,1)S(1)}, bf16[4,128,1024]{2,1,0:T(8,128)(2,1)S(1)}, u32[]{:S(2)}, u32[]{:S(2)}) %collective-permute-start.54) | collective-permute-done | bytes 1048608 | tf_op jit(solution)/shard_map/ppermute | solution.py:845
  283.6 5.5 %collective-permute-done.66 = bf16[2,128,1024]{2,1,0:T(8,128)(2,1)S(1)} collective-permute-done((bf16[2,128,1024]{2,1,0:T(8,128)(2,1)S(1)}, bf16[2,128,1024]{2,1,0:T(8,128)(2,1)S(1)}, u32[]{:S(2)}, u32[]{:S(2)}) %collective-permute-start.66) | collective-permute-done | bytes 524320 | tf_op jit(solution)/shard_map/ppermute | solution.py:845
  290.6 2.5 collective-permute-start.64
  304.7 4.1 %collective-permute-done.64 = bf16[2,128,1024]{2,1,0:T(8,128)(2,1)} collective-permute-done((bf16[2,128,1024]{2,1,0:T(8,128)(2,1)}, bf16[2,128,1024]{2,1,0:T(8,128)(2,1)}, u32[]{:S(2)}, u32[]{:S(2)}) %collective-permute-start.64) | collective-permute-done | bytes 524320 | tf_op jit(solution)/shard_map/ppermute | solution.py:845
  315.1 5.8 %collective-permute-done.69 = bf16[1,128,1024]{2,1,0:T(8,128)(2,1)S(1)} collective-permute-done((bf16[1,128,1024]{2,1,0:T(8,128)(2,1)S(1)}, bf16[1,128,1024]{2,1,0:T(8,128)(2,1)S(1)}, u32[]{:S(2)}, u32[]{:S(2)}) %collective-permute-start.69) | collective-permute-done | bytes 262176 | tf_op jit(solution)/shard_map/ppermute | solution.py:845
  (226 shorter events, 97.0 us)
Async XLA Ops:
  0.7 35.5 %collective-permute-start.10 = (bf16[1024,1024]{1,0:T(8,128)(2,1)}, bf16[1024,1024]{1,0:T(8,128)(2,1)S(1)}, u32[]{:S(2)}, u32[]{:S(2)}) collective-permute-start(bf16[1024,1024]{1,0:T(8,128)(2,1)} %refs_7_.1), channel_id=1, source_target_pairs={{0,1},{1,0},{2,3},{3,2},{4,5},{5,4},{6,7},{7,6},{8,9},{9,8},{10,11... | collective-permute-start | bytes 6291464 | tf_op jit(solution)/shard_map/ppermute | solution.py:845
  1.2 35.0 %collective-permute-start.11 = (bf16[1024,1024]{1,0:T(8,128)(2,1)}, bf16[1024,1024]{1,0:T(8,128)(2,1)}, u32[]{:S(2)}, u32[]{:S(2)}) collective-permute-start(bf16[1024,1024]{1,0:T(8,128)(2,1)} %refs_9_.3), channel_id=1, source_target_pairs={{0,1},{1,0},{2,3},{3,2},{4,5},{5,4},{6,7},{7,6},{8,9},{9,8},{10,11... | collective-permute-start | bytes 6291464 | tf_op jit(solution)/shard_map/ppermute | solution.py:845
  2.9 7.6 %collective-permute-start = (f32[8,1024]{1,0:T(8,128)S(1)}, f32[8,1024]{1,0:T(8,128)S(1)}, u32[]{:S(2)}, u32[]{:S(2)}) collective-permute-start(f32[8,1024]{1,0:T(8,128)S(1)} %dynamic_update_slice.3.refs_0_), channel_id=1, source_target_pairs={{0,1},{1,0},{2,3},{3,2},{4,5},{5,4},{6,7},{7,6},{8,9},{9,8},{10,11... | collective-permute-start | bytes 98312 | tf_op jit(solution)/shard_map/ppermute | solution.py:845
  5.4 13.5 %collective-permute-start.4 = (bf16[1,128,768]{2,1,0:T(8,128)(2,1)S(1)}, bf16[1,128,768]{2,1,0:T(8,128)(2,1)S(1)}, u32[]{:S(2)}, u32[]{:S(2)}) collective-permute-start(bf16[1,128,768]{2,1,0:T(8,128)(2,1)S(1)} %maximum_bitcast_fusion.refs_1_), channel_id=1, source_target_pairs={{0,16},{4,20},{8,24},{12,28},{16,0},{20,4},{24,8},{28,12},{1,17},{... | collective-permute-start | bytes 589832 | tf_op jit(solution)/shard_map/ppermute | solution.py:845
  9.1 17.2 %collective-permute-start.6 = (bf16[2,64,1024]{2,1,0:T(8,128)(2,1)}, bf16[2,64,1024]{2,1,0:T(8,128)(2,1)S(1)}, u32[]{:S(2)}, u32[]{:S(2)}) collective-permute-start(bf16[2,64,1024]{2,1,0:T(8,128)(2,1)} %refs_2_.1), channel_id=1, source_target_pairs={{0,2},{1,3},{2,0},{3,1},{4,6},{5,7},{6,4},{7,5},{8,10},{9,11},{10,... | collective-permute-start | bytes 786440 | tf_op jit(solution)/shard_map/ppermute | solution.py:845
  19.5 12.2 %collective-permute-start.5 = (bf16[2,128,768]{2,1,0:T(8,128)(2,1)S(1)}, bf16[2,128,768]{2,1,0:T(8,128)(2,1)S(1)}, u32[]{:S(2)}, u32[]{:S(2)}) collective-permute-start(bf16[2,128,768]{2,1,0:T(8,128)(2,1)S(1)} %bitcast.87), channel_id=1, source_target_pairs={{0,8},{4,12},{8,0},{12,4},{16,24},{20,28},{24,16},{28,20},{1,9},{5... | collective-permute-start | bytes 1179656 | tf_op jit(solution)/shard_map/ppermute | solution.py:845
  26.2 6.1 %collective-permute-start.3 = (f32[8,256]{1,0:T(8,128)S(1)}, f32[8,256]{1,0:T(8,128)S(1)}, u32[]{:S(2)}, u32[]{:S(2)}) collective-permute-start(f32[8,256]{1,0:T(8,128)S(1)} %pad_maximum_fusion.2), channel_id=1, source_target_pairs={{0,1},{1,0},{2,3},{3,2},{4,5},{5,4},{6,7},{7,6},{8,9},{9,8},{10,11... | collective-permute-start | bytes 24584 | tf_op jit(solution)/shard_map/ppermute | solution.py:845
  26.8 4.9 %collective-permute-start.8 = (f32[8,1024]{1,0:T(8,128)S(1)}, f32[8,1024]{1,0:T(8,128)S(1)}, u32[]{:S(2)}, u32[]{:S(2)}) collective-permute-start(f32[8,1024]{1,0:T(8,128)S(1)} %shard_map.404.refs_0_), channel_id=1, source_target_pairs={{0,16},{4,20},{8,24},{12,28},{16,0},{20,4},{24,8},{28,12},{1,17},{... | collective-permute-start | bytes 98312 | tf_op jit(solution)/shard_map/ppermute | solution.py:845
  32.3 12.3 %collective-permute-start.13 = (bf16[1024,768]{1,0:T(8,128)(2,1)S(1)}, bf16[1024,768]{1,0:T(8,128)(2,1)S(1)}, u32[]{:S(2)}, u32[]{:S(2)}) collective-permute-start(bf16[1024,768]{1,0:T(8,128)(2,1)S(1)} %pad_maximum_fusion.refs_7_.refs_8_), channel_id=1, source_target_pairs={{0,1},{1,0},{2,3},{3,2},{4,5},{5,4},{6,7},{7,6},{8,9},{9,8},{10,11... | collective-permute-start | bytes 4718600 | tf_op jit(solution)/shard_map/ppermute | solution.py:845
  32.9 29.4 %collective-permute-start.16 = (bf16[4,128,768]{2,1,0:T(8,128)(2,1)S(1)}, bf16[4,128,768]{2,1,0:T(8,128)(2,1)S(1)}, u32[]{:S(2)}, u32[]{:S(2)}) collective-permute-start(bf16[4,128,768]{2,1,0:T(8,128)(2,1)S(1)} %bitcast.79), channel_id=1, source_target_pairs={{0,4},{4,0},{8,12},{12,8},{16,20},{20,16},{24,28},{28,24},{1,5},{5... | collective-permute-start | bytes 2359304 | tf_op jit(solution)/shard_map/ppermute | solution.py:845
  43.0 14.2 %collective-permute-start.12 = (bf16[256,1024]{1,0:T(8,128)(2,1)S(1)}, bf16[256,1024]{1,0:T(8,128)(2,1)S(1)}, u32[]{:S(2)}, u32[]{:S(2)}) collective-permute-start(bf16[256,1024]{1,0:T(8,128)(2,1)S(1)} %get-tuple-element.327.refs_3_), channel_id=1, source_target_pairs={{0,2},{1,3},{2,0},{3,1},{4,6},{5,7},{6,4},{7,5},{8,10},{9,11},{10,... | collective-permute-start | bytes 1572872 | tf_op jit(solution)/shard_map/ppermute | solution.py:845
  63.0 14.9 %collective-permute-start.19 = (bf16[1024,768]{1,0:T(8,128)(2,1)S(1)}, bf16[1024,768]{1,0:T(8,128)(2,1)S(1)}, u32[]{:S(2)}, u32[]{:S(2)}) collective-permute-start(bf16[1024,768]{1,0:T(8,128)(2,1)S(1)} %bitcast.73), channel_id=1, source_target_pairs={{0,1},{1,0},{2,3},{3,2},{4,5},{5,4},{6,7},{7,6},{8,9},{9,8},{10,11... | collective-permute-start | bytes 4718600 | tf_op jit(solution)/shard_map/ppermute | solution.py:845
  63.6 4.4 %collective-permute-start.17 = (bf16[256,1024]{1,0:T(8,128)(2,1)S(1)}, bf16[256,1024]{1,0:T(8,128)(2,1)S(1)}, u32[]{:S(2)}, u32[]{:S(2)}) collective-permute-start(bf16[256,1024]{1,0:T(8,128)(2,1)S(1)} %get-tuple-element.338.refs_1_), channel_id=1, source_target_pairs={{0,1},{1,0},{2,3},{3,2},{4,5},{5,4},{6,7},{7,6},{8,9},{9,8},{10,11... | collective-permute-start | bytes 1572872 | tf_op jit(solution)/shard_map/ppermute | solution.py:845
  63.7 14.3 %collective-permute-start.15 = (bf16[256,1024]{1,0:T(8,128)(2,1)S(1)}, bf16[256,1024]{1,0:T(8,128)(2,1)S(1)}, u32[]{:S(2)}, u32[]{:S(2)}) collective-permute-start(bf16[256,1024]{1,0:T(8,128)(2,1)S(1)} %get-tuple-element.332.refs_1_), channel_id=1, source_target_pairs={{0,2},{1,3},{2,0},{3,1},{4,6},{5,7},{6,4},{7,5},{8,10},{9,11},{10,... | collective-permute-start | bytes 1572872 | tf_op jit(solution)/shard_map/ppermute | solution.py:845
  81.5 30.5 %collective-permute-start.28 = (bf16[1024,1024]{1,0:T(8,128)(2,1)S(1)}, bf16[1024,1024]{1,0:T(8,128)(2,1)S(1)}, u32[]{:S(2)}, u32[]{:S(2)}) collective-permute-start(bf16[1024,1024]{1,0:T(8,128)(2,1)S(1)} %copy-done.9), channel_id=1, source_target_pairs={{0,1},{1,0},{2,3},{3,2},{4,5},{5,4},{6,7},{7,6},{8,9},{9,8},{10,11... | collective-permute-start | bytes 6291464 | tf_op jit(solution)/shard_map/ppermute | solution.py:845
  81.6 30.4 %collective-permute-start.29 = (bf16[1024,1024]{1,0:T(8,128)(2,1)S(1)}, bf16[1024,1024]{1,0:T(8,128)(2,1)S(1)}, u32[]{:S(2)}, u32[]{:S(2)}) collective-permute-start(bf16[1024,1024]{1,0:T(8,128)(2,1)S(1)} %copy-done.10), channel_id=1, source_target_pairs={{0,1},{1,0},{2,3},{3,2},{4,5},{5,4},{6,7},{7,6},{8,9},{9,8},{10,11... | collective-permute-start | bytes 6291464 | tf_op jit(solution)/shard_map/ppermute | solution.py:845
  82.1 12.4 %collective-permute-start.23 = (bf16[256,1024]{1,0:T(8,128)(2,1)S(1)}, bf16[256,1024]{1,0:T(8,128)(2,1)S(1)}, u32[]{:S(2)}, u32[]{:S(2)}) collective-permute-start(bf16[256,1024]{1,0:T(8,128)(2,1)S(1)} %get-tuple-element.347.refs_9_), channel_id=1, source_target_pairs={{0,1},{1,0},{2,3},{3,2},{4,5},{5,4},{6,7},{7,6},{8,9},{9,8},{10,11... | collective-permute-start | bytes 1572872 | tf_op jit(solution)/shard_map/ppermute | solution.py:845
  82.1 12.3 %collective-permute-start.25 = (bf16[2,64,1024]{2,1,0:T(8,128)(2,1)S(1)}, bf16[2,64,1024]{2,1,0:T(8,128)(2,1)S(1)}, u32[]{:S(2)}, u32[]{:S(2)}) collective-permute-start(bf16[2,64,1024]{2,1,0:T(8,128)(2,1)S(1)} %copy-done.2), channel_id=1, source_target_pairs={{0,2},{1,3},{2,0},{3,1},{4,6},{5,7},{6,4},{7,5},{8,10},{9,11},{10,... | collective-permute-start | bytes 786440 | tf_op jit(solution)/shard_map/ppermute | solution.py:845
  92.6 4.6 %collective-permute-start.22 = (f32[8,512]{1,0:T(8,128)S(1)}, f32[8,512]{1,0:T(8,128)S(1)}, u32[]{:S(2)}, u32[]{:S(2)}) collective-permute-start(f32[8,512]{1,0:T(8,128)S(1)} %shard_map.412.refs_0_), channel_id=1, source_target_pairs={{0,16},{4,20},{8,24},{12,28},{16,0},{20,4},{24,8},{28,12},{1,17},{... | collective-permute-start | bytes 49160 | tf_op jit(solution)/shard_map/ppermute | solution.py:845
  99.1 12.9 %collective-permute-start.26 = (bf16[256,1024]{1,0:T(8,128)(2,1)S(1)}, bf16[256,1024]{1,0:T(8,128)(2,1)S(1)}, u32[]{:S(2)}, u32[]{:S(2)}) collective-permute-start(bf16[256,1024]{1,0:T(8,128)(2,1)S(1)} %get-tuple-element.352.refs_0_), channel_id=1, source_target_pairs={{0,2},{1,3},{2,0},{3,1},{4,6},{5,7},{6,4},{7,5},{8,10},{9,11},{10,... | collective-permute-start | bytes 1572872 | tf_op jit(solution)/shard_map/ppermute | solution.py:845
  117.0 14.3 %collective-permute-start.30 = (bf16[256,1024]{1,0:T(8,128)(2,1)S(1)}, bf16[256,1024]{1,0:T(8,128)(2,1)S(1)}, u32[]{:S(2)}, u32[]{:S(2)}) collective-permute-start(bf16[256,1024]{1,0:T(8,128)(2,1)S(1)} %get-tuple-element.360.refs_1_), channel_id=1, source_target_pairs={{0,2},{1,3},{2,0},{3,1},{4,6},{5,7},{6,4},{7,5},{8,10},{9,11},{10,... | collective-permute-start | bytes 1572872 | tf_op jit(solution)/shard_map/ppermute | solution.py:845
  138.1 13.9 %collective-permute-start.35 = (bf16[256,1024]{1,0:T(8,128)(2,1)S(1)}, bf16[256,1024]{1,0:T(8,128)(2,1)S(1)}, u32[]{:S(2)}, u32[]{:S(2)}) collective-permute-start(bf16[256,1024]{1,0:T(8,128)(2,1)S(1)} %get-tuple-element.373.refs_0_), channel_id=1, source_target_pairs={{0,2},{1,3},{2,0},{3,1},{4,6},{5,7},{6,4},{7,5},{8,10},{9,11},{10,... | collective-permute-start | bytes 1572872 | tf_op jit(solution)/shard_map/ppermute | solution.py:845
  155.3 12.7 %collective-permute-start.42 = (bf16[256,1024]{1,0:T(8,128)(2,1)S(1)}, bf16[256,1024]{1,0:T(8,128)(2,1)S(1)}, u32[]{:S(2)}, u32[]{:S(2)}) collective-permute-start(bf16[256,1024]{1,0:T(8,128)(2,1)S(1)} %get-tuple-element.392.refs_10_.refs_5_), channel_id=1, source_target_pairs={{0,1},{1,0},{2,3},{3,2},{4,5},{5,4},{6,7},{7,6},{8,9},{9,8},{10,11... | collective-permute-start | bytes 1572872 | tf_op jit(solution)/shard_map/ppermute | solution.py:845
  155.4 12.6 %collective-permute-start.41 = (bf16[64,1024]{1,0:T(8,128)(2,1)S(1)}, bf16[64,1024]{1,0:T(8,128)(2,1)S(1)}, u32[]{:S(2)}, u32[]{:S(2)}) collective-permute-start(bf16[64,1024]{1,0:T(8,128)(2,1)S(1)} %get-tuple-element.391), channel_id=1, source_target_pairs={{0,1},{1,0},{2,3},{3,2},{4,5},{5,4},{6,7},{7,6},{8,9},{9,8},{10,11... | collective-permute-start | bytes 393224 | tf_op jit(solution)/shard_map/ppermute | solution.py:845
  163.3 4.6 %collective-permute-start.40 = (f32[8,512]{1,0:T(8,128)S(1)}, f32[8,512]{1,0:T(8,128)S(1)}, u32[]{:S(2)}, u32[]{:S(2)}) collective-permute-start(f32[8,512]{1,0:T(8,128)S(1)} %shard_map.421.refs_1_), channel_id=1, source_target_pairs={{0,16},{4,20},{8,24},{12,28},{16,0},{20,4},{24,8},{28,12},{1,17},{... | collective-permute-start | bytes 49160 | tf_op jit(solution)/shard_map/ppermute | solution.py:845
  168.0 22.1 %collective-permute-start.47 = (bf16[4,128,1024]{2,1,0:T(8,128)(2,1)S(1)}, bf16[4,128,1024]{2,1,0:T(8,128)(2,1)S(1)}, u32[]{:S(2)}, u32[]{:S(2)}) collective-permute-start(bf16[4,128,1024]{2,1,0:T(8,128)(2,1)S(1)} %get-tuple-element.420), channel_id=1, source_target_pairs={{0,4},{4,0},{8,12},{12,8},{16,20},{20,16},{24,28},{28,24},{1,5},{5... | collective-permute-start | bytes 3145736 | tf_op jit(solution)/shard_map/ppermute | solution.py:845
  169.6 21.4 %collective-permute-start.46 = (bf16[4,128,1024]{2,1,0:T(8,128)(2,1)S(1)}, bf16[4,128,1024]{2,1,0:T(8,128)(2,1)S(1)}, u32[]{:S(2)}, u32[]{:S(2)}) collective-permute-start(bf16[4,128,1024]{2,1,0:T(8,128)(2,1)S(1)} %get-tuple-element.418), channel_id=1, source_target_pairs={{0,8},{4,12},{8,0},{12,4},{16,24},{20,28},{24,16},{28,20},{1,9},{5... | collective-permute-start | bytes 3145736 | tf_op jit(solution)/shard_map/ppermute | solution.py:845
  174.3 9.8 %collective-permute-start.43 = (bf16[256,1024]{1,0:T(8,128)(2,1)S(1)}, bf16[256,1024]{1,0:T(8,128)(2,1)S(1)}, u32[]{:S(2)}, u32[]{:S(2)}) collective-permute-start(bf16[256,1024]{1,0:T(8,128)(2,1)S(1)} %get-tuple-element.400.refs_0_), channel_id=1, source_target_pairs={{0,2},{1,3},{2,0},{3,1},{4,6},{5,7},{6,4},{7,5},{8,10},{9,11},{10,... | collective-permute-start | bytes 1572872 | tf_op jit(solution)/shard_map/ppermute | solution.py:845
  195.1 48.0 %collective-permute-start.56 = (bf16[4,128,1792]{2,1,0:T(8,128)(2,1)S(1)}, bf16[4,128,1792]{2,1,0:T(8,128)(2,1)S(1)}, u32[]{:S(2)}, u32[]{:S(2)}) collective-permute-start(bf16[4,128,1792]{2,1,0:T(8,128)(2,1)S(1)} %get-tuple-element.477), channel_id=1, source_target_pairs={{0,4},{4,0},{8,12},{12,8},{16,20},{20,16},{24,28},{28,24},{1,5},{5... | collective-permute-start | bytes 5505032 | tf_op jit(solution)/shard_map/ppermute | solution.py:845
  196.0 13.3 %collective-permute-start.45 = (bf16[256,1024]{1,0:T(8,128)(2,1)S(1)}, bf16[256,1024]{1,0:T(8,128)(2,1)S(1)}, u32[]{:S(2)}, u32[]{:S(2)}) collective-permute-start(bf16[256,1024]{1,0:T(8,128)(2,1)S(1)} %get-tuple-element.407.refs_1_), channel_id=1, source_target_pairs={{0,2},{1,3},{2,0},{3,1},{4,6},{5,7},{6,4},{7,5},{8,10},{9,11},{10,... | collective-permute-start | bytes 1572872 | tf_op jit(solution)/shard_map/ppermute | solution.py:845
  196.5 24.3 %collective-permute-start.52 = (bf16[2,128,1024]{2,1,0:T(8,128)(2,1)S(1)}, bf16[2,128,1024]{2,1,0:T(8,128)(2,1)S(1)}, u32[]{:S(2)}, u32[]{:S(2)}) collective-permute-start(bf16[2,128,1024]{2,1,0:T(8,128)(2,1)S(1)} %get-tuple-element.447), channel_id=1, source_target_pairs={{0,8},{4,12},{8,0},{12,4},{16,24},{20,28},{24,16},{28,20},{1,9},{5... | collective-permute-start | bytes 1572872 | tf_op jit(solution)/shard_map/ppermute | solution.py:845
  198.3 24.7 %collective-permute-start.51 = (bf16[1,256,1024]{2,1,0:T(8,128)(2,1)S(1)}, bf16[1,256,1024]{2,1,0:T(8,128)(2,1)S(1)}, u32[]{:S(2)}, u32[]{:S(2)}) collective-permute-start(bf16[1,256,1024]{2,1,0:T(8,128)(2,1)S(1)} %get-tuple-element.445), channel_id=1, source_target_pairs={{0,16},{4,20},{8,24},{12,28},{16,0},{20,4},{24,8},{28,12},{1,17},{... | collective-permute-start | bytes 1572872 | tf_op jit(solution)/shard_map/ppermute | solution.py:845
  216.3 7.5 %collective-permute-start.53 = (bf16[256,1024]{1,0:T(8,128)(2,1)S(1)}, bf16[256,1024]{1,0:T(8,128)(2,1)S(1)}, u32[]{:S(2)}, u32[]{:S(2)}) collective-permute-start(bf16[256,1024]{1,0:T(8,128)(2,1)S(1)} %get-tuple-element.465), channel_id=1, source_target_pairs={{0,1},{1,0},{2,3},{3,2},{4,5},{5,4},{6,7},{7,6},{8,9},{9,8},{10,11... | collective-permute-start | bytes 1572872 | tf_op jit(solution)/shard_map/ppermute | solution.py:845
  216.4 10.9 %collective-permute-start.50 = (bf16[256,1024]{1,0:T(8,128)(2,1)S(1)}, bf16[256,1024]{1,0:T(8,128)(2,1)S(1)}, u32[]{:S(2)}, u32[]{:S(2)}) collective-permute-start(bf16[256,1024]{1,0:T(8,128)(2,1)S(1)} %get-tuple-element.441.refs_1_), channel_id=1, source_target_pairs={{0,1},{1,0},{2,3},{3,2},{4,5},{5,4},{6,7},{7,6},{8,9},{9,8},{10,11... | collective-permute-start | bytes 1572872 | tf_op jit(solution)/shard_map/ppermute | solution.py:845
  220.8 8.4 %collective-permute-start.58 = (bf16[128,1024]{1,0:T(8,128)(2,1)S(1)}, bf16[128,1024]{1,0:T(8,128)(2,1)S(1)}, u32[]{:S(2)}, u32[]{:S(2)}) collective-permute-start(bf16[128,1024]{1,0:T(8,128)(2,1)S(1)} %get-tuple-element.483), channel_id=1, source_target_pairs={{0,2},{1,3},{2,0},{3,1},{4,6},{5,7},{6,4},{7,5},{8,10},{9,11},{10,... | collective-permute-start | bytes 786440 | tf_op jit(solution)/shard_map/ppermute | solution.py:845
  223.0 19.5 %collective-permute-start.57 = (bf16[1,128,1024]{2,1,0:T(8,128)(2,1)S(1)}, bf16[1,128,1024]{2,1,0:T(8,128)(2,1)S(1)}, u32[]{:S(2)}, u32[]{:S(2)}) collective-permute-start(bf16[1,128,1024]{2,1,0:T(8,128)(2,1)S(1)} %get-tuple-element.479), channel_id=1, source_target_pairs={{0,16},{4,20},{8,24},{12,28},{16,0},{20,4},{24,8},{28,12},{1,17},{... | collective-permute-start | bytes 786440 | tf_op jit(solution)/shard_map/ppermute | solution.py:845
  225.7 41.1 %collective-permute-start.55 = (bf16[4,128,1024]{2,1,0:T(8,128)(2,1)S(1)}, bf16[4,128,1024]{2,1,0:T(8,128)(2,1)S(1)}, u32[]{:S(2)}, u32[]{:S(2)}) collective-permute-start(bf16[4,128,1024]{2,1,0:T(8,128)(2,1)S(1)} %get-tuple-element.475), channel_id=1, source_target_pairs={{0,4},{4,0},{8,12},{12,8},{16,20},{20,16},{24,28},{28,24},{1,5},{5... | collective-permute-start | bytes 3145736 | tf_op jit(solution)/shard_map/ppermute | solution.py:845
  244.1 21.9 %collective-permute-start.62 = (bf16[2,128,1792]{2,1,0:T(8,128)(2,1)S(1)}, bf16[2,128,1792]{2,1,0:T(8,128)(2,1)S(1)}, u32[]{:S(2)}, u32[]{:S(2)}) collective-permute-start(bf16[2,128,1792]{2,1,0:T(8,128)(2,1)S(1)} %get-tuple-element.508), channel_id=1, source_target_pairs={{0,8},{4,12},{8,0},{12,4},{16,24},{20,28},{24,16},{28,20},{1,9},{5... | collective-permute-start | bytes 2752520 | tf_op jit(solution)/shard_map/ppermute | solution.py:845
  246.2 36.0 %collective-permute-start.54 = (bf16[4,128,1024]{2,1,0:T(8,128)(2,1)S(1)}, bf16[4,128,1024]{2,1,0:T(8,128)(2,1)S(1)}, u32[]{:S(2)}, u32[]{:S(2)}) collective-permute-start(bf16[4,128,1024]{2,1,0:T(8,128)(2,1)S(1)} %get-tuple-element.473), channel_id=1, source_target_pairs={{0,4},{4,0},{8,12},{12,8},{16,20},{20,16},{24,28},{28,24},{1,5},{5... | collective-permute-start | bytes 3145736 | tf_op jit(solution)/shard_map/ppermute | solution.py:845
  246.7 18.5 %collective-permute-start.63 = (f32[8,1280]{1,0:T(8,128)S(1)}, f32[8,1280]{1,0:T(8,128)S(1)}, u32[]{:S(2)}, u32[]{:S(2)}) collective-permute-start(f32[8,1280]{1,0:T(8,128)S(1)} %shard_map.438.refs_0_), channel_id=1, source_target_pairs={{0,16},{4,20},{8,24},{12,28},{16,0},{20,4},{24,8},{28,12},{1,17},{... | collective-permute-start | bytes 122888 | tf_op jit(solution)/shard_map/ppermute | solution.py:845
  267.5 21.7 %collective-permute-start.66 = (bf16[2,128,1024]{2,1,0:T(8,128)(2,1)S(1)}, bf16[2,128,1024]{2,1,0:T(8,128)(2,1)S(1)}, u32[]{:S(2)}, u32[]{:S(2)}) collective-permute-start(bf16[2,128,1024]{2,1,0:T(8,128)(2,1)S(1)} %get-tuple-element.537), channel_id=1, source_target_pairs={{0,8},{4,12},{8,0},{12,4},{16,24},{20,28},{24,16},{28,20},{1,9},{5... | collective-permute-start | bytes 1572872 | tf_op jit(solution)/shard_map/ppermute | solution.py:845
  270.0 23.1 %collective-permute-start.65 = (bf16[1,128,1792]{2,1,0:T(8,128)(2,1)S(1)}, bf16[1,128,1792]{2,1,0:T(8,128)(2,1)S(1)}, u32[]{:S(2)}, u32[]{:S(2)}) collective-permute-start(bf16[1,128,1792]{2,1,0:T(8,128)(2,1)S(1)} %get-tuple-element.535), channel_id=1, source_target_pairs={{0,16},{4,20},{8,24},{12,28},{16,0},{20,4},{24,8},{28,12},{1,17},{... | collective-permute-start | bytes 1376264 | tf_op jit(solution)/shard_map/ppermute | solution.py:845
  270.3 26.5 %collective-permute-start.70 = (f32[64,1024]{1,0:T(8,128)}, f32[64,1024]{1,0:T(8,128)}, u32[]{:S(2)}, u32[]{:S(2)}) collective-permute-start(f32[64,1024]{1,0:T(8,128)} %get-tuple-element.570), channel_id=1, source_target_pairs={{0,1},{1,0},{2,3},{3,2},{4,5},{5,4},{6,7},{7,6},{8,9},{9,8},{10,11... | collective-permute-start | bytes 786440 | tf_op jit(solution)/shard_map/ppermute | solution.py:845
  290.5 12.5 %collective-permute-start.68 = (bf16[1,128,1024]{2,1,0:T(8,128)(2,1)}, bf16[1,128,1024]{2,1,0:T(8,128)(2,1)}, u32[]{:S(2)}, u32[]{:S(2)}) collective-permute-start(bf16[1,128,1024]{2,1,0:T(8,128)(2,1)} %get-tuple-element.556), channel_id=1, source_target_pairs={{0,16},{4,20},{8,24},{12,28},{16,0},{20,4},{24,8},{28,12},{1,17},{... | collective-permute-start | bytes 786440 | tf_op jit(solution)/shard_map/ppermute | solution.py:845
  290.6 18.2 %collective-permute-start.64 = (bf16[2,128,1024]{2,1,0:T(8,128)(2,1)}, bf16[2,128,1024]{2,1,0:T(8,128)(2,1)}, u32[]{:S(2)}, u32[]{:S(2)}) collective-permute-start(bf16[2,128,1024]{2,1,0:T(8,128)(2,1)} %get-tuple-element.532), channel_id=1, source_target_pairs={{0,8},{4,12},{8,0},{12,4},{16,24},{20,28},{24,16},{28,20},{1,9},{5... | collective-permute-start | bytes 1572872 | tf_op jit(solution)/shard_map/ppermute | solution.py:845
  293.9 10.1 %collective-permute-start.67 = (f32[8,1280]{1,0:T(8,128)S(1)}, f32[8,1280]{1,0:T(8,128)S(1)}, u32[]{:S(2)}, u32[]{:S(2)}) collective-permute-start(f32[8,1280]{1,0:T(8,128)S(1)} %shard_map.441.refs_0_), channel_id=1, source_target_pairs={{0,4},{4,0},{8,12},{12,8},{16,20},{20,16},{24,28},{28,24},{1,5},{5... | collective-permute-start | bytes 122888 | tf_op jit(solution)/shard_map/ppermute | solution.py:845
  294.7 16.1 %collective-permute-start.71 = (bf16[1,128,1024]{2,1,0:T(8,128)(2,1)}, bf16[1,128,1024]{2,1,0:T(8,128)(2,1)S(1)}, u32[]{:S(2)}, u32[]{:S(2)}) collective-permute-start(bf16[1,128,1024]{2,1,0:T(8,128)(2,1)} %copy-done.7), channel_id=1, source_target_pairs={{0,4},{4,0},{8,12},{12,8},{16,20},{20,16},{24,28},{28,24},{1,5},{5... | collective-permute-start | bytes 786440 | tf_op jit(solution)/shard_map/ppermute | solution.py:845
  309.9 11.0 %collective-permute-start.69 = (bf16[1,128,1024]{2,1,0:T(8,128)(2,1)S(1)}, bf16[1,128,1024]{2,1,0:T(8,128)(2,1)S(1)}, u32[]{:S(2)}, u32[]{:S(2)}) collective-permute-start(bf16[1,128,1024]{2,1,0:T(8,128)(2,1)S(1)} %get-tuple-element.568), channel_id=1, source_target_pairs={{0,16},{4,20},{8,24},{12,28},{16,0},{20,4},{24,8},{28,12},{1,17},{... | collective-permute-start | bytes 786440 | tf_op jit(solution)/shard_map/ppermute | solution.py:845
  (44 other events, 233.8 us)
